TPU v7x, 32 devices: a whole 2x2x4 slice. The times are simulated.
32 devices in a mesh: gx: 2 (over x), gy: 4 (over z), col: 4 (over y, core).
Axes of the slice: x: 2, y: 2, z: 4, core: 2. Of those that a mesh axis runs over, the one named last changes fastest.
Arguments:
- right_side: float32 [8, 128, 512], P('gx', 'gy', 'col'), may hold values from -12 to 12
- diag_shift: float32 [8, 128, 512], P('gx', 'gy', 'col'), may hold values from 0.05 to 1
- stiffness: float32 [8, 128, 512], P('gx', 'gy', 'col'), may hold values from 0.5 to 2
- block_owner: int32 [32, 128], P(('gx', 'gy', 'col')), may hold values from 0 to 3, as said below
- block_group: int32 [32, 128], P(('gx', 'gy', 'col')), may hold values from 0 to 127
- coarse_inverse: float32 [32, 8, 128, 128], P(('gx', 'gy', 'col')), may hold values from -2e-05 to 0.0152
Outputs:
- solution_field: float32 [8, 128, 512], P('gx', 'gy', 'col')
- residual: float32 [8, 128, 512], P('gx', 'gy', 'col')
Inputs may be any that keep to these rules, and one draw needn't show every extreme that they name: `block_owner`: the row blocks of one device name at most 64 blocks for one owner, and in every group of 4 devices that share gx and gy one owner gets exactly 64 blocks from each device of the group.
All inputs are finite; a program needn't handle non-finite values.
Results may differ from a plain program's by a relative error of at most 0.0003.
Values sent between devices are 32-bit elements; how exact they have to be, the bound alone decides.
No kernel may reach another device: no remote copies, remote signals or barrier semaphores. Data moves between devices by JAX's collectives and lax.ppermute only.
A program may use at most 64 MiB of HBM per device.

v0:
```python
import jax
import jax.numpy as jnp
from jax import lax
from jax.sharding import PartitionSpec as P

AGG = 16
ITERS = 4


cheb_first = 1.0 / 1.7364
cheb_second = 1.0 / 0.4636
highest = lax.Precision.HIGHEST


def extended(cells, sides, width):
    for axis, dim in sides:
        count = lax.axis_size(axis)
        ends = count - 1
        head = lax.slice_in_dim(cells, 0, width, axis=dim)
        tail = lax.slice_in_dim(cells, cells.shape[dim] - width, cells.shape[dim], axis=dim)
        cells = jnp.concatenate(
            [
                lax.ppermute(tail, axis, [(i, (i + 1) % count) for i in range(ends)]),
                cells,
                lax.ppermute(head, axis, [((i + 1) % count, i) for i in range(ends)]),
            ],
            axis=dim,
        )
    return cells


def neighbour_sum(field):
    padded = extended(field, (("gx", 0), ("gy", 1), ("col", 2)), 1)
    total = padded[2:, 1:-1, 1:-1] + padded[:-2, 1:-1, 1:-1]
    total = total + padded[1:-1, 2:, 1:-1] + padded[1:-1, :-2, 1:-1]
    total = total + padded[1:-1, 1:-1, 2:] + padded[1:-1, 1:-1, :-2]
    return total


def global_sum(local_value):
    return lax.psum(local_value, ("gx", "gy", "col"))


def on_device(right_side, diag_shift, stiffness, block_owner, block_group, coarse_inverse):
    grid_shape = right_side.shape
    nblock = grid_shape[0] * grid_shape[1]
    depth = grid_shape[2]
    per_block = depth // AGG
    capacity = nblock // 2
    n_col = lax.axis_size("col")
    owners = block_owner[0]
    groups_of = block_group[0]
    targets = owners * nblock + groups_of
    stiff_sum = neighbour_sum(stiffness)
    diagonal = diag_shift + stiffness * stiff_sum

    def operate(vector):
        return diag_shift * vector + stiffness * (
            stiff_sum * vector - neighbour_sum(stiffness * vector)
        )

    owner_hot = (owners[:, None] == jnp.arange(n_col, dtype=jnp.int32)[None, :]).astype(jnp.int32)
    earlier = jnp.cumsum(owner_hot, axis=0) - owner_hot
    slot_index = jnp.sum(earlier * owner_hot, axis=1)
    owner_match = owners[None, None, :] == jnp.arange(n_col, dtype=jnp.int32)[:, None, None]
    slot_match = slot_index[None, None, :] == jnp.arange(capacity, dtype=jnp.int32)[None, :, None]
    selector = (owner_match & slot_match).astype(jnp.float32)
    send_groups = jnp.einsum(
        "ksb,b->ks", selector, groups_of.astype(jnp.float32), precision=highest
    )
    group_ids = jnp.arange(nblock, dtype=jnp.int32).astype(jnp.float32)

    def coarse(field):
        send_rows = jnp.einsum(
            "ksb,bz->ksz", selector, field.reshape(nblock, depth), precision=highest
        )
        received, received_groups = (
            lax.all_to_all(send_rows, "col", split_axis=0, concat_axis=0, tiled=True),
            lax.all_to_all(send_groups, "col", split_axis=0, concat_axis=0, tiled=True),
        )
        aggregates = received.reshape(n_col * capacity, per_block, AGG).sum(axis=2)
        matches = (received_groups.reshape(-1)[:, None] == group_ids[None, :]).astype(jnp.float32)
        coarse_rows = jnp.einsum("sg,sk->gk", matches, aggregates, precision=highest)
        solved = jnp.einsum(
            "bij,bj->bi", coarse_inverse[0], coarse_rows.reshape(-1, 128), precision=highest
        )
        solved = solved.reshape(nblock, per_block)
        gathered = lax.all_gather(solved, "col", axis=0, tiled=True)
        chosen = jnp.take(gathered, targets, axis=0)
        spread = jnp.broadcast_to(chosen[:, :, None], (nblock, per_block, AGG))
        return spread.reshape(grid_shape)

    def precondition(field):
        iterate = cheb_first * field / diagonal
        iterate = iterate + cheb_second * (field - operate(iterate)) / diagonal
        iterate = iterate + coarse(field - operate(iterate))
        iterate = iterate + cheb_second * (field - operate(iterate)) / diagonal
        iterate = iterate + cheb_first * (field - operate(iterate)) / diagonal
        return iterate

    solution_field = jnp.zeros_like(right_side)
    residual = right_side
    precond = precondition(residual)
    direction = precond
    gamma_now = global_sum(jnp.sum(residual * precond))
    for iteration in range(ITERS):
        image_vec = operate(direction)
        curve_sum = lax.psum(jnp.sum(direction * image_vec), ("gx", "gy", "col"))
        alpha_step = gamma_now / curve_sum
        solution_field = solution_field + alpha_step * direction
        residual = residual - alpha_step * image_vec
        if iteration + 1 < ITERS:
            precond = precondition(residual)
            gamma_next = global_sum(jnp.sum(residual * precond))
            direction = precond + gamma_next / gamma_now * direction
            gamma_now = gamma_next
    return (solution_field, residual)


def solution(mesh):
    placed = (
        P("gx", "gy", "col"),
        P("gx", "gy", "col"),
        P("gx", "gy", "col"),
        P(("gx", "gy", "col"), None),
        P(("gx", "gy", "col"), None),
        P(("gx", "gy", "col"), None, None, None),
    )
    return jax.shard_map(
        on_device,
        mesh=mesh,
        in_specs=placed,
        out_specs=(P("gx", "gy", "col"), P("gx", "gy", "col")),
        check_vma=False,
    )
```

profile of v0, /device:TPU:0, one launch (start us, length us, event | category | flops | bytes accessed | tf_op | source)
XLA Modules:
  0.0 870.6 jit_solution(10276868697711923111)
XLA Ops:
  1.5 4.8 collective-permute-start.1
  7.7 4.2 collective-permute-done
  52.2 8.4 all-to-all-start
  76.0 6.3 all-to-all-start.1
  88.8 5.8 all_gather.12
  95.7 4.4 collective-permute-start.19
  101.6 4.2 collective-permute-done.18
  109.0 4.2 collective-permute-done.20
  121.8 4.2 collective-permute-done.24
  142.1 4.2 collective-permute-done.30
  160.3 44.6 %all-reduce = (f32[]{:T(128)}, f32[]{:T(128)}) all-reduce(f32[]{:T(128)} %get-tuple-element.6, f32[]{:T(128)} %get-tuple-element.5), channel_id=1, replica_groups=mesh['gx'=2,'gy'=4,'col'=4] {'gx','gy','col'}, use_global_device_ids=true, to_apply=%region_4.6 | all-reduce | flops 2 | bytes 16 | tf_op jit(solution)/shard_map/psum | solution.py:41
  206.3 4.2 collective-permute-start.37
  211.9 4.2 collective-permute-done.36
  234.1 4.2 collective-permute-done.42
  242.3 4.2 collective-permute-done.44
  252.2 13.5 %all_to_all.32 = f32[4,64,128]{2,1,0:T(8,128)S(1)} all-to-all(f32[4,64,128]{2,1,0:T(8,128)S(1)} %fusion.12), channel_id=1, replica_groups=mesh['gx'=2,'gy'=4,'col'=4] {'col'}, dimensions={0} | all-to-all | bytes 262144 | tf_op jit(solution)/shard_map/all_to_all | solution.py:78
  267.5 5.8 all_gather.13
  277.5 4.2 collective-permute-done.48
  285.0 4.2 collective-permute-done.50
  297.8 4.2 collective-permute-done.54
  305.2 4.2 collective-permute-done.56
  315.6 42.3 %psum.58 = f32[]{:T(128)} all-reduce(f32[]{:T(128)} %get-tuple-element.41), channel_id=1, replica_groups=mesh['gx'=2,'gy'=4,'col'=4] {'gx','gy','col'}, use_global_device_ids=true, to_apply=%region_9.11 | all-reduce | flops 1 | bytes 8 | tf_op jit(solution)/shard_map/psum | solution.py:41
  359.3 4.2 collective-permute-start.61
  364.9 4.2 collective-permute-done.60
  374.3 4.2 collective-permute-done.62
  384.6 41.6 %psum.59 = f32[]{:T(128)} all-reduce(f32[]{:T(128)} %get-tuple-element.37), channel_id=1, replica_groups=mesh['gx'=2,'gy'=4,'col'=4] {'gx','gy','col'}, use_global_device_ids=true, to_apply=%region_11.13 | all-reduce | flops 1 | bytes 8 | tf_op jit(solution)/shard_map/psum | solution.py:108
  427.6 4.2 collective-permute-start.67
  433.2 4.2 collective-permute-done.66
  454.8 4.2 collective-permute-done.72
  472.8 13.6 %all_to_all.33 = f32[4,64,128]{2,1,0:T(8,128)S(1)} all-to-all(f32[4,64,128]{2,1,0:T(8,128)S(1)} %fusion.10), channel_id=1, replica_groups=mesh['gx'=2,'gy'=4,'col'=4] {'col'}, dimensions={0} | all-to-all | bytes 262144 | tf_op jit(solution)/shard_map/all_to_all | solution.py:78
  488.3 5.8 all_gather.14
  498.2 4.2 collective-permute-done.78
  519.2 4.2 collective-permute-done.84
  536.9 42.2 %psum.60 = f32[]{:T(128)} all-reduce(f32[]{:T(128)} %get-tuple-element.27), channel_id=1, replica_groups=mesh['gx'=2,'gy'=4,'col'=4] {'gx','gy','col'}, use_global_device_ids=true, to_apply=%region_14.16 | all-reduce | flops 1 | bytes 8 | tf_op jit(solution)/shard_map/psum | solution.py:41
  580.5 4.2 collective-permute-start.91
  586.1 4.2 collective-permute-done.90
  605.8 41.6 %psum.61 = f32[]{:T(128)} all-reduce(f32[]{:T(128)} %get-tuple-element.23), channel_id=1, replica_groups=mesh['gx'=2,'gy'=4,'col'=4] {'gx','gy','col'}, use_global_device_ids=true, to_apply=%region_16.18 | all-reduce | flops 1 | bytes 8 | tf_op jit(solution)/shard_map/psum | solution.py:108
  648.8 4.2 collective-permute-start.97
  654.4 4.2 collective-permute-done.96
  676.0 4.2 collective-permute-done.102
  694.0 13.6 %all_to_all.34 = f32[4,64,128]{2,1,0:T(8,128)S(1)} all-to-all(f32[4,64,128]{2,1,0:T(8,128)S(1)} %fusion.8), channel_id=1, replica_groups=mesh['gx'=2,'gy'=4,'col'=4] {'col'}, dimensions={0} | all-to-all | bytes 262144 | tf_op jit(solution)/shard_map/all_to_all | solution.py:78
  709.4 5.8 all_gather.15
  719.4 4.2 collective-permute-done.108
  740.3 4.2 collective-permute-done.114
  758.1 42.2 %psum.62 = f32[]{:T(128)} all-reduce(f32[]{:T(128)} %get-tuple-element.13), channel_id=1, replica_groups=mesh['gx'=2,'gy'=4,'col'=4] {'gx','gy','col'}, use_global_device_ids=true, to_apply=%region_19.21 | all-reduce | flops 1 | bytes 8 | tf_op jit(solution)/shard_map/psum | solution.py:41
  801.7 4.2 collective-permute-start.121
  807.3 4.2 collective-permute-done.120
  827.0 41.6 %psum.63 = f32[]{:T(128)} all-reduce(f32[]{:T(128)} %get-tuple-element.9), channel_id=1, replica_groups=mesh['gx'=2,'gy'=4,'col'=4] {'gx','gy','col'}, use_global_device_ids=true, to_apply=%region_21.23 | all-reduce | flops 1 | bytes 8 | tf_op jit(solution)/shard_map/psum | solution.py:108
  (421 shorter events, 348.6 us)
Async XLA Ops:
  1.5 6.3 collective-permute-start.1
  6.3 5.6 collective-permute-start
  15.4 5.5 collective-permute-start.2
  28.2 5.6 collective-permute-start.6
  37.3 5.5 collective-permute-start.8
  48.4 12.2 %collective-permute-start.13 = (f32[1,32,128]{2,1,0:T(8,128)S(1)}, f32[1,32,128]{2,1,0:T(8,128)S(1)}, u32[]{:S(2)}, u32[]{:S(2)}) collective-permute-start(f32[1,32,128]{2,1,0:T(8,128)S(1)} %get-tuple-element.184), channel_id=1, source_target_pairs={{0,16},{1,17},{2,18},{3,19},{4,20},{5,21},{6,22},{7,23},{8,24},{9,... | collective-permute-start | bytes 49160 | tf_op jit(solution)/shard_map/ppermute | solution.py:23
  50.0 10.6 %collective-permute-start.12 = (f32[1,32,128]{2,1,0:T(8,128)S(1)}, f32[1,32,128]{2,1,0:T(8,128)S(1)}, u32[]{:S(2)}, u32[]{:S(2)}) collective-permute-start(f32[1,32,128]{2,1,0:T(8,128)S(1)} %get-tuple-element.185), channel_id=1, source_target_pairs={{16,0},{17,1},{18,2},{19,3},{20,4},{21,5},{22,6},{23,7},{24,8},{25... | collective-permute-start | bytes 49160 | tf_op jit(solution)/shard_map/ppermute | solution.py:25
  52.2 23.8 %all-to-all-start = ((f32[4,1,64]{2,1,0:T(1,128)}), f32[4,1,64]{2,1,0:T(1,128)S(1)}, u32[]{:S(2)}, u32[]{:S(2)}) async-start(f32[4,1,64]{2,1,0:T(1,128)} %convolution_bitcast_fusion), calls=%async_computation | async-start | bytes 4096 | tf_op jit(solution)/shard_map/all_to_all | solution.py:79
  64.1 5.5 collective-permute-start.14
  76.0 10.9 %all-to-all-start.1 = ((f32[4,64,128]{2,1,0:T(8,128)}), f32[4,64,128]{2,1,0:T(8,128)S(1)}, u32[]{:S(2)}, u32[]{:S(2)}) async-start(f32[4,64,128]{2,1,0:T(8,128)} %fusion.14), calls=%async_computation.1 | async-start | bytes 262144 | tf_op jit(solution)/shard_map/all_to_all | solution.py:78
  95.7 5.8 collective-permute-start.19
  100.1 5.6 collective-permute-start.18
  107.7 5.5 collective-permute-start.20
  120.4 5.6 collective-permute-start.24
  128.0 5.5 collective-permute-start.26
  140.7 5.6 collective-permute-start.30
  148.2 5.5 collective-permute-start.32
  206.3 5.6 collective-permute-start.37
  210.5 5.6 collective-permute-start.36
  220.0 5.5 collective-permute-start.38
  232.7 5.6 collective-permute-start.42
  241.0 5.5 collective-permute-start.44
  276.1 5.6 collective-permute-start.48
  283.7 5.5 collective-permute-start.50
  296.4 5.6 collective-permute-start.54
  303.9 5.5 collective-permute-start.56
  359.3 5.6 collective-permute-start.61
  363.5 5.6 collective-permute-start.60
  373.0 5.5 collective-permute-start.62
  427.6 5.6 collective-permute-start.67
  431.8 5.6 collective-permute-start.66
  440.7 5.5 collective-permute-start.68
  453.4 5.6 collective-permute-start.72
  461.6 5.5 collective-permute-start.74
  496.8 5.6 collective-permute-start.78
  505.0 5.5 collective-permute-start.80
  517.7 5.6 collective-permute-start.84
  525.3 5.5 collective-permute-start.86
  580.5 5.6 collective-permute-start.91
  584.7 5.6 collective-permute-start.90
  594.1 5.5 collective-permute-start.92
  648.8 5.6 collective-permute-start.97
  653.0 5.6 collective-permute-start.96
  674.6 5.6 collective-permute-start.102
  718.0 5.6 collective-permute-start.108
  738.9 5.6 collective-permute-start.114
  801.7 5.6 collective-permute-start.121
  805.8 5.6 collective-permute-start.120
  (86 other events, 429.0 us)
where the time goes:
time: 875 us; the launch traced here: 871 us
  blocking collectives  360 us (41%)
  starting transfers between devices  275 us (31%)
  waiting for transfers between devices  197 us (23%)
  between operations  12.3 us (1%)
  other arithmetic  10.2 us (1%)
  local copies, waits for them, and re-layouts  9.52 us (1%)
    ppermute x63, starting transfers between devices, extended(): lax.ppermute(tail, axis, [(i, (i + 1) % count) for i in range(ends)])  178 us
    ppermute x63, waiting for transfers between devices, extended(): lax.ppermute(head, axis, [((i + 1) % count, i) for i in range(ends)])  172 us
    psum x4, blocking collectives, global_sum(): return lax.psum(local_value, ('gx', 'gy', 'col'))  171 us
    psum x3, blocking collectives, on_device(): curve_sum = lax.psum(jnp.sum(direction * image_vec), ('gx', 'gy', 'col'))  125 us
    ppermute x63, starting transfers between devices, extended(): lax.ppermute(head, axis, [((i + 1) % count, i) for i in range(ends)])  81.6 us
    all_to_all x3, blocking collectives, coarse(): lax.all_to_all(send_rows, 'col', split_axis=0, concat_axis=0, tiled=True)  40.6 us
    all_gather x4, blocking collectives, coarse(): gathered = lax.all_gather(solved, 'col', axis=0, tiled=True)  23.2 us
    ppermute x63, waiting for transfers between devices, extended(): lax.ppermute(tail, axis, [(i, (i + 1) % count) for i in range(ends)])  21.9 us
  transfers between devices with their start and end apart: 128, of which 82 were waited for; matrix products, arithmetic and copies ran while one was open for 0% of the time, Pallas kernels for 0%

commit v1 on v0

v1 whole, which is shorter than its diff:
```python
import functools

import jax
import jax.numpy as jnp
from jax import lax
from jax.experimental import pallas as pl
from jax.experimental.pallas import tpu as pltpu
from jax.sharding import PartitionSpec as P

AGG = 16
ITERS = 4
HALO = 16
LANES = 128
ALL = ("gx", "gy", "col")

w1 = 1.0 / 1.7364
w2 = 1.0 / 0.4636
f32 = jnp.float32


def iota(shape, dim):
    return lax.broadcasted_iota(jnp.int32, shape, dim)


def cross_sums(rows):
    n = rows[0].shape[0]
    lane = iota((n, LANES), 1)
    zero = jnp.zeros((n, LANES), f32)
    ahead = [pltpu.roll(x, 1, 1) for x in rows]
    behind = [pltpu.roll(x, LANES - 1, 1) for x in rows]
    out = []
    for c, x in enumerate(rows):
        left = jnp.where(lane == 0, ahead[c - 1] if c else zero, ahead[c])
        right = jnp.where(lane == LANES - 1, behind[c + 1] if c + 1 < len(rows) else zero, behind[c])
        out.append(left + right + pltpu.roll(x, 1, 0) + pltpu.roll(x, n - 1, 0))
    return out


class Sizes:
    def __init__(self, mesh_shape, cx, cy):
        self.gx, self.gy, self.col = mesh_shape
        self.devices = self.gx * self.gy * self.col
        self.cx, self.cy = cx, cy
        self.planes = self.gx * cx
        self.rows = cy + 2 * HALO
        self.nblock = cx * cy
        self.ngroup = self.nblock * (LANES // AGG) // LANES


def plane_sums(src, i, rows, z):
    mid = [src[i + 1, c, rows] for c in range(z.col)]
    return mid, [
        s + (src[i, c, rows] + src[i + 2, c, rows]) for c, s in enumerate(cross_sums(mid))
    ]


def clear_ends(ref, z):
    zero = jnp.zeros(ref.shape[1:], f32)
    ref[0] = zero
    ref[z.planes + 1] = zero


def each_plane(z, body):
    lax.fori_loop(0, z.planes, lambda i, carry: (body(i), carry)[1], 0)


def presmooth(rho, g, out, rows, z):
    c0, c1 = w1 * (1.0 - w2) + w2, w1 * w2

    def body(i):
        mid, total = plane_sums(rho, i, rows, z)
        for c in range(z.col):
            out[i + 1, c, rows] = c0 * mid[c] + c1 * (g[i, c, rows] * total[c])

    each_plane(z, body)


def smooth(src, rho, g, out, w, rows, z):
    def body(i):
        mid, total = plane_sums(src, i, rows, z)
        for c in range(z.col):
            out[i + 1, c, rows] = (1.0 - w) * mid[c] + w * (
                rho[i + 1, c, rows] + g[i, c, rows] * total[c]
            )

    each_plane(z, body)


def restrict_solve(rho, y2, g, s, hot, inv_t, parts, grouped, msg, rows, z):
    first = lax.axis_index("gx") * z.cx
    own = slice(HALO - rows.start, HALO - rows.start + z.cy)

    def body(k, carry):
        i = first + k
        mid, total = plane_sums(y2, i, rows, z)
        for c in range(z.col):
            gg = g[i, c, rows]
            left = (rho[i + 1, c, rows] - mid[c] + gg * total[c])[own]
            value = left * (s[i, c, rows][own] / gg[own])
            high = value.astype(jnp.bfloat16)
            rest = value - high.astype(f32)
            middle = rest.astype(jnp.bfloat16)
            low = (rest - middle.astype(f32)).astype(jnp.bfloat16)
            for n, part in enumerate((high, middle, low)):
                parts[n, c, k] = part
        return carry

    lax.fori_loop(0, z.cx, body, 0)
    total = jnp.zeros((z.nblock, LANES), f32)
    for n in range(3):
        flat = parts[n].reshape(z.col * z.nblock, LANES)
        total = total + jnp.dot(hot[...], flat, preferred_element_type=f32)
    grouped[...] = total
    per = LANES // AGG
    mask = (iota((per, LANES), 1) // AGG == iota((per, LANES), 0)).astype(f32)

    def solve(c, carry):
        acc = jnp.zeros((per, LANES), f32)
        for half in range(2):
            tile = grouped[pl.ds(pl.multiple_of(c * 16 + half * 8, 8), 8), :]
            for k in range(8):
                value = jnp.broadcast_to(tile[k : k + 1, :], (per, LANES)) * mask
                value = jnp.sum(value, axis=1, keepdims=True)
                acc = acc + value * inv_t[c, (half * 8 + k) * per : (half * 8 + k + 1) * per, :]
        msg[c] = jnp.sum(acc, axis=0, keepdims=True)
        return carry

    lax.fori_loop(0, z.ngroup, solve, 0)


def kernel_first(z, shifted, *refs):
    pieces = refs[: z.col]
    inv_t, g, s, targets, rho, y2, hot, out = refs[z.col : z.col + 8]
    wide, parts, grouped, msg = refs[z.col + 8 :]
    gx, col = lax.axis_index("gx"), lax.axis_index("col")
    clear_ends(wide, z)
    clear_ends(rho, z)
    clear_ends(y2, z)
    r = z.rows
    all_rows = slice(0, r)

    def place(p):
        if not shifted:
            return p
        q = p + gx * z.cx
        return jnp.where(q >= z.planes, q - z.planes, q)

    lane = iota((r, LANES), 1)
    row = iota((r, LANES), 0)

    def unpack(p):
        i = place(p)
        for m in range(z.col):
            c = col ^ m
            value = pieces[m][p, 2 * r : 3 * r, :]
            wide[i + 1, c] = value
            s[i, c] = value
            names = jnp.broadcast_to(pieces[m][p, 3 * r + 2 : 3 * r + 3, :], (r, LANES))
            names = jnp.sum(jnp.where(lane == row, names, 0.0), axis=1, keepdims=True)
            targets[i, c] = jnp.broadcast_to(names, (r, LANES)).astype(jnp.int32)

    each_plane(z, unpack)

    def coefficients(p):
        i = place(p)
        for m in range(z.col):
            c = col ^ m
            x = wide[i + 1, c]
            before = wide[i + 1, jnp.maximum(c - 1, 0)]
            after = wide[i + 1, jnp.minimum(c + 1, z.col - 1)]
            up = jnp.where(row == 0, pieces[m][p, 3 * r : 3 * r + 1, :], pltpu.roll(x, 1, 0))
            down = jnp.where(
                row == r - 1, pieces[m][p, 3 * r + 1 : 3 * r + 2, :], pltpu.roll(x, r - 1, 0)
            )
            left = jnp.where(lane == 0, pltpu.roll(before, 1, 1) * (c > 0).astype(f32), pltpu.roll(x, 1, 1))
            right = jnp.where(
                lane == LANES - 1,
                pltpu.roll(after, LANES - 1, 1) * (c < z.col - 1).astype(f32),
                pltpu.roll(x, LANES - 1, 1),
            )
            total = up + down + left + right + wide[i, c] + wide[i + 2, c]
            diagonal = pieces[m][p, r : 2 * r, :] + x * total
            inside = diagonal > 0.0
            scale = x / jnp.where(inside, diagonal, 1.0)
            scale = jnp.where(inside, scale, 0.0)
            g[i, c] = x * scale
            rho[i + 1, c] = pieces[m][p, 0:r, :] * scale

    each_plane(z, coefficients)
    group = iota((z.nblock, LANES), 0).astype(f32) + (col * z.nblock).astype(f32)
    for m in range(z.col):
        names = pieces[m][0, 3 * r + 3 : 3 * r + 4, :]
        hot[col ^ m] = (jnp.broadcast_to(names, (z.nblock, LANES)) == group).astype(jnp.bfloat16)
    presmooth(rho, g, y2, all_rows, z)
    hots = jnp.concatenate([hot[c] for c in range(z.col)], axis=1)
    restrict_solve(rho, y2, g, s, Whole(hots), inv_t, parts, grouped, msg, all_rows, z)
    for c in range(z.ngroup):
        out[:, c : c + 1, :] = jnp.broadcast_to(msg[c][None], (z.devices, 1, LANES))


class Whole:
    def __init__(self, value):
        self.value = value

    def __getitem__(self, key):
        return self.value


def prolong(recv, table, y2, s, targets, out, z, packed):
    n = z.ngroup
    if packed:

        def unpack(d, carry):
            for c in range(n):
                table[d, c : c + 1, :] = recv[d, :, c * LANES : (c + 1) * LANES]
            return carry

        lax.fori_loop(0, z.devices, unpack, 0)
    else:
        table = recv
    gy = lax.axis_index("gy")
    aggregate = iota((8, LANES), 1) // AGG

    def body(i):
        gx = i // z.cx
        for tile in range(z.rows // 8):
            rows = slice(tile * 8, tile * 8 + 8)
            side = -1 if tile * 8 < HALO else (1 if tile * 8 >= HALO + z.cy else 0)
            layer = jnp.clip(gy + side, 0, z.gy - 1)
            base = (gx * z.gy + layer) * z.col
            tables = [table[base + o] for o in range(z.col)]
            for c in range(z.col):
                t = targets[i, c, rows]
                line = t >> 4
                owner, block = line >> 3, line & 7
                picked = jnp.take_along_axis(tables[0], block, axis=0, mode="promise_in_bounds")
                for o in range(1, z.col):
                    other = jnp.take_along_axis(tables[o], block, axis=0, mode="promise_in_bounds")
                    picked = jnp.where(owner == o, other, picked)
                lane = (t & 15) * 8 + aggregate
                picked = jnp.take_along_axis(picked, lane, axis=1, mode="promise_in_bounds")
                out[i + 1, c, rows] = y2[i + 1, c, rows] + s[i, c, rows] * picked

    each_plane(z, body)


def weighted(a, b, h):
    return jnp.sum(jnp.sum(a * b * h, axis=(0, 1), keepdims=True)[0], axis=1, keepdims=True)


def kernel_next(z, step, *refs):
    first, last = step == 0, step == ITERS - 1
    names = ["recv", "g", "s", "targets", "rho", "y2", "hot", "inv_t"]
    if not first:
        names += ["state"]
    if step >= 2:
        names += ["old", "z_old"]
    outs = ["state_out", "out"]
    if not last:
        outs += ["w_out", "y2_out"]
    if step >= 1 and not last:
        outs += ["z_out"]
    if not first:
        outs += ["old_out"]
    scratch = ["ya", "yb", "table", "parts", "grouped", "msg"]
    k = dict(zip(names + outs + scratch, refs))
    g, s, rho = k["g"], k["s"], k["rho"]
    ya, yb, table = k["ya"], k["yb"], k["table"]
    clear_ends(ya, z)
    clear_ends(yb, z)
    wide_rows = slice(0, z.rows)
    trim = 8 if step >= 1 else 0
    rows = slice(trim, z.rows - trim)
    early = wide_rows if step <= 1 else rows
    prolong(k["recv"], table, k["y2"], s, k["targets"], ya, z, packed=not first)
    smooth(ya, rho, g, yb, w2, early, z)
    smooth(yb, rho, g, ya, w1, early, z)

    gx, col = lax.axis_index("gx"), lax.axis_index("col")
    own_rows = slice(HALO, HALO + z.cy)
    planes = pl.ds(gx * z.cx, z.cx)
    planes1 = pl.ds(gx * z.cx + 1, z.cx)
    h = 1.0 / g[planes, col, own_rows]
    w_new = k["w_out"] if not last else yb
    if first:
        clear_ends(w_new, z)

        def image(i):
            mid, total = plane_sums(ya, i, rows, z)
            for c in range(z.col):
                w_new[i + 1, c, rows] = mid[c] - g[i, c, rows] * total[c]

        each_plane(z, image)
        r, u, w = rho[planes1, col, own_rows], ya[planes1, col, own_rows], w_new[planes1, col, own_rows]
        k["state_out"][0] = r
        k["state_out"][1] = u
        dots = [weighted(r, u, h), weighted(w, u, h)]
    else:
        sums = jnp.zeros((1, LANES), f32)
        lo = z.ngroup * LANES

        def gather(d, acc):
            return acc + k["recv"][d, :, lo : lo + LANES]

        sums = lax.fori_loop(0, z.devices, gather, sums)
        lane1 = iota((1, LANES), 1)
        pick = lambda n: jnp.sum(jnp.where(lane1 == n, sums, 0.0), axis=1, keepdims=True)
        gamma, delta = pick(0), pick(1)
        k["old_out"][...] = jnp.broadcast_to(gamma, (1, LANES))
        if step == 1:
            beta = None
            alpha = gamma / delta
        else:
            beta = gamma / k["old"][0:1, 0:1]
            alpha = gamma / (delta + 2.0 * beta * pick(2) + beta * beta * pick(3))
        trim_new = w_new

        def image(i):
            mid, total = plane_sums(ya, i, rows, z)
            for c in range(z.col):
                n_vec = mid[c] - g[i, c, rows] * total[c]
                if beta is not None:
                    n_vec = n_vec + beta * k["z_old"][i, c, rows]
                if not last:
                    k["z_out"][i, c, rows] = n_vec
                trim_new[i + 1, c, rows] = rho[i + 1, c, rows] - alpha * n_vec

        w_now = rho[planes1, col, own_rows]
        m_now = ya[planes1, col, own_rows]
        if not last:
            clear_ends(w_new, z)
        each_plane(z, image)
        state, state_out = k["state"], k["state_out"]
        r, u = state[0], state[1]
        p, q, sv = u, m_now, w_now
        if beta is not None:
            p, q, sv = p + beta * state[2], q + beta * state[3], sv + beta * state[4]
            x = state[5] + alpha * p
        else:
            x = alpha * p
        r = r - alpha * sv
        u = u - alpha * q
        w = trim_new[planes1, col, own_rows]
        for n, value in enumerate((r, u, p, q, sv, x)):
            state_out[n] = value
        if last:
            state_out[6] = w
        dots = [weighted(r, u, h), weighted(w, u, h), weighted(sv, u, h), weighted(sv, p, h)]

    lane1 = iota((1, LANES), 1)
    line = jnp.zeros((1, LANES), f32)
    for n, value in enumerate(dots):
        line = jnp.where(lane1 == n, value, line)
    out = k["out"]
    if last:
        out[...] = jnp.broadcast_to(line[None], (z.devices, 1, LANES))
        return
    presmooth(w_new, g, k["y2_out"], rows, z)
    clear_ends(k["y2_out"], z)
    restrict_solve(
        w_new, k["y2_out"], g, s, k["hot"], k["inv_t"], k["parts"], k["grouped"], k["msg"], rows, z
    )
    for c in range(z.ngroup):
        out[:, :, c * LANES : (c + 1) * LANES] = jnp.broadcast_to(k["msg"][c][None], (z.devices, 1, LANES))
    lo = z.ngroup * LANES
    out[:, :, lo : lo + LANES] = jnp.broadcast_to(line[None], (z.devices, 1, LANES))


def kernel_last(z, recv, old, state, g, s, x_out, r_out):
    def gather(d, acc):
        return acc + recv[d]

    sums = lax.fori_loop(0, z.devices, gather, jnp.zeros((1, LANES), f32))
    lane1 = iota((1, LANES), 1)
    pick = lambda n: jnp.sum(jnp.where(lane1 == n, sums, 0.0), axis=1, keepdims=True)
    gamma, delta = pick(0), pick(1)
    beta = gamma / old[0:1, 0:1]
    alpha = gamma / (delta + 2.0 * beta * pick(2) + beta * beta * pick(3))
    gx, col = lax.axis_index("gx"), lax.axis_index("col")
    own_rows = slice(HALO, HALO + z.cy)
    for i in range(z.cx):
        gg = g[gx * z.cx + i, col, own_rows]
        ss = s[gx * z.cx + i, col, own_rows]
        p = state[1, i] + beta * state[2, i]
        sv = state[6, i] + beta * state[4, i]
        x_out[i] = (state[5, i] + alpha * p) / ss
        r_out[i] = (state[0, i] - alpha * sv) * (ss / gg)


def call(body, outs, scratch, *args, limit=None, name=None):
    vmem = pl.BlockSpec(memory_space=pltpu.VMEM)
    return pl.pallas_call(
        body,
        out_shape=outs,
        in_specs=[vmem] * len(args),
        out_specs=[vmem] * len(outs),
        scratch_shapes=scratch,
        compiler_params=pltpu.CompilerParams(vmem_limit_bytes=limit or 60 * 1024 * 1024),
        name=name,
    )(*args)


def gather_fields(z, right_side, diag_shift, stiffness, names):
    n_gx, n_gy, n_col = z.gx, z.gy, z.col
    grid_names = jnp.pad(names.reshape(z.cx, 1, z.cy), ((0, 0), (0, 0), (0, LANES - z.cy)))
    flat_names = jnp.broadcast_to(names.reshape(1, 1, z.nblock), (z.cx, 1, LANES))
    own = jnp.concatenate([right_side, diag_shift, stiffness, grid_names, flat_names], axis=1)

    def edge(part, a, b):
        lists = jnp.pad(
            names.reshape(z.cx, 1, z.cy)[:, :, a:b], ((0, 0), (0, 0), (0, LANES - HALO))
        )
        fields = [part(right_side, HALO), part(diag_shift, HALO), part(stiffness, HALO + 1)]
        return jnp.concatenate(fields + [lists], axis=1)

    head = edge(lambda f, n: f[:, :n], 0, HALO)
    tail = edge(lambda f, n: f[:, z.cy - n :], z.cy - HALO, z.cy)

    def pack(own, above, below):
        h = HALO
        n = z.cy
        lists = jnp.concatenate(
            [above[:, 3 * h + 1 :, :h], own[:, 3 * n : 3 * n + 1, :n], below[:, 3 * h + 1 :, :h]], axis=2
        )
        lists = jnp.pad(lists, ((0, 0), (0, 0), (0, LANES - z.rows)))
        return jnp.concatenate(
            [
                above[:, :h], own[:, :n], below[:, :h],
                above[:, h : 2 * h], own[:, n : 2 * n], below[:, h : 2 * h],
                above[:, 2 * h + 1 : 3 * h + 1], own[:, 2 * n : 3 * n], below[:, 2 * h : 3 * h],
                above[:, 2 * h : 2 * h + 1], below[:, 3 * h : 3 * h + 1],
                lists, own[:, 3 * n + 1 :], jnp.zeros((own.shape[0], 4, LANES), f32),
            ],
            axis=1,
        )

    def shift(value, step, swap):
        pairs = []
        for a in range(n_gx):
            for b in range(n_gy):
                if 0 <= b + step < n_gy:
                    pairs.append((a * n_gy + b, (a ^ swap) * n_gy + b + step))
        return lax.ppermute(value, ("gx", "gy"), pairs)

    if n_gx == 2:
        other = shift(own, 0, 1)
        above, below = shift(tail, 1, 0), shift(head, -1, 0)
        above2, below2 = shift(tail, 1, 1), shift(head, -1, 1)
        both = [pack(own, above, below), pack(other, above2, below2)]
        packed = jnp.concatenate(both, axis=0)
    else:
        packed = pack(own, shift(tail, 1, 0), shift(head, -1, 0))
        packed = lax.all_gather(packed, "gx", axis=0, tiled=True)
    pieces = [packed]
    for bit in (2, 1):
        pairs = [(i, i ^ bit) for i in range(n_col)]
        pieces = pieces + [lax.ppermute(piece, "col", pairs) for piece in pieces]
    return [pieces[0], pieces[2], pieces[1], pieces[3]]


def on_device(right_side, diag_shift, stiffness, block_owner, block_group, coarse_inverse):
    cx, cy, depth = right_side.shape
    z = Sizes([lax.axis_size(a) for a in ALL], cx, cy)
    names = (block_owner[0] * z.nblock + block_group[0]).astype(f32)
    pieces = gather_fields(z, right_side, diag_shift, stiffness, names)
    inv_t = jnp.swapaxes(coarse_inverse[0], 1, 2)

    shape = lambda *dims, dtype=f32: jax.ShapeDtypeStruct(dims, dtype)
    field = (z.planes, z.col, z.rows, LANES)
    padded = (z.planes + 2,) + field[1:]
    common = [
        pltpu.VMEM((3, z.col, z.cx, z.cy, LANES), jnp.bfloat16),
        pltpu.VMEM((z.nblock, LANES), f32),
        pltpu.VMEM((z.ngroup, 1, LANES), f32),
    ]
    g, s, targets, rho, y2, hot, msg = call(
        functools.partial(kernel_first, z, z.gx == 2),
        [
            shape(*field), shape(*field), shape(*field, dtype=jnp.int32), shape(*padded), shape(*padded),
            shape(z.col, z.nblock, LANES, dtype=jnp.bfloat16), shape(z.devices, z.ngroup, LANES),
        ],
        [pltpu.VMEM(padded, f32)] + common,
        *pieces, inv_t, name="begin",
    )
    hot = jnp.concatenate([hot[c] for c in range(z.col)], axis=1)
    swap = lambda m: lax.all_to_all(m, ALL, split_axis=0, concat_axis=0, tiled=True)
    state = old = z_old = None
    for step in range(ITERS):
        first, last = step == 0, step == ITERS - 1
        recv = swap(msg)
        args = [recv, g, s, targets, rho, y2, hot, inv_t]
        if not first:
            args += [state]
        if step >= 2:
            args += [old, z_old]
        width = (0 if last else z.ngroup * LANES) + LANES
        outs = [shape(7 if last else 6, cx, cy, LANES), shape(z.devices, 1, width)]
        if not last:
            outs += [shape(*padded), shape(*padded)]
        if step >= 1 and not last:
            outs += [shape(*field)]
        if not first:
            outs += [shape(1, LANES)]
        scratch = [pltpu.VMEM(padded, f32)] * 2 + [pltpu.VMEM((z.devices, z.ngroup, LANES), f32)] + common
        result = list(call(functools.partial(kernel_next, z, step), outs, scratch, *args, name=f"step{step}"))
        state, msg = result[:2]
        result = result[2:]
        if not last:
            rho, y2 = result[:2]
            result = result[2:]
        if step >= 1 and not last:
            z_old = result.pop(0)
        if not first:
            old = result.pop(0)
        else:
            old = None
    recv = swap(msg)
    x, r = call(
        functools.partial(kernel_last, z),
        [shape(cx, cy, LANES), shape(cx, cy, LANES)],
        [],
        recv, old, state, g, s, name="end",
    )
    return x, r


def solution(mesh):
    placed = (
        P("gx", "gy", "col"),
        P("gx", "gy", "col"),
        P("gx", "gy", "col"),
        P(("gx", "gy", "col"), None),
        P(("gx", "gy", "col"), None),
        P(("gx", "gy", "col"), None, None, None),
    )
    return jax.shard_map(
        on_device,
        mesh=mesh,
        in_specs=placed,
        out_specs=(P("gx", "gy", "col"), P("gx", "gy", "col")),
        check_vma=False,
    )
```

time: 875 us -> 174 us (0.20)
  blocking collectives: 360 us -> 45.2 us
  starting transfers between devices: 275 us -> 18.5 us
  waiting for transfers between devices: 197 us -> 33.9 us
  Pallas kernels: 0 us -> 63.1 us
  between operations: 12.3 us -> 0.91 us
    psum x7 -> x0, blocking collectives: 296 us -> none  [the longest x4 171 us: global_sum(): return lax.psum(local_value, ('gx', 'gy', 'col'))]
    ppermute x126 -> x8, starting transfers between devices: 260 us -> 15.1 us  [the longest x5 13.5 us: shift(): return lax.ppermute(value, ('gx', 'gy'), pairs)]
    ppermute x126 -> x8, waiting for transfers between devices: 194 us -> 27.2 us  [the longest x3 16.8 us: gather_fields(): pieces = pieces + [lax.ppermute(piece, 'col', pairs) for piece in pieces]]
    pallas_call x0 -> x6, Pallas kernels: none -> 63.1 us  [call(): pl.pallas_call(body, out_shape=outs, in_specs=[vmem] * len(args), out_spe...]
    all_gather x4 -> x0, blocking collectives: 23.2 us -> none  [coarse(): gathered = lax.all_gather(solved, 'col', axis=0, tiled=True)]
    all_to_all x2 -> x1, starting transfers between devices: 14.7 us -> 3.41 us  [on_device(): lax.all_to_all(m, ALL, split_axis=0, concat_axis=0, tiled=True)]
    all_to_all x3 -> x4, blocking collectives: 40.6 us -> 45.2 us  [on_device(): lax.all_to_all(m, ALL, split_axis=0, concat_axis=0, tiled=True)]
  transfers between devices with their start and end apart: 128 -> 9, of which waited for: 82 -> 4; matrix products, arithmetic and copies ran while one was open for 0% -> 4% of each run, Pallas kernels for 0% -> 0%
where the time goes in v1:
time: 174 us
  Pallas kernels  63.1 us (36%)
  blocking collectives  45.2 us (26%)
  waiting for transfers between devices  33.9 us (19%)
  starting transfers between devices  18.5 us (11%)
  local copies, waits for them, and re-layouts  9.64 us (6%)
  other arithmetic  2.33 us (1%)
    pallas_call x6, Pallas kernels, call(): pl.pallas_call(body, out_shape=outs, in_specs=[vmem] * len(args), out_spe...  63.1 us
    all_to_all x4, blocking collectives, on_device(): lax.all_to_all(m, ALL, split_axis=0, concat_axis=0, tiled=True)  45.2 us
    ppermute x3, waiting for transfers between devices, gather_fields(): pieces = pieces + [lax.ppermute(piece, 'col', pairs) for piece in pieces]  16.8 us
    ppermute x5, starting transfers between devices, shift(): return lax.ppermute(value, ('gx', 'gy'), pairs)  13.5 us
    ppermute x5, waiting for transfers between devices, shift(): return lax.ppermute(value, ('gx', 'gy'), pairs)  10.4 us
    all_to_all x1, waiting for transfers between devices, on_device(): lax.all_to_all(m, ALL, split_axis=0, concat_axis=0, tiled=True)  6.74 us
    unnamed x17, local copies, waits for them, and re-layouts  4.19 us
  transfers between devices with their start and end apart: 9, of which 4 were waited for; matrix products, arithmetic and copies ran while one was open for 4% of the time, Pallas kernels for 0%

profile of v1, /device:TPU:0, one launch (start us, length us, event | category | flops | bytes accessed | tf_op | source)
XLA Modules:
  0.0 173.6 jit_solution(15690464851761772698)
XLA Ops:
  0.6 0.0 copy-start.4
  0.6 0.0 copy-start.6
  0.7 0.0 copy-start.5
  0.7 0.7 convert_reduce_fusion
  1.4 0.1 convert_element_type.29
  1.5 0.1 fusion.8
  1.6 0.9 fusion.7
  2.5 0.8 fusion.5
  3.3 5.9 %collective-permute-start.2 = (f32[4,50,128]{2,1,0:T(8,128)S(1)}, f32[4,50,128]{2,1,0:T(8,128)S(1)}, u32[]{:S(2)}, u32[]{:S(2)}) collective-permute-start(f32[4,50,128]{2,1,0:T(8,128)S(1)} %select_maximum_fusion.1), channel_id=1, source_target_pairs={{0,20},{4,24},{8,28},{16,4},{20,8},{24,12},{1,21},{5,25},{9,29},{1... | collective-permute-start | bytes 307208 | tf_op jit(solution)/shard_map/ppermute | solution.py:443
  9.2 3.5 %collective-permute-start = (f32[4,50,128]{2,1,0:T(8,128)S(1)}, f32[4,50,128]{2,1,0:T(8,128)S(1)}, u32[]{:S(2)}, u32[]{:S(2)}) collective-permute-start(f32[4,50,128]{2,1,0:T(8,128)S(1)} %select_maximum_fusion.1), channel_id=1, source_target_pairs={{0,4},{4,8},{8,12},{16,20},{20,24},{24,28},{1,5},{5,9},{9,13},{17,... | collective-permute-start | bytes 307208 | tf_op jit(solution)/shard_map/ppermute | solution.py:443
  12.7 1.3 collective-permute-start.4
  14.0 1.3 collective-permute-start.1
  15.3 0.7 convert_bitcast_fusion
  16.0 0.0 collective-permute-done
  16.0 5.8 %collective-permute-done.1 = f32[4,50,128]{2,1,0:T(8,128)S(1)} collective-permute-done((f32[4,50,128]{2,1,0:T(8,128)S(1)}, f32[4,50,128]{2,1,0:T(8,128)S(1)}, u32[]{:S(2)}, u32[]{:S(2)}) %collective-permute-start.1) | collective-permute-done | bytes 102432 | tf_op jit(solution)/shard_map/ppermute | solution.py:443
  21.8 0.1 select_maximum_fusion.4
  21.9 2.6 %concatenate.31 = f32[4,98,128]{2,1,0:T(8,128)S(1)} concatenate(f32[4,32,128]{2,1,0:T(8,128)} %param.6, f32[4,32,128]{2,1,0:T(8,128)} %param.7, f32[4,32,128]{2,1,0:T(8,128)} %param.8, f32[4,1,128]{2,1,0:T(1,128)S(1)} %get-tuple-element.80, f32[4,1,128]{2,1,0:T(1,128)S(1)} %broadcast_in_dim.2), dimensions={1} | concatenate | bytes 401408 | tf_op jit(solution)/shard_map/concatenate | solution.py:407
  24.4 1.5 collective-permute-start.3
  26.0 0.0 collective-permute-done.2
  26.1 0.1 concatenate.30
  26.2 0.0 collective-permute-done.4
  26.2 4.5 %collective-permute-done.3 = f32[4,98,128]{2,1,0:T(8,128)S(1)} collective-permute-done((f32[4,98,128]{2,1,0:T(8,128)S(1)}, f32[4,98,128]{2,1,0:T(8,128)S(1)}, u32[]{:S(2)}, u32[]{:S(2)}) %collective-permute-start.3) | collective-permute-done | bytes 200736 | tf_op jit(solution)/shard_map/ppermute | solution.py:443
  30.8 0.1 select_maximum_fusion.2
  30.9 0.1 concatenate.33
  31.0 0.1 pad_maximum_fusion.refs_0_
  31.0 1.6 collective-permute-start.6
  32.6 0.0 collective-permute-start.5
  32.6 16.8 %collective-permute-done.6.refs_2_ = f32[8,200,128]{2,1,0:T(8,128)S(1)} collective-permute-done((f32[8,200,128]{2,1,0:T(8,128)S(1)}, f32[8,200,128]{2,1,0:T(8,128)S(1)}, u32[]{:S(2)}, u32[]{:S(2)}) %collective-permute-start.6) | collective-permute-done | bytes 819232 | tf_op jit(solution)/shard_map/ppermute | solution.py:457
  49.4 0.0 collective-permute-start.7
  49.4 2.4 %copy.12 = f32[1,8,128,128]{2,3,1,0:T(8,128)} copy(f32[1,8,128,128]{3,2,1,0:T(8,128)} %param.11) | data formatting | bytes 1048576 | tf_op args[5]
  51.8 0.0 collective-permute-done.5.refs_1_
  51.9 0.9 copy-done.2
  52.7 0.3 copy-done.3
  53.0 10.3 %begin.1 = (f32[8,4,64,128]{3,2,1,0:T(8,128)}, f32[8,4,64,128]{3,2,1,0:T(8,128)}, s32[8,4,64,128]{3,2,1,0:T(8,128)}, f32[10,4,64,128]{3,2,1,0:T(8,128)}, f32[10,...) custom-call(f32[8,200,128]{2,1,0:T(8,128)} %copy-done, f32[8,200,128]{2,1,0:T(8,128)} %copy-done.2, ...), custom_call_target="tpu_custom_call" | custom-call | tf_op jit(solution)/shard_map/begin/pallas_call | solution.py:392
  63.3 3.4 %all-to-all-start = ((f32[32,8,128]{2,1,0:T(8,128)}), f32[32,8,128]{2,1,0:T(8,128)S(1)}, u32[]{:S(2)}, u32[]{:S(2)}) async-start(f32[32,8,128]{2,1,0:T(8,128)} %get-tuple-element.28), calls=%async_computation | async-start | bytes 262144 | tf_op jit(solution)/shard_map/all_to_all | solution.py:486
  66.7 0.8 slice_bitcast_fusion.3
  67.5 0.7 pad_maximum_fusion.1.refs_6_
  68.2 6.7 %all-to-all-done.refs_0_ = f32[32,8,128]{2,1,0:T(8,128)S(1)} async-done(((f32[32,8,128]{2,1,0:T(8,128)}), f32[32,8,128]{2,1,0:T(8,128)S(1)}, u32[]{:S(2)}, u32[]{:S(2)}) %all-to-all-start) | async-done | bytes 131104 | tf_op jit(solution)/shard_map/all_to_all | solution.py:486
  75.0 0.7 copy-done.7
  75.6 13.1 %step0.1 = (f32[6,4,32,128]{3,2,1,0:T(8,128)}, f32[32,1,1152]{2,1,0:T(1,128)}, f32[10,4,64,128]{3,2,1,0:T(8,128)}, f32[10,4,64,128]{3,2,1,0:T(8,128)}) custom-call(f32[32,8,128]{2,1,0:T(8,128)} %copy-done.7, f32[8,4,64,128]{3,2,1,0:T(8,128)} %get-tuple-element.29.refs_1_.g, f32[8,4,64,128]{3,2,1,0:T(8,128)} %get-tuple-element.30.refs_2_.s, ...), custom_call_target="tpu_custom_call" | custom-call | tf_op jit(solution)/shard_map/step0/pallas_call | solution.py:392
  88.7 11.7 %all_to_all.25.refs_0_ = f32[32,1,1152]{2,1,0:T(1,128)} all-to-all(f32[32,1,1152]{2,1,0:T(1,128)} %get-tuple-element.35), channel_id=1, replica_groups=mesh['gx'=2,'gy'=4,'col'=4] {'gx','gy','col'}, dimensions={0} | all-to-all | bytes 294912 | tf_op jit(solution)/shard_map/all_to_all | solution.py:486
  100.4 13.7 %step1.1 = (f32[6,4,32,128]{3,2,1,0:T(8,128)}, f32[32,1,1152]{2,1,0:T(1,128)}, f32[10,4,64,128]{3,2,1,0:T(8,128)}, f32[10,4,64,128]{3,2,1,0:T(8,128)}, f32[8,4,64,128]{3,2,1,0:T(8,128)}, /*index=5*/f32[1,128]{1,0:T(1,128)}) custom-call(f32[32,1,1152]{2,1,0:T(1,128)} %all_to_all.25.refs_0_, f32[8,4,64,128]{3,2,1,0:T(8,128)} %get-tuple-element.29.refs_1_.g, ...), custom_call_target="tpu_custom_call" | custom-call | tf_op jit(solution)/shard_map/step1/pallas_call | solution.py:392
  114.1 11.7 %all_to_all.26.refs_0_ = f32[32,1,1152]{2,1,0:T(1,128)} all-to-all(f32[32,1,1152]{2,1,0:T(1,128)} %get-tuple-element.39), channel_id=1, replica_groups=mesh['gx'=2,'gy'=4,'col'=4] {'gx','gy','col'}, dimensions={0} | all-to-all | bytes 294912 | tf_op jit(solution)/shard_map/all_to_all | solution.py:486
  125.8 13.8 %step2.1 = (f32[6,4,32,128]{3,2,1,0:T(8,128)}, f32[32,1,1152]{2,1,0:T(1,128)}, f32[10,4,64,128]{3,2,1,0:T(8,128)}, f32[10,4,64,128]{3,2,1,0:T(8,128)}, f32[8,4,64,128]{3,2,1,0:T(8,128)}, /*index=5*/f32[1,128]{1,0:T(1,128)}) custom-call(f32[32,1,1152]{2,1,0:T(1,128)} %all_to_all.26.refs_0_, f32[8,4,64,128]{3,2,1,0:T(8,128)} %get-tuple-element.29.refs_1_.g, ...), custom_call_target="tpu_custom_call" | custom-call | tf_op jit(solution)/shard_map/step2/pallas_call | solution.py:392
  139.6 11.7 %all_to_all.27.refs_0_ = f32[32,1,1152]{2,1,0:T(1,128)} all-to-all(f32[32,1,1152]{2,1,0:T(1,128)} %get-tuple-element.45), channel_id=1, replica_groups=mesh['gx'=2,'gy'=4,'col'=4] {'gx','gy','col'}, dimensions={0} | all-to-all | bytes 294912 | tf_op jit(solution)/shard_map/all_to_all | solution.py:486
  151.3 9.5 %step3.1 = (f32[7,4,32,128]{3,2,1,0:T(8,128)}, f32[32,1,128]{2,1,0:T(1,128)}, f32[1,128]{1,0:T(1,128)}) custom-call(f32[32,1,1152]{2,1,0:T(1,128)} %all_to_all.27.refs_0_, f32[8,4,64,128]{3,2,1,0:T(8,128)} %get-tuple-element.29.refs_1_.g, f32[8,4,64,128]{3,2,1,0:T(8,128)} %get-tuple-element.30.refs_2_.s, s32[8,4,64,128]{3,2,1,0:T(8,128)} %get-tuple-element.31.refs_3_, ...), custom_call_target="tpu_custom_call" | custom-call | tf_op jit(solution)/shard_map/step3/pallas_call | solution.py:392
  160.8 10.1 %all_to_all.28.recv = f32[32,1,128]{2,1,0:T(1,128)} all-to-all(f32[32,1,128]{2,1,0:T(1,128)} %get-tuple-element.51), channel_id=1, replica_groups=mesh['gx'=2,'gy'=4,'col'=4] {'gx','gy','col'}, dimensions={0} | all-to-all | bytes 32768 | tf_op jit(solution)/shard_map/all_to_all | solution.py:486
  171.0 2.6 %end.1 = (f32[4,32,128]{2,1,0:T(8,128)}, f32[4,32,128]{2,1,0:T(8,128)}) custom-call(f32[32,1,128]{2,1,0:T(1,128)} %all_to_all.28.recv, f32[1,128]{1,0:T(1,128)} %get-tuple-element.52.old, f32[7,4,32,128]{3,2,1,0:T(8,128)} %get-tuple-element.53.state, f32[8,4,64,128]{3,2,1,0:T(8,128)} %get-tuple-element.29.refs_1_.g, ...), custom_call_target="tpu_custom_call" | custom-call | tf_op jit(solution)/shard_map/end/pallas_call | solution.py:392
  (30 shorter events, 0.1 us)
Async XLA Ops:
  0.6 25.5 %copy-start.4 = (f32[4,32,128]{2,1,0:T(8,128)S(1)}, f32[4,32,128]{2,1,0:T(8,128)}, u32[]{:S(2)}) copy-start(f32[4,32,128]{2,1,0:T(8,128)} %param.8) | copy-start | bytes 196612
  0.6 25.5 %copy-start.6 = (f32[4,32,128]{2,1,0:T(8,128)S(1)}, f32[4,32,128]{2,1,0:T(8,128)}, u32[]{:S(2)}) copy-start(f32[4,32,128]{2,1,0:T(8,128)} %param.7) | copy-start | bytes 196612
  0.7 25.5 %copy-start.5 = (f32[4,32,128]{2,1,0:T(8,128)S(1)}, f32[4,32,128]{2,1,0:T(8,128)}, u32[]{:S(2)}) copy-start(f32[4,32,128]{2,1,0:T(8,128)} %param.6) | copy-start | bytes 196612
  3.3 22.7 %collective-permute-start.2 = (f32[4,50,128]{2,1,0:T(8,128)S(1)}, f32[4,50,128]{2,1,0:T(8,128)S(1)}, u32[]{:S(2)}, u32[]{:S(2)}) collective-permute-start(f32[4,50,128]{2,1,0:T(8,128)S(1)} %select_maximum_fusion.1), channel_id=1, source_target_pairs={{0,20},{4,24},{8,28},{16,4},{20,8},{24,12},{1,21},{5,25},{9,29},{1... | collective-permute-start | bytes 307208 | tf_op jit(solution)/shard_map/ppermute | solution.py:443
  9.2 6.8 %collective-permute-start = (f32[4,50,128]{2,1,0:T(8,128)S(1)}, f32[4,50,128]{2,1,0:T(8,128)S(1)}, u32[]{:S(2)}, u32[]{:S(2)}) collective-permute-start(f32[4,50,128]{2,1,0:T(8,128)S(1)} %select_maximum_fusion.1), channel_id=1, source_target_pairs={{0,4},{4,8},{8,12},{16,20},{20,24},{24,28},{1,5},{5,9},{9,13},{17,... | collective-permute-start | bytes 307208 | tf_op jit(solution)/shard_map/ppermute | solution.py:443
  12.7 13.5 %collective-permute-start.4 = (f32[4,50,128]{2,1,0:T(8,128)S(1)}, f32[4,50,128]{2,1,0:T(8,128)S(1)}, u32[]{:S(2)}, u32[]{:S(2)}) collective-permute-start(f32[4,50,128]{2,1,0:T(8,128)S(1)} %select_maximum_fusion), channel_id=1, source_target_pairs={{4,16},{8,20},{12,24},{20,0},{24,4},{28,8},{5,17},{9,21},{13,25},{... | collective-permute-start | bytes 307208 | tf_op jit(solution)/shard_map/ppermute | solution.py:443
  14.0 7.8 %collective-permute-start.1 = (f32[4,50,128]{2,1,0:T(8,128)S(1)}, f32[4,50,128]{2,1,0:T(8,128)S(1)}, u32[]{:S(2)}, u32[]{:S(2)}) collective-permute-start(f32[4,50,128]{2,1,0:T(8,128)S(1)} %select_maximum_fusion), channel_id=1, source_target_pairs={{4,0},{8,4},{12,8},{20,16},{24,20},{28,24},{5,1},{9,5},{13,9},{21,... | collective-permute-start | bytes 307208 | tf_op jit(solution)/shard_map/ppermute | solution.py:443
  24.4 6.3 %collective-permute-start.3 = (f32[4,98,128]{2,1,0:T(8,128)S(1)}, f32[4,98,128]{2,1,0:T(8,128)S(1)}, u32[]{:S(2)}, u32[]{:S(2)}) collective-permute-start(f32[4,98,128]{2,1,0:T(8,128)S(1)} %concatenate.31), channel_id=1, source_target_pairs={{0,16},{4,20},{8,24},{12,28},{16,0},{20,4},{24,8},{28,12},{1,17},{... | collective-permute-start | bytes 602120 | tf_op jit(solution)/shard_map/ppermute | solution.py:443
  31.0 20.8 %copy-start = (f32[8,200,128]{2,1,0:T(8,128)}, f32[8,200,128]{2,1,0:T(8,128)S(1)}, u32[]{:S(2)}) copy-start(f32[8,200,128]{2,1,0:T(8,128)S(1)} %pad_maximum_fusion.refs_0_) | copy-start | bytes 2457604
  31.0 18.4 %collective-permute-start.6 = (f32[8,200,128]{2,1,0:T(8,128)S(1)}, f32[8,200,128]{2,1,0:T(8,128)S(1)}, u32[]{:S(2)}, u32[]{:S(2)}) collective-permute-start(f32[8,200,128]{2,1,0:T(8,128)S(1)} %pad_maximum_fusion.refs_0_), channel_id=1, source_target_pairs={{0,2},{1,3},{2,0},{3,1},{4,6},{5,7},{6,4},{7,5},{8,10},{9,11},{10,... | collective-permute-start | bytes 2457608 | tf_op jit(solution)/shard_map/ppermute | solution.py:457
  32.6 19.2 %collective-permute-start.5 = (f32[8,200,128]{2,1,0:T(8,128)S(1)}, f32[8,200,128]{2,1,0:T(8,128)S(1)}, u32[]{:S(2)}, u32[]{:S(2)}) collective-permute-start(f32[8,200,128]{2,1,0:T(8,128)S(1)} %pad_maximum_fusion.refs_0_), channel_id=1, source_target_pairs={{0,1},{1,0},{2,3},{3,2},{4,5},{5,4},{6,7},{7,6},{8,9},{9,8},{10,11... | collective-permute-start | bytes 2457608 | tf_op jit(solution)/shard_map/ppermute | solution.py:457
  49.4 2.4 %copy-start.1 = (f32[8,200,128]{2,1,0:T(8,128)}, f32[8,200,128]{2,1,0:T(8,128)S(1)}, u32[]{:S(2)}) copy-start(f32[8,200,128]{2,1,0:T(8,128)S(1)} %collective-permute-done.6.refs_2_) | copy-start | bytes 2457604
  49.4 2.4 %collective-permute-start.7 = (f32[8,200,128]{2,1,0:T(8,128)S(1)}, f32[8,200,128]{2,1,0:T(8,128)S(1)}, u32[]{:S(2)}, u32[]{:S(2)}) collective-permute-start(f32[8,200,128]{2,1,0:T(8,128)S(1)} %collective-permute-done.6.refs_2_), channel_id=1, source_target_pairs={{0,1},{1,0},{2,3},{3,2},{4,5},{5,4},{6,7},{7,6},{8,9},{9,8},{10,11... | collective-permute-start | bytes 2457608 | tf_op jit(solution)/shard_map/ppermute | solution.py:457
  51.8 0.9 copy-start.2
  51.8 1.2 copy-start.3
  63.3 11.6 %all-to-all-start = ((f32[32,8,128]{2,1,0:T(8,128)}), f32[32,8,128]{2,1,0:T(8,128)S(1)}, u32[]{:S(2)}, u32[]{:S(2)}) async-start(f32[32,8,128]{2,1,0:T(8,128)} %get-tuple-element.28), calls=%async_computation | async-start | bytes 262144 | tf_op jit(solution)/shard_map/all_to_all | solution.py:486
  75.0 0.7 copy-start.7

commit v2 on v1

v2 whole, which is shorter than its diff:
```python
import functools

import jax
import jax.numpy as jnp
from jax import lax
from jax.experimental import pallas as pl
from jax.experimental.pallas import tpu as pltpu
from jax.sharding import PartitionSpec as P

AGG = 16
ITERS = 4
HALO = 16
LANES = 128
ALL = ("gx", "gy", "col")

w1 = 1.0 / 1.7364
w2 = 1.0 / 0.4636
f32 = jnp.float32


def iota(shape, dim):
    return lax.broadcasted_iota(jnp.int32, shape, dim)


class Sizes:
    def __init__(self, mesh_shape, cx, cy):
        self.gx, self.gy, self.col = mesh_shape
        self.devices = self.gx * self.gy * self.col
        self.cx, self.cy = cx, cy
        self.planes = self.gx * cx
        self.rows = cy + 2 * HALO
        self.nblock = cx * cy
        self.ngroup = self.nblock * (LANES // AGG) // LANES


PAD = 8


def plain(t):
    return pl.ds(pl.multiple_of(t * 8, 8), 8)


def inner(t):
    return pl.ds(pl.multiple_of(t * 8 + PAD, 8), 8)


def row_sums(src, i, t, mid, z):
    lane = iota((8, LANES), 1)
    zero = jnp.zeros((8, LANES), f32)
    ahead = [pltpu.roll(x, 1, 1) for x in mid]
    behind = [pltpu.roll(x, LANES - 1, 1) for x in mid]
    out = []
    for c in range(z.col):
        left = jnp.where(lane == 0, ahead[c - 1] if c else zero, ahead[c])
        right = jnp.where(lane == LANES - 1, behind[c + 1] if c + 1 < z.col else zero, behind[c])
        up = src[i, c, pl.ds(t * 8 + PAD - 1, 8)]
        down = src[i, c, pl.ds(t * 8 + PAD + 1, 8)]
        out.append((left + right) + (up + down))
    return out


def sweep(src, tiles, z, visit):
    def body(t, carry):
        load = lambda i: [src[i, c, inner(t)] for c in range(z.col)]
        below, mid = load(0), load(1)
        for i in range(z.planes):
            above = load(i + 2)
            across = row_sums(src, i + 1, t, mid, z)
            for c in range(z.col):
                visit(i, t, c, mid[c], across[c] + (below[c] + above[c]))
            below, mid = mid, above
        return carry

    lax.fori_loop(tiles[0], tiles[1], body, 0)


def clear_ends(ref, z):
    zero = jnp.zeros(ref.shape[1:], f32)
    ref[0] = zero
    ref[z.planes + 1] = zero


def presmooth(rho, g, out, tiles, z):
    c0, c1 = w1 * (1.0 - w2) + w2, w1 * w2

    def visit(i, t, c, value, total):
        out[i + 1, c, inner(t)] = c0 * value + (c1 * g[i, c, plain(t)]) * total

    sweep(rho, tiles, z, visit)


def smooth(src, rho, g, out, w, tiles, z):
    def visit(i, t, c, value, total):
        out[i + 1, c, inner(t)] = (1.0 - w) * value + w * (
            rho[i + 1, c, inner(t)] + g[i, c, plain(t)] * total
        )

    sweep(src, tiles, z, visit)


def restrict_solve(rho, y2, g, s, hot, inv_t, parts, grouped, msg, z):
    first = lax.axis_index("gx") * z.cx
    col = lax.axis_index("col")

    def body(k, carry):
        i = first + k
        for j in range(z.cy // 8):
            t = HALO // 8 + j
            mid = [y2[i + 1, c, inner(t)] for c in range(z.col)]
            across = row_sums(y2, i + 1, t + 0 * k, mid, z)
            for c in range(z.col):
                total = across[c] + (y2[i, c, inner(t)] + y2[i + 2, c, inner(t)])
                gg = g[i, c, plain(t)]
                value = (rho[i + 1, c, inner(t)] - mid[c] + gg * total) * (s[i, c, plain(t)] / gg)
                high = value.astype(jnp.bfloat16).astype(f32)
                middle = (value - high).astype(jnp.bfloat16).astype(f32)
                low = value - high - middle
                for n, part in enumerate((high, middle, low)):
                    parts[n, c ^ col, k, j * 8 : j * 8 + 8] = part
        return carry

    lax.fori_loop(0, z.cx, body, 0)
    total = jnp.zeros((z.nblock, LANES), f32)
    for n in range(3):
        flat = parts[n].reshape(z.col * z.nblock, LANES).astype(jnp.bfloat16)
        total = total + jnp.dot(hot[...], flat, preferred_element_type=f32)
    grouped[...] = total
    per = LANES // AGG
    mask = (iota((per, LANES), 1) // AGG == iota((per, LANES), 0)).astype(f32)

    def solve(c, carry):
        acc = jnp.zeros((per, LANES), f32)
        for half in range(2):
            tile = grouped[pl.ds(pl.multiple_of(c * 16 + half * 8, 8), 8), :]
            for k in range(8):
                value = jnp.broadcast_to(tile[k : k + 1, :], (per, LANES)) * mask
                value = jnp.sum(value, axis=1, keepdims=True)
                acc = acc + value * inv_t[c, (half * 8 + k) * per : (half * 8 + k + 1) * per, :]
        msg[c] = jnp.sum(acc, axis=0, keepdims=True)
        return carry

    lax.fori_loop(0, z.ngroup, solve, 0)


def list_row(owner, group, z):
    return (owner[...] * z.nblock + group[...]).astype(f32)


def kernel_edges(z, r, d, s, owner, group, head, tail):
    h, n = HALO, z.cy
    names = list_row(owner, group, z)
    for out, rows, extra, first in ((head, slice(0, h), h, 0), (tail, slice(n - h, n), n - h - 1, n - h)):
        for k, field in enumerate((r, d, s)):
            out[:, k * h : (k + 1) * h] = field[:, rows]
        out[:, 3 * h : 3 * h + 8] = jnp.zeros((z.cx, 8, LANES), f32)
        out[:, 3 * h : 3 * h + 1] = s[:, extra : extra + 1]
        for i in range(z.cx):
            turn = (i * n + first) % LANES
            out[i, 3 * h + 1 : 3 * h + 2] = pltpu.roll(names, (LANES - turn) % LANES, 1) if turn else names


def kernel_pack(z, r, d, s, owner, group, above, below, out):
    h, n, m = HALO, z.cy, z.rows
    names = list_row(owner, group, z)
    lane = iota((1, LANES), 1)
    for k, field in enumerate((r, d, s)):
        out[:, k * m : k * m + h] = above[:, k * h : (k + 1) * h]
        out[:, k * m + h : k * m + h + n] = field[...]
        out[:, k * m + h + n : (k + 1) * m] = below[:, k * h : (k + 1) * h]
    out[:, 3 * m : 3 * m + 8] = jnp.zeros((z.cx, 8, LANES), f32)
    out[:, 3 * m : 3 * m + 1] = above[:, 3 * h : 3 * h + 1]
    out[:, 3 * m + 1 : 3 * m + 2] = below[:, 3 * h : 3 * h + 1]
    for i in range(z.cx):
        turn = (LANES + h - i * n) % LANES
        mine = pltpu.roll(names, turn, 1) if turn else names
        left = above[i, 3 * h + 1 : 3 * h + 2]
        right = pltpu.roll(below[i, 3 * h + 1 : 3 * h + 2], h + n, 1)
        out[i, 3 * m + 2 : 3 * m + 3] = jnp.where(lane < h, left, jnp.where(lane < h + n, mine, right))
        out[i, 3 * m + 3 : 3 * m + 4] = names


def kernel_first(z, layout, *refs):
    pieces = refs[: len(layout)]
    refs = refs[len(layout) :]
    inv_t, g, s, targets, rho, y2, hot, out = refs[:8]
    parts, grouped, msg = refs[8:]
    wide = y2
    gx, col = lax.axis_index("gx"), lax.axis_index("col")
    clear_ends(rho, z)
    clear_ends(y2, z)
    r = z.rows
    tiles = (0, r // 8)

    lane = iota((r, LANES), 1)
    row = iota((r, LANES), 0)

    def unpack(piece, c, i, p):
        rho[i + 1, c, PAD : PAD + r] = piece[p, 0:r]
        g[i, c] = piece[p, r : 2 * r]
        wide[i + 1, c, PAD : PAD + r] = piece[p, 2 * r : 3 * r]
        wide[i + 1, c, PAD - 1 : PAD] = piece[p, 3 * r : 3 * r + 1]
        wide[i + 1, c, PAD + r : PAD + r + 1] = piece[p, 3 * r + 1 : 3 * r + 2]
        names = jnp.broadcast_to(piece[p, 3 * r + 2 : 3 * r + 3], (r, LANES))
        names = jnp.sum(jnp.where(lane == row, names, 0.0), axis=1, keepdims=True)
        targets[i, c] = jnp.broadcast_to(names, (r, LANES)).astype(jnp.int32)

    for piece, (m, start, rotated) in zip(pieces, layout):

        def each(p, carry, piece=piece, m=m, start=start, rotated=rotated):
            i = p + start
            if rotated:
                i = i + gx * z.cx
                i = jnp.where(i >= z.planes, i - z.planes, i)
            unpack(piece, col ^ m, i, p)
            return carry

        lax.fori_loop(0, piece.shape[0], each, 0)

    def coefficients(i, t, c, x, total):
        diagonal = g[i, c, plain(t)] + x * total
        inside = diagonal > 0.0
        scale = jnp.where(inside, x / jnp.where(inside, diagonal, 1.0), 0.0)
        s[i, c, plain(t)] = x
        g[i, c, plain(t)] = x * scale
        rho[i + 1, c, inner(t)] = rho[i + 1, c, inner(t)] * scale

    sweep(wide, tiles, z, coefficients)
    group = iota((z.nblock, LANES), 0).astype(f32) + (col * z.nblock).astype(f32)
    for piece, (m, start, _) in zip(pieces, layout):
        if start:
            continue
        names = piece[0 if _ else gx * z.cx, 3 * r + 3 : 3 * r + 4, :].reshape(1, LANES)
        match = jnp.broadcast_to(names, (z.nblock, LANES)) == group
        hot[:, m * LANES : (m + 1) * LANES] = match.astype(jnp.bfloat16)
    presmooth(rho, g, y2, tiles, z)
    restrict_solve(rho, y2, g, s, hot, inv_t, parts, grouped, msg, z)
    for c in range(z.ngroup):
        out[:, c : c + 1, :] = jnp.broadcast_to(msg[c][None], (z.devices, 1, LANES))


def prolong(recv, table, y2, s, targets, out, tiles, z, packed):
    n = z.ngroup
    if packed:

        def unpack(d, carry):
            for c in range(n):
                table[d, c : c + 1, :] = recv[d, :, c * LANES : (c + 1) * LANES]
            return carry

        lax.fori_loop(0, z.devices, unpack, 0)
    else:
        table = recv
    gy = lax.axis_index("gy")
    aggregate = iota((8, LANES), 1) // AGG

    tiles = tuple(range(tiles[0], tiles[1]))

    def body(i, carry):
        gx = i // z.cx
        for tile in tiles:
            side = -1 if tile * 8 < HALO else (1 if tile * 8 >= HALO + z.cy else 0)
            layer = jnp.clip(gy + side, 0, z.gy - 1)
            base = (gx * z.gy + layer) * z.col
            tables = [table[base + o] for o in range(z.col)]
            for c in range(z.col):
                t = targets[i, c, plain(tile)]
                line = t >> 4
                owner, block = line >> 3, line & 7
                picked = jnp.take_along_axis(tables[0], block, axis=0, mode="promise_in_bounds")
                for o in range(1, z.col):
                    other = jnp.take_along_axis(tables[o], block, axis=0, mode="promise_in_bounds")
                    picked = jnp.where(owner == o, other, picked)
                lane = (t & 15) * 8 + aggregate
                picked = jnp.take_along_axis(picked, lane, axis=1, mode="promise_in_bounds")
                out[i + 1, c, inner(tile)] = y2[i + 1, c, inner(tile)] + s[i, c, plain(tile)] * picked
        return carry

    lax.fori_loop(0, z.planes, body, 0)


def weighted(a, b, h):
    return jnp.sum(jnp.sum(a * b * h, axis=(0, 1), keepdims=True)[0], axis=1, keepdims=True)


def kernel_next(z, step, *refs):
    first, last = step == 0, step == ITERS - 1
    names = ["recv", "g", "s", "targets", "rho", "y2", "hot", "inv_t"]
    if not first:
        names += ["state"]
    if step >= 2:
        names += ["old", "z_old"]
    outs = ["state_out", "out"]
    if not last:
        outs += ["w_out", "y2_out"]
    if step >= 1 and not last:
        outs += ["z_out"]
    if not first:
        outs += ["old_out"]
    scratch = ["table", "parts", "grouped", "msg"] + (["y2_out", "w_out"] if last else [])
    k = dict(zip(names + outs + scratch, refs))
    g, s, rho = k["g"], k["s"], k["rho"]
    ya, yb, table = k["y2_out"], k["w_out"], k["table"]
    clear_ends(ya, z)
    clear_ends(yb, z)
    trim = 1 if step >= 1 else 0
    rows = (trim, z.rows // 8 - trim)
    early = (0, z.rows // 8) if step <= 1 else rows
    prolong(k["recv"], table, k["y2"], s, k["targets"], ya, early, z, packed=not first)
    smooth(ya, rho, g, yb, w2, early, z)
    smooth(yb, rho, g, ya, w1, early, z)

    gx, col = lax.axis_index("gx"), lax.axis_index("col")
    own_rows = slice(HALO, HALO + z.cy)
    own_inner = slice(HALO + PAD, HALO + PAD + z.cy)
    planes = pl.ds(gx * z.cx, z.cx)
    planes1 = pl.ds(gx * z.cx + 1, z.cx)
    h = 1.0 / g[planes, col, own_rows]
    w_new = yb
    if first:

        def image(i, t, c, value, total):
            w_new[i + 1, c, inner(t)] = value - g[i, c, plain(t)] * total

        sweep(ya, rows, z, image)
        r, u, w = (ref[planes1, col, own_inner] for ref in (rho, ya, w_new))
        k["state_out"][0] = r
        k["state_out"][1] = u
        dots = [weighted(r, u, h), weighted(w, u, h)]
    else:
        sums = jnp.zeros((1, LANES), f32)
        lo = z.ngroup * LANES

        def gather(d, acc):
            return acc + k["recv"][d, :, lo : lo + LANES]

        sums = lax.fori_loop(0, z.devices, gather, sums)
        lane1 = iota((1, LANES), 1)
        pick = lambda n: jnp.sum(jnp.where(lane1 == n, sums, 0.0), axis=1, keepdims=True)
        gamma, delta = pick(0), pick(1)
        k["old_out"][...] = jnp.broadcast_to(gamma, (1, LANES))
        if step == 1:
            beta = None
            alpha = gamma / delta
        else:
            beta = gamma / k["old"][0:1, 0:1]
            alpha = gamma / (delta + 2.0 * beta * pick(2) + beta * beta * pick(3))

        def image(i, t, c, value, total):
            n_vec = value - g[i, c, plain(t)] * total
            if beta is not None:
                n_vec = n_vec + beta * k["z_old"][i, c, plain(t)]
            if not last:
                k["z_out"][i, c, plain(t)] = n_vec
            w_new[i + 1, c, inner(t)] = rho[i + 1, c, inner(t)] - alpha * n_vec

        w_now = rho[planes1, col, own_inner]
        m_now = ya[planes1, col, own_inner]
        sweep(ya, rows, z, image)
        state, state_out = k["state"], k["state_out"]
        r, u = state[0], state[1]
        p, q, sv = u, m_now, w_now
        if beta is not None:
            p, q, sv = p + beta * state[2], q + beta * state[3], sv + beta * state[4]
            x = state[5] + alpha * p
        else:
            x = alpha * p
        r = r - alpha * sv
        u = u - alpha * q
        w = w_new[planes1, col, own_inner]
        for n, value in enumerate((r, u, p, q, sv, x)):
            state_out[n] = value
        if last:
            state_out[6] = w
        dots = [weighted(r, u, h), weighted(w, u, h), weighted(sv, u, h), weighted(sv, p, h)]

    lane1 = iota((1, LANES), 1)
    line = jnp.zeros((1, LANES), f32)
    for n, value in enumerate(dots):
        line = jnp.where(lane1 == n, value, line)
    out = k["out"]
    if last:
        out[...] = jnp.broadcast_to(line[None], (z.devices, 1, LANES))
        return
    presmooth(w_new, g, k["y2_out"], rows, z)
    restrict_solve(
        w_new, k["y2_out"], g, s, k["hot"], k["inv_t"], k["parts"], k["grouped"], k["msg"], z
    )
    for c in range(z.ngroup):
        out[:, :, c * LANES : (c + 1) * LANES] = jnp.broadcast_to(k["msg"][c][None], (z.devices, 1, LANES))
    lo = z.ngroup * LANES
    out[:, :, lo : lo + LANES] = jnp.broadcast_to(line[None], (z.devices, 1, LANES))


def kernel_last(z, recv, old, state, g, s, x_out, r_out):
    def gather(d, acc):
        return acc + recv[d]

    sums = lax.fori_loop(0, z.devices, gather, jnp.zeros((1, LANES), f32))
    lane1 = iota((1, LANES), 1)
    pick = lambda n: jnp.sum(jnp.where(lane1 == n, sums, 0.0), axis=1, keepdims=True)
    gamma, delta = pick(0), pick(1)
    beta = gamma / old[0:1, 0:1]
    alpha = gamma / (delta + 2.0 * beta * pick(2) + beta * beta * pick(3))
    gx, col = lax.axis_index("gx"), lax.axis_index("col")
    own_rows = slice(HALO, HALO + z.cy)
    for i in range(z.cx):
        gg = g[gx * z.cx + i, col, own_rows]
        ss = s[gx * z.cx + i, col, own_rows]
        p = state[1, i] + beta * state[2, i]
        sv = state[6, i] + beta * state[4, i]
        x_out[i] = (state[5, i] + alpha * p) / ss
        r_out[i] = (state[0, i] - alpha * sv) * (ss / gg)


def call(z, body, outs, scratch, *args, name=None):
    room = 13 * (z.planes + 2) * z.col * z.rows * LANES * 4
    vmem = pl.BlockSpec(memory_space=pltpu.VMEM)
    return pl.pallas_call(
        body,
        out_shape=outs,
        in_specs=[vmem] * len(args),
        out_specs=[vmem] * len(outs),
        scratch_shapes=scratch,
        compiler_params=pltpu.CompilerParams(vmem_limit_bytes=min(room, 60 * 1024 * 1024)),
        name=name,
    )(*args)


def gather_fields(z, right_side, diag_shift, stiffness, owner, group):
    fields = (right_side, diag_shift, stiffness, owner, group)
    edge = jax.ShapeDtypeStruct((z.cx, 3 * HALO + 8, LANES), f32)
    head, tail = call(z, functools.partial(kernel_edges, z), [edge, edge], [], *fields, name="edges")
    above = lax.ppermute(tail, "gy", [(i, i + 1) for i in range(z.gy - 1)])
    below = lax.ppermute(head, "gy", [(i + 1, i) for i in range(z.gy - 1)])
    (packed,) = call(
        z, functools.partial(kernel_pack, z), [jax.ShapeDtypeStruct((z.cx, 3 * z.rows + 8, LANES), f32)],
        [], *fields, above, below, name="pack",
    )

    def turn(value, bit):
        return lax.ppermute(value, "col", [(i, i ^ bit) for i in range(z.col)])

    if z.gx == 2:
        swap = lambda value: lax.ppermute(value, "gx", [(0, 1), (1, 0)])
        cut = z.cx // 2
        across, beside = swap(packed), turn(packed, 2)
        corner_low, corner_high = turn(across[:cut], 2), swap(beside[cut:])
        pieces = [(packed, 0, 0), (across, 0, z.cx), (beside, 2, 0)]
        pieces += [(corner_low, 2, z.cx), (corner_high, 2, z.cx + cut)]
        rotated = True
    else:
        packed = lax.all_gather(packed, "gx", axis=0, tiled=True)
        pieces = [(packed, 0, 0), (turn(packed, 2), 2, 0)]
        rotated = False
    pieces = pieces + [(turn(value, 1), m ^ 1, start) for value, m, start in pieces]
    return [value for value, _, _ in pieces], [(m, start, rotated) for _, m, start in pieces]


def on_device(right_side, diag_shift, stiffness, block_owner, block_group, coarse_inverse):
    cx, cy, depth = right_side.shape
    z = Sizes([lax.axis_size(a) for a in ALL], cx, cy)
    pieces, layout = gather_fields(z, right_side, diag_shift, stiffness, block_owner, block_group)
    inv_t = jnp.swapaxes(coarse_inverse[0], 1, 2)

    shape = lambda *dims, dtype=f32: jax.ShapeDtypeStruct(dims, dtype)
    field = (z.planes, z.col, z.rows, LANES)
    padded = (z.planes + 2, z.col, z.rows + 2 * PAD, LANES)
    common = [
        pltpu.VMEM((3, z.col, z.cx, z.cy, LANES), f32),
        pltpu.VMEM((z.nblock, LANES), f32),
        pltpu.VMEM((z.ngroup, 1, LANES), f32),
    ]
    g, s, targets, rho, y2, hot, msg = call(
        z,
        functools.partial(kernel_first, z, layout),
        [
            shape(*field), shape(*field), shape(*field, dtype=jnp.int32), shape(*padded), shape(*padded),
            shape(z.nblock, z.col * LANES, dtype=jnp.bfloat16), shape(z.devices, z.ngroup, LANES),
        ],
        common,
        *pieces, inv_t, name="begin",
    )
    swap = lambda m: lax.all_to_all(m, ALL, split_axis=0, concat_axis=0, tiled=True)
    state = old = z_old = None
    for step in range(ITERS):
        first, last = step == 0, step == ITERS - 1
        recv = swap(msg)
        args = [recv, g, s, targets, rho, y2, hot, inv_t]
        if not first:
            args += [state]
        if step >= 2:
            args += [old, z_old]
        width = (0 if last else z.ngroup * LANES) + LANES
        outs = [shape(7 if last else 6, cx, cy, LANES), shape(z.devices, 1, width)]
        if not last:
            outs += [shape(*padded), shape(*padded)]
        if step >= 1 and not last:
            outs += [shape(*field)]
        if not first:
            outs += [shape(1, LANES)]
        scratch = [pltpu.VMEM((z.devices, z.ngroup, LANES), f32)] + common
        if last:
            scratch += [pltpu.VMEM(padded, f32)] * 2
        result = list(call(z, functools.partial(kernel_next, z, step), outs, scratch, *args, name=f"step{step}"))
        state, msg = result[:2]
        result = result[2:]
        if not last:
            rho, y2 = result[:2]
            result = result[2:]
        if step >= 1 and not last:
            z_old = result.pop(0)
        if not first:
            old = result.pop(0)
        else:
            old = None
    recv = swap(msg)
    x, r = call(
        z,
        functools.partial(kernel_last, z),
        [shape(cx, cy, LANES), shape(cx, cy, LANES)],
        [],
        recv, old, state, g, s, name="end",
    )
    return x, r


def solution(mesh):
    placed = (
        P("gx", "gy", "col"),
        P("gx", "gy", "col"),
        P("gx", "gy", "col"),
        P(("gx", "gy", "col"), None),
        P(("gx", "gy", "col"), None),
        P(("gx", "gy", "col"), None, None, None),
    )
    return jax.shard_map(
        on_device,
        mesh=mesh,
        in_specs=placed,
        out_specs=(P("gx", "gy", "col"), P("gx", "gy", "col")),
        check_vma=False,
    )
```

time: 174 us -> 124 us (0.71)
  Pallas kernels: 63.1 us -> 36 us
  waiting for transfers between devices: 33.9 us -> 17.5 us
  starting transfers between devices: 18.5 us -> 12.2 us
  blocking collectives: 45.2 us -> 51.5 us
  local copies, waits for them, and re-layouts: 9.64 us -> 5.09 us
  other arithmetic: 2.33 us -> 0 us
    pallas_call x6 -> x8, Pallas kernels: 63.1 us -> 36 us  [call(): pl.pallas_call(body, out_shape=outs, in_specs=[vmem] * len(args), out_spe...]
    ppermute x8 -> x11, waiting for transfers between devices: 27.2 us -> 17.5 us  [the longest x7 9.33 us: turn(): return lax.ppermute(value, 'col', [(i, i ^ bit) for i in range(z.col)])]
    all_to_all x1 -> x0, waiting for transfers between devices: 6.74 us -> none  [on_device(): lax.all_to_all(m, ALL, split_axis=0, concat_axis=0, tiled=True)]
    all_to_all x4 -> x5, blocking collectives: 45.2 us -> 51.5 us  [on_device(): lax.all_to_all(m, ALL, split_axis=0, concat_axis=0, tiled=True)]
    all_to_all x1 -> x0, starting transfers between devices: 3.41 us -> none  [on_device(): lax.all_to_all(m, ALL, split_axis=0, concat_axis=0, tiled=True)]
    ppermute x8 -> x11, starting transfers between devices: 15.1 us -> 12.2 us  [the longest x1 4.92 us: gather_fields(): above = lax.ppermute(tail, 'gy', [(i, i + 1) for i in range(z.gy - 1)])]
    concatenate x3 -> x0, local copies, waits for them, and re-layouts: 2.67 us -> none  [the longest x1 2.56 us: gather_fields(): jnp.concatenate([right_side, diag_shift, stiffness, grid_names, flat_name...]
    slice x18 -> x2, local copies, waits for them, and re-layouts: 1.87 us -> 0.03 us  [gather_fields(): corner_low, corner_high = (turn(across[:cut], 2), swap(beside[cut:]))]
  transfers between devices with their start and end apart: 9 -> 11, of which waited for: 4 -> 7; matrix products, arithmetic and copies ran while one was open for 4% -> 1% of each run, Pallas kernels for 0% -> 0%
where the time goes in v2:
time: 124 us; the launch traced here: 123 us
  blocking collectives  51.5 us (42%)
  Pallas kernels  36 us (29%)
  waiting for transfers between devices  17.5 us (14%)
  starting transfers between devices  12.2 us (10%)
  local copies, waits for them, and re-layouts  5.09 us (4%)
    all_to_all x5, blocking collectives, on_device(): lax.all_to_all(m, ALL, split_axis=0, concat_axis=0, tiled=True)  51.5 us
    pallas_call x8, Pallas kernels, call(): pl.pallas_call(body, out_shape=outs, in_specs=[vmem] * len(args), out_spe...  36 us
    ppermute x7, waiting for transfers between devices, turn(): return lax.ppermute(value, 'col', [(i, i ^ bit) for i in range(z.col)])  9.33 us
    unnamed x11, local copies, waits for them, and re-layouts  5.06 us
    ppermute x1, starting transfers between devices, gather_fields(): above = lax.ppermute(tail, 'gy', [(i, i + 1) for i in range(z.gy - 1)])  4.92 us
    ppermute x1, waiting for transfers between devices, gather_fields(): below = lax.ppermute(head, 'gy', [(i + 1, i) for i in range(z.gy - 1)])  4.31 us
    ppermute x2, starting transfers between devices, gather_fields(): swap = lambda value: lax.ppermute(value, 'gx', [(0, 1), (1, 0)])  3.05 us
    ppermute x7, starting transfers between devices, turn(): return lax.ppermute(value, 'col', [(i, i ^ bit) for i in range(z.col)])  2.99 us
  transfers between devices with their start and end apart: 11, of which 7 were waited for; matrix products, arithmetic and copies ran while one was open for 1% of the time, Pallas kernels for 0%

profile of v2, /device:TPU:0, one launch (start us, length us, event | category | flops | bytes accessed | tf_op | source)
XLA Modules:
  0.0 123.2 jit_solution(11162688279957605139)
XLA Ops:
  0.6 0.0 copy-start
  0.6 0.8 copy-done
  1.5 0.0 copy-start.1
  1.5 0.8 copy-done.1
  2.3 0.0 copy-start.2
  2.3 0.8 copy-done.2
  3.2 0.0 copy-start.3
  3.2 0.7 copy-done.3
  3.8 0.0 copy-start.4
  3.8 0.7 copy-done.4
  4.5 0.1 edges.1
  4.5 4.9 %collective-permute-start = (f32[4,56,128]{2,1,0:T(8,128)S(1)}, f32[4,56,128]{2,1,0:T(8,128)S(1)}, u32[]{:S(2)}, u32[]{:S(2)}) collective-permute-start(f32[4,56,128]{2,1,0:T(8,128)S(1)} %get-tuple-element.30), channel_id=1, source_target_pairs={{0,4},{4,8},{8,12},{1,5},{5,9},{9,13},{2,6},{6,10},{10,14},{3,7},{... | collective-permute-start | bytes 344072 | tf_op jit(solution)/shard_map/ppermute | solution.py:433
  9.5 1.3 %collective-permute-start.1 = (f32[4,56,128]{2,1,0:T(8,128)S(1)}, f32[4,56,128]{2,1,0:T(8,128)S(1)}, u32[]{:S(2)}, u32[]{:S(2)}) collective-permute-start(f32[4,56,128]{2,1,0:T(8,128)S(1)} %get-tuple-element.31), channel_id=1, source_target_pairs={{4,0},{8,4},{12,8},{5,1},{9,5},{13,9},{6,2},{10,6},{14,10},{7,3},{... | collective-permute-start | bytes 344072 | tf_op jit(solution)/shard_map/ppermute | solution.py:434
  10.8 1.1 collective-permute-done.above
  11.9 4.3 %collective-permute-done.1.below = f32[4,56,128]{2,1,0:T(8,128)S(1)} collective-permute-done((f32[4,56,128]{2,1,0:T(8,128)S(1)}, f32[4,56,128]{2,1,0:T(8,128)S(1)}, u32[]{:S(2)}, u32[]{:S(2)}) %collective-permute-start.1) | collective-permute-done | bytes 114720 | tf_op jit(solution)/shard_map/ppermute | solution.py:434
  16.2 0.1 pack.1.refs_0_
  16.2 1.6 %collective-permute-start.3 = (f32[4,200,128]{2,1,0:T(8,128)S(1)}, f32[4,200,128]{2,1,0:T(8,128)S(1)}, u32[]{:S(2)}, u32[]{:S(2)}) collective-permute-start(f32[4,200,128]{2,1,0:T(8,128)S(1)} %pack.1.refs_0_), channel_id=1, source_target_pairs={{0,2},{1,3},{2,0},{3,1},{4,6},{5,7},{6,4},{7,5},{8,10},{9,11},{10,... | collective-permute-start | bytes 1228808 | tf_op jit(solution)/shard_map/ppermute | solution.py:441
  17.8 1.5 %collective-permute-start.2 = (f32[4,200,128]{2,1,0:T(8,128)S(1)}, f32[4,200,128]{2,1,0:T(8,128)S(1)}, u32[]{:S(2)}, u32[]{:S(2)}) collective-permute-start(f32[4,200,128]{2,1,0:T(8,128)S(1)} %pack.1.refs_0_), channel_id=1, source_target_pairs={{0,16},{16,0},{1,17},{17,1},{2,18},{18,2},{3,19},{19,3},{4,20},{20... | collective-permute-start | bytes 1228808 | tf_op jit(solution)/shard_map/ppermute | solution.py:444
  19.3 0.0 collective-permute-start.6
  19.3 6.8 %collective-permute-done.3.refs_2_ = f32[4,200,128]{2,1,0:T(8,128)S(1)} collective-permute-done((f32[4,200,128]{2,1,0:T(8,128)S(1)}, f32[4,200,128]{2,1,0:T(8,128)S(1)}, u32[]{:S(2)}, u32[]{:S(2)}) %collective-permute-start.3) | collective-permute-done | bytes 409632 | tf_op jit(solution)/shard_map/ppermute | solution.py:441
  26.1 1.6 %collective-permute-start.5 = (f32[2,200,128]{2,1,0:T(8,128)S(1)}, f32[2,200,128]{2,1,0:T(8,128)S(1)}, u32[]{:S(2)}, u32[]{:S(2)}) collective-permute-start(f32[2,200,128]{2,1,0:T(8,128)S(1)} %slice.9), channel_id=1, source_target_pairs={{0,16},{16,0},{1,17},{17,1},{2,18},{18,2},{3,19},{19,3},{4,20},{20... | collective-permute-start | bytes 614408 | tf_op jit(solution)/shard_map/ppermute | solution.py:444
  27.6 0.7 collective-permute-done.2.refs_1_
  28.3 0.9 collective-permute-start.4
  29.2 0.0 collective-permute-start.8
  29.2 0.5 collective-permute-start.7
  29.7 2.1 %collective-permute-done.5.refs_4_ = f32[2,200,128]{2,1,0:T(8,128)S(1)} collective-permute-done((f32[2,200,128]{2,1,0:T(8,128)S(1)}, f32[2,200,128]{2,1,0:T(8,128)S(1)}, u32[]{:S(2)}, u32[]{:S(2)}) %collective-permute-start.5) | collective-permute-done | bytes 204832 | tf_op jit(solution)/shard_map/ppermute | solution.py:444
  31.9 0.0 collective-permute-start.10
  31.9 2.3 %collective-permute-done.4.refs_3_ = f32[2,200,128]{2,1,0:T(8,128)S(1)} collective-permute-done((f32[2,200,128]{2,1,0:T(8,128)S(1)}, f32[2,200,128]{2,1,0:T(8,128)S(1)}, u32[]{:S(2)}, u32[]{:S(2)}) %collective-permute-start.4) | collective-permute-done | bytes 204832 | tf_op jit(solution)/shard_map/ppermute | solution.py:441
  34.1 0.0 collective-permute-start.9
  34.2 1.2 %copy.8 = f32[1,8,128,128]{2,3,1,0:T(8,128)S(1)} copy(f32[1,8,128,128]{3,2,1,0:T(8,128)} %param.11) | data formatting | bytes 1048576 | tf_op args[5]
  35.4 0.0 collective-permute-done.6.refs_5_
  35.4 0.0 collective-permute-done.10.refs_9_
  35.4 0.0 collective-permute-done.8.refs_7_
  35.4 0.3 collective-permute-done.9.refs_8_
  35.7 0.0 collective-permute-done.7.refs_6_
  35.7 7.9 %begin.1 = (f32[8,4,64,128]{3,2,1,0:T(8,128)S(1)}, f32[8,4,64,128]{3,2,1,0:T(8,128)S(1)}, s32[8,4,64,128]{3,2,1,0:T(8,128)S(1)}, f32[10,4,80,128]{3,2,1,0:T(8,12...) custom-call(f32[4,200,128]{2,1,0:T(8,128)S(1)} %pack.1.refs_0_, ...), custom_call_target="tpu_custom_call" | custom-call | tf_op jit(solution)/shard_map/begin/pallas_call | solution.py:418
  43.6 11.9 %all_to_all.25.refs_0_ = f32[32,8,128]{2,1,0:T(8,128)S(1)} all-to-all(f32[32,8,128]{2,1,0:T(8,128)S(1)} %get-tuple-element.32), channel_id=1, replica_groups=mesh['gx'=2,'gy'=4,'col'=4] {'gx','gy','col'}, dimensions={0} | all-to-all | bytes 262144 | tf_op jit(solution)/shard_map/all_to_all | solution.py:483
  55.5 7.8 %step0.1 = (f32[6,4,32,128]{3,2,1,0:T(8,128)S(1)}, f32[32,1,1152]{2,1,0:T(1,128)S(1)}, f32[10,4,80,128]{3,2,1,0:T(8,128)S(1)}, f32[10,4,80,128]{3,2,1,0:T(8,128)S(1)}) custom-call(f32[32,8,128]{2,1,0:T(8,128)S(1)} %all_to_all.25.refs_0_, f32[8,4,64,128]{3,2,1,0:T(8,128)S(1)} %get-tuple-element.33.refs_1_.g, ...), custom_call_target="tpu_custom_call" | custom-call | tf_op jit(solution)/shard_map/step0/pallas_call | solution.py:418
  63.4 10.1 %all_to_all.26.refs_0_ = f32[32,1,1152]{2,1,0:T(1,128)S(1)} all-to-all(f32[32,1,1152]{2,1,0:T(1,128)S(1)} %get-tuple-element.39), channel_id=1, replica_groups=mesh['gx'=2,'gy'=4,'col'=4] {'gx','gy','col'}, dimensions={0} | all-to-all | bytes 294912 | tf_op jit(solution)/shard_map/all_to_all | solution.py:483
  73.5 7.8 %step1.1 = (f32[6,4,32,128]{3,2,1,0:T(8,128)S(1)}, f32[32,1,1152]{2,1,0:T(1,128)S(1)}, f32[10,4,80,128]{3,2,1,0:T(8,128)S(1)}, f32[10,4,80,128]{3,2,1,0:T(8,128)...) custom-call(f32[32,1,1152]{2,1,0:T(1,128)S(1)} %all_to_all.26.refs_0_, ...), custom_call_target="tpu_custom_call" | custom-call | tf_op jit(solution)/shard_map/step1/pallas_call | solution.py:418
  81.3 10.2 %all_to_all.27.refs_0_ = f32[32,1,1152]{2,1,0:T(1,128)S(1)} all-to-all(f32[32,1,1152]{2,1,0:T(1,128)S(1)} %get-tuple-element.43), channel_id=1, replica_groups=mesh['gx'=2,'gy'=4,'col'=4] {'gx','gy','col'}, dimensions={0} | all-to-all | bytes 294912 | tf_op jit(solution)/shard_map/all_to_all | solution.py:483
  91.5 7.0 %step2.1 = (f32[6,4,32,128]{3,2,1,0:T(8,128)S(1)}, f32[32,1,1152]{2,1,0:T(1,128)S(1)}, f32[10,4,80,128]{3,2,1,0:T(8,128)S(1)}, f32[10,4,80,128]{3,2,1,0:T(8,128)...) custom-call(f32[32,1,1152]{2,1,0:T(1,128)S(1)} %all_to_all.27.refs_0_, ...), custom_call_target="tpu_custom_call" | custom-call | tf_op jit(solution)/shard_map/step2/pallas_call | solution.py:418
  98.5 10.3 %all_to_all.28.refs_0_ = f32[32,1,1152]{2,1,0:T(1,128)S(1)} all-to-all(f32[32,1,1152]{2,1,0:T(1,128)S(1)} %get-tuple-element.49), channel_id=1, replica_groups=mesh['gx'=2,'gy'=4,'col'=4] {'gx','gy','col'}, dimensions={0} | all-to-all | bytes 294912 | tf_op jit(solution)/shard_map/all_to_all | solution.py:483
  108.8 4.5 %step3.1 = (f32[7,4,32,128]{3,2,1,0:T(8,128)S(1)}, f32[32,1,128]{2,1,0:T(1,128)S(1)}, f32[1,128]{1,0:T(1,128)S(1)}) custom-call(f32[32,1,1152]{2,1,0:T(1,128)S(1)} %all_to_all.28.refs_0_, f32[8,4,64,128]{3,2,1,0:T(8,128)S(1)} %get-tuple-element.33.refs_1_.g, f32[8,4,64,128]{3,2,1,0:T(8,128)S(1)} %get-tuple-element.34.refs_2_.s, ...), custom_call_target="tpu_custom_call" | custom-call | tf_op jit(solution)/shard_map/step3/pallas_call | solution.py:418
  113.3 9.0 %all_to_all.29.recv = f32[32,1,128]{2,1,0:T(1,128)S(1)} all-to-all(f32[32,1,128]{2,1,0:T(1,128)S(1)} %get-tuple-element.55), channel_id=1, replica_groups=mesh['gx'=2,'gy'=4,'col'=4] {'gx','gy','col'}, dimensions={0} | all-to-all | bytes 32768 | tf_op jit(solution)/shard_map/all_to_all | solution.py:483
  122.2 0.9 end.1
  (2 shorter events, 0.0 us)
Async XLA Ops:
  0.6 0.8 copy-start
  1.5 0.8 copy-start.1
  2.3 0.8 copy-start.2
  3.2 0.7 copy-start.3
  3.8 0.7 copy-start.4
  4.5 7.3 %collective-permute-start = (f32[4,56,128]{2,1,0:T(8,128)S(1)}, f32[4,56,128]{2,1,0:T(8,128)S(1)}, u32[]{:S(2)}, u32[]{:S(2)}) collective-permute-start(f32[4,56,128]{2,1,0:T(8,128)S(1)} %get-tuple-element.30), channel_id=1, source_target_pairs={{0,4},{4,8},{8,12},{1,5},{5,9},{9,13},{2,6},{6,10},{10,14},{3,7},{... | collective-permute-start | bytes 344072 | tf_op jit(solution)/shard_map/ppermute | solution.py:433
  9.5 6.7 %collective-permute-start.1 = (f32[4,56,128]{2,1,0:T(8,128)S(1)}, f32[4,56,128]{2,1,0:T(8,128)S(1)}, u32[]{:S(2)}, u32[]{:S(2)}) collective-permute-start(f32[4,56,128]{2,1,0:T(8,128)S(1)} %get-tuple-element.31), channel_id=1, source_target_pairs={{4,0},{8,4},{12,8},{5,1},{9,5},{13,9},{6,2},{10,6},{14,10},{7,3},{... | collective-permute-start | bytes 344072 | tf_op jit(solution)/shard_map/ppermute | solution.py:434
  16.2 9.8 %collective-permute-start.3 = (f32[4,200,128]{2,1,0:T(8,128)S(1)}, f32[4,200,128]{2,1,0:T(8,128)S(1)}, u32[]{:S(2)}, u32[]{:S(2)}) collective-permute-start(f32[4,200,128]{2,1,0:T(8,128)S(1)} %pack.1.refs_0_), channel_id=1, source_target_pairs={{0,2},{1,3},{2,0},{3,1},{4,6},{5,7},{6,4},{7,5},{8,10},{9,11},{10,... | collective-permute-start | bytes 1228808 | tf_op jit(solution)/shard_map/ppermute | solution.py:441
  17.8 10.5 %collective-permute-start.2 = (f32[4,200,128]{2,1,0:T(8,128)S(1)}, f32[4,200,128]{2,1,0:T(8,128)S(1)}, u32[]{:S(2)}, u32[]{:S(2)}) collective-permute-start(f32[4,200,128]{2,1,0:T(8,128)S(1)} %pack.1.refs_0_), channel_id=1, source_target_pairs={{0,16},{16,0},{1,17},{17,1},{2,18},{18,2},{3,19},{19,3},{4,20},{20... | collective-permute-start | bytes 1228808 | tf_op jit(solution)/shard_map/ppermute | solution.py:444
  19.3 16.1 %collective-permute-start.6 = (f32[4,200,128]{2,1,0:T(8,128)S(1)}, f32[4,200,128]{2,1,0:T(8,128)S(1)}, u32[]{:S(2)}, u32[]{:S(2)}) collective-permute-start(f32[4,200,128]{2,1,0:T(8,128)S(1)} %pack.1.refs_0_), channel_id=1, source_target_pairs={{0,1},{1,0},{2,3},{3,2},{4,5},{5,4},{6,7},{7,6},{8,9},{9,8},{10,11... | collective-permute-start | bytes 1228808 | tf_op jit(solution)/shard_map/ppermute | solution.py:441
  26.1 5.8 %collective-permute-start.5 = (f32[2,200,128]{2,1,0:T(8,128)S(1)}, f32[2,200,128]{2,1,0:T(8,128)S(1)}, u32[]{:S(2)}, u32[]{:S(2)}) collective-permute-start(f32[2,200,128]{2,1,0:T(8,128)S(1)} %slice.9), channel_id=1, source_target_pairs={{0,16},{16,0},{1,17},{17,1},{2,18},{18,2},{3,19},{19,3},{4,20},{20... | collective-permute-start | bytes 614408 | tf_op jit(solution)/shard_map/ppermute | solution.py:444
  28.3 5.8 %collective-permute-start.4 = (f32[2,200,128]{2,1,0:T(8,128)S(1)}, f32[2,200,128]{2,1,0:T(8,128)S(1)}, u32[]{:S(2)}, u32[]{:S(2)}) collective-permute-start(f32[2,200,128]{2,1,0:T(8,128)S(1)} %slice.8), channel_id=1, source_target_pairs={{0,2},{1,3},{2,0},{3,1},{4,6},{5,7},{6,4},{7,5},{8,10},{9,11},{10,... | collective-permute-start | bytes 614408 | tf_op jit(solution)/shard_map/ppermute | solution.py:441
  29.2 6.2 %collective-permute-start.8 = (f32[4,200,128]{2,1,0:T(8,128)S(1)}, f32[4,200,128]{2,1,0:T(8,128)S(1)}, u32[]{:S(2)}, u32[]{:S(2)}) collective-permute-start(f32[4,200,128]{2,1,0:T(8,128)S(1)} %collective-permute-done.3.refs_2_), channel_id=1, source_target_pairs={{0,1},{1,0},{2,3},{3,2},{4,5},{5,4},{6,7},{7,6},{8,9},{9,8},{10,11... | collective-permute-start | bytes 1228808 | tf_op jit(solution)/shard_map/ppermute | solution.py:441
  29.2 6.5 %collective-permute-start.7 = (f32[4,200,128]{2,1,0:T(8,128)S(1)}, f32[4,200,128]{2,1,0:T(8,128)S(1)}, u32[]{:S(2)}, u32[]{:S(2)}) collective-permute-start(f32[4,200,128]{2,1,0:T(8,128)S(1)} %collective-permute-done.2.refs_1_), channel_id=1, source_target_pairs={{0,1},{1,0},{2,3},{3,2},{4,5},{5,4},{6,7},{7,6},{8,9},{9,8},{10,11... | collective-permute-start | bytes 1228808 | tf_op jit(solution)/shard_map/ppermute | solution.py:441
  31.9 3.5 %collective-permute-start.10 = (f32[2,200,128]{2,1,0:T(8,128)S(1)}, f32[2,200,128]{2,1,0:T(8,128)}, u32[]{:S(2)}, u32[]{:S(2)}) collective-permute-start(f32[2,200,128]{2,1,0:T(8,128)S(1)} %collective-permute-done.5.refs_4_), channel_id=1, source_target_pairs={{0,1},{1,0},{2,3},{3,2},{4,5},{5,4},{6,7},{7,6},{8,9},{9,8},{10,11... | collective-permute-start | bytes 614408 | tf_op jit(solution)/shard_map/ppermute | solution.py:441
  34.1 1.6 %collective-permute-start.9 = (f32[2,200,128]{2,1,0:T(8,128)S(1)}, f32[2,200,128]{2,1,0:T(8,128)}, u32[]{:S(2)}, u32[]{:S(2)}) collective-permute-start(f32[2,200,128]{2,1,0:T(8,128)S(1)} %collective-permute-done.4.refs_3_), channel_id=1, source_target_pairs={{0,1},{1,0},{2,3},{3,2},{4,5},{5,4},{6,7},{7,6},{8,9},{9,8},{10,11... | collective-permute-start | bytes 614408 | tf_op jit(solution)/shard_map/ppermute | solution.py:441

commit v3 on v2

--- a/solution.py
+++ b/solution.py
@@ -28,6 +28,7 @@
         self.devices = self.gx * self.gy * self.col
         self.cx, self.cy = cx, cy
         self.planes = self.gx * cx
+        self.small = self.planes <= 8
         self.rows = cy + 2 * HALO
         self.nblock = cx * cy
         self.ngroup = self.nblock * (LANES // AGG) // LANES
@@ -59,19 +60,57 @@
     return out
 
 
+DELAY = 0
+
+
+def loop(count, body, unroll):
+    if unroll:
+        for i in range(count):
+            body(i, 0)
+    else:
+        lax.fori_loop(0, count, body, 0)
+
+
+class Stores:
+    def __init__(self):
+        self.waiting = []
+
+    def add(self, *stores):
+        self.waiting.append(stores)
+        if len(self.waiting) > DELAY:
+            self.release()
+
+    def release(self):
+        for ref, where, value in self.waiting.pop(0):
+            ref[where] = value
+
+    def close(self):
+        while self.waiting:
+            self.release()
+
+
 def sweep(src, tiles, z, visit):
-    def body(t, carry):
-        load = lambda i: [src[i, c, inner(t)] for c in range(z.col)]
-        below, mid = load(0), load(1)
-        for i in range(z.planes):
-            above = load(i + 2)
-            across = row_sums(src, i + 1, t, mid, z)
-            for c in range(z.col):
-                visit(i, t, c, mid[c], across[c] + (below[c] + above[c]))
-            below, mid = mid, above
+    lo, hi = tiles
+    each = hi - lo if z.small else 1
+
+    def body(turn, carry):
+        stores = Stores()
+        for part in range(each):
+            t = lo + turn * each + part
+            load = lambda i: [src[i, c, inner(t)] for c in range(z.col)]
+            below, mid = load(0), load(1)
+            for i in range(z.planes):
+                above = load(i + 2)
+                across = row_sums(src, i + 1, t, mid, z)
+                made = []
+                for c in range(z.col):
+                    made += visit(i, t, c, mid[c], across[c] + (below[c] + above[c]))
+                stores.add(*made)
+                below, mid = mid, above
+        stores.close()
         return carry
 
-    lax.fori_loop(tiles[0], tiles[1], body, 0)
+    lax.fori_loop(0, (hi - lo) // each, body, 0)
 
 
 def clear_ends(ref, z):
@@ -84,16 +123,15 @@
     c0, c1 = w1 * (1.0 - w2) + w2, w1 * w2
 
     def visit(i, t, c, value, total):
-        out[i + 1, c, inner(t)] = c0 * value + (c1 * g[i, c, plain(t)]) * total
+        return [(out, (i + 1, c, inner(t)), c0 * value + (c1 * g[i, c, plain(t)]) * total)]
 
     sweep(rho, tiles, z, visit)
 
 
 def smooth(src, rho, g, out, w, tiles, z):
     def visit(i, t, c, value, total):
-        out[i + 1, c, inner(t)] = (1.0 - w) * value + w * (
-            rho[i + 1, c, inner(t)] + g[i, c, plain(t)] * total
-        )
+        moved = rho[i + 1, c, inner(t)] + g[i, c, plain(t)] * total
+        return [(out, (i + 1, c, inner(t)), (1.0 - w) * value + w * moved)]
 
     sweep(src, tiles, z, visit)
 
@@ -104,10 +142,12 @@
 
     def body(k, carry):
         i = first + k
+        stores = Stores()
         for j in range(z.cy // 8):
             t = HALO // 8 + j
             mid = [y2[i + 1, c, inner(t)] for c in range(z.col)]
             across = row_sums(y2, i + 1, t + 0 * k, mid, z)
+            made = []
             for c in range(z.col):
                 total = across[c] + (y2[i, c, inner(t)] + y2[i + 2, c, inner(t)])
                 gg = g[i, c, plain(t)]
@@ -116,10 +156,12 @@
                 middle = (value - high).astype(jnp.bfloat16).astype(f32)
                 low = value - high - middle
                 for n, part in enumerate((high, middle, low)):
-                    parts[n, c ^ col, k, j * 8 : j * 8 + 8] = part
+                    made += [(parts, (n, c ^ col, k, slice(j * 8, j * 8 + 8)), part)]
+            stores.add(*made)
+        stores.close()
         return carry
 
-    lax.fori_loop(0, z.cx, body, 0)
+    loop(z.cx, body, z.small)
     total = jnp.zeros((z.nblock, LANES), f32)
     for n in range(3):
         flat = parts[n].reshape(z.col * z.nblock, LANES).astype(jnp.bfloat16)
@@ -131,7 +173,7 @@
     def solve(c, carry):
         acc = jnp.zeros((per, LANES), f32)
         for half in range(2):
-            tile = grouped[pl.ds(pl.multiple_of(c * 16 + half * 8, 8), 8), :]
+            tile = grouped[pl.ds(c * 16 + half * 8, 8), :]
             for k in range(8):
                 value = jnp.broadcast_to(tile[k : k + 1, :], (per, LANES)) * mask
                 value = jnp.sum(value, axis=1, keepdims=True)
@@ -139,7 +181,7 @@
         msg[c] = jnp.sum(acc, axis=0, keepdims=True)
         return carry
 
-    lax.fori_loop(0, z.ngroup, solve, 0)
+    loop(z.ngroup, solve, z.small)
 
 
 def list_row(owner, group, z):
@@ -214,15 +256,17 @@
             unpack(piece, col ^ m, i, p)
             return carry
 
-        lax.fori_loop(0, piece.shape[0], each, 0)
+        loop(piece.shape[0], each, z.small)
 
     def coefficients(i, t, c, x, total):
         diagonal = g[i, c, plain(t)] + x * total
         inside = diagonal > 0.0
         scale = jnp.where(inside, x / jnp.where(inside, diagonal, 1.0), 0.0)
-        s[i, c, plain(t)] = x
-        g[i, c, plain(t)] = x * scale
-        rho[i + 1, c, inner(t)] = rho[i + 1, c, inner(t)] * scale
+        return [
+            (s, (i, c, plain(t)), x),
+            (g, (i, c, plain(t)), x * scale),
+            (rho, (i + 1, c, inner(t)), rho[i + 1, c, inner(t)] * scale),
+        ]
 
     sweep(wide, tiles, z, coefficients)
     group = iota((z.nblock, LANES), 0).astype(f32) + (col * z.nblock).astype(f32)
@@ -247,7 +291,7 @@
                 table[d, c : c + 1, :] = recv[d, :, c * LANES : (c + 1) * LANES]
             return carry
 
-        lax.fori_loop(0, z.devices, unpack, 0)
+        loop(z.devices, unpack, z.small)
     else:
         table = recv
     gy = lax.axis_index("gy")
@@ -257,11 +301,13 @@
 
     def body(i, carry):
         gx = i // z.cx
+        stores = Stores()
         for tile in tiles:
             side = -1 if tile * 8 < HALO else (1 if tile * 8 >= HALO + z.cy else 0)
             layer = jnp.clip(gy + side, 0, z.gy - 1)
             base = (gx * z.gy + layer) * z.col
             tables = [table[base + o] for o in range(z.col)]
+            made = []
             for c in range(z.col):
                 t = targets[i, c, plain(tile)]
                 line = t >> 4
@@ -272,10 +318,13 @@
                     picked = jnp.where(owner == o, other, picked)
                 lane = (t & 15) * 8 + aggregate
                 picked = jnp.take_along_axis(picked, lane, axis=1, mode="promise_in_bounds")
-                out[i + 1, c, inner(tile)] = y2[i + 1, c, inner(tile)] + s[i, c, plain(tile)] * picked
+                value = y2[i + 1, c, inner(tile)] + s[i, c, plain(tile)] * picked
+                made += [(out, (i + 1, c, inner(tile)), value)]
+            stores.add(*made)
+        stores.close()
         return carry
 
-    lax.fori_loop(0, z.planes, body, 0)
+    loop(z.planes, body, z.small)
 
 
 def weighted(a, b, h):
@@ -319,7 +368,7 @@
     if first:
 
         def image(i, t, c, value, total):
-            w_new[i + 1, c, inner(t)] = value - g[i, c, plain(t)] * total
+            return [(w_new, (i + 1, c, inner(t)), value - g[i, c, plain(t)] * total)]
 
         sweep(ya, rows, z, image)
         r, u, w = (ref[planes1, col, own_inner] for ref in (rho, ya, w_new))
@@ -349,9 +398,10 @@
             n_vec = value - g[i, c, plain(t)] * total
             if beta is not None:
                 n_vec = n_vec + beta * k["z_old"][i, c, plain(t)]
+            made = [(w_new, (i + 1, c, inner(t)), rho[i + 1, c, inner(t)] - alpha * n_vec)]
             if not last:
-                k["z_out"][i, c, plain(t)] = n_vec
-            w_new[i + 1, c, inner(t)] = rho[i + 1, c, inner(t)] - alpha * n_vec
+                made += [(k["z_out"], (i, c, plain(t)), n_vec)]
+            return made
 
         w_now = rho[planes1, col, own_inner]
         m_now = ya[planes1, col, own_inner]

time: 124 us -> 106 us (0.85)
  Pallas kernels: 36 us -> 18.8 us
    pallas_call x8, Pallas kernels: 36 us -> 18.8 us  [call(): pl.pallas_call(body, out_shape=outs, in_specs=[vmem] * len(args), out_spe...]
where the time goes in v3:
time: 106 us
  blocking collectives  51.5 us (49%)
  Pallas kernels  18.8 us (18%)
  waiting for transfers between devices  17.5 us (17%)
  starting transfers between devices  12.2 us (12%)
  local copies, waits for them, and re-layouts  5.09 us (5%)
    all_to_all x5, blocking collectives, on_device(): lax.all_to_all(m, ALL, split_axis=0, concat_axis=0, tiled=True)  51.5 us
    pallas_call x8, Pallas kernels, call(): pl.pallas_call(body, out_shape=outs, in_specs=[vmem] * len(args), out_spe...  18.8 us
    ppermute x7, waiting for transfers between devices, turn(): return lax.ppermute(value, 'col', [(i, i ^ bit) for i in range(z.col)])  9.33 us
    unnamed x11, local copies, waits for them, and re-layouts  5.06 us
    ppermute x1, starting transfers between devices, gather_fields(): above = lax.ppermute(tail, 'gy', [(i, i + 1) for i in range(z.gy - 1)])  4.92 us
    ppermute x1, waiting for transfers between devices, gather_fields(): below = lax.ppermute(head, 'gy', [(i + 1, i) for i in range(z.gy - 1)])  4.31 us
    ppermute x2, starting transfers between devices, gather_fields(): swap = lambda value: lax.ppermute(value, 'gx', [(0, 1), (1, 0)])  3.05 us
    ppermute x7, starting transfers between devices, turn(): return lax.ppermute(value, 'col', [(i, i ^ bit) for i in range(z.col)])  2.99 us
  transfers between devices with their start and end apart: 11, of which 7 were waited for; matrix products, arithmetic and copies ran while one was open for 1% of the time, Pallas kernels for 0%

profile of v3, /device:TPU:0, one launch (start us, length us, event | category | flops | bytes accessed | tf_op | source)
XLA Modules:
  0.0 106.0 jit_solution(16954386025667752681)
XLA Ops:
  0.6 0.0 copy-start
  0.6 0.8 copy-done
  1.5 0.0 copy-start.1
  1.5 0.8 copy-done.1
  2.3 0.0 copy-start.2
  2.3 0.8 copy-done.2
  3.2 0.0 copy-start.3
  3.2 0.7 copy-done.3
  3.8 0.0 copy-start.4
  3.8 0.7 copy-done.4
  4.5 0.1 edges.1
  4.5 4.9 %collective-permute-start = (f32[4,56,128]{2,1,0:T(8,128)S(1)}, f32[4,56,128]{2,1,0:T(8,128)S(1)}, u32[]{:S(2)}, u32[]{:S(2)}) collective-permute-start(f32[4,56,128]{2,1,0:T(8,128)S(1)} %get-tuple-element.30), channel_id=1, source_target_pairs={{0,4},{4,8},{8,12},{1,5},{5,9},{9,13},{2,6},{6,10},{10,14},{3,7},{... | collective-permute-start | bytes 344072 | tf_op jit(solution)/shard_map/ppermute | solution.py:483
  9.5 1.3 %collective-permute-start.1 = (f32[4,56,128]{2,1,0:T(8,128)S(1)}, f32[4,56,128]{2,1,0:T(8,128)S(1)}, u32[]{:S(2)}, u32[]{:S(2)}) collective-permute-start(f32[4,56,128]{2,1,0:T(8,128)S(1)} %get-tuple-element.31), channel_id=1, source_target_pairs={{4,0},{8,4},{12,8},{5,1},{9,5},{13,9},{6,2},{10,6},{14,10},{7,3},{... | collective-permute-start | bytes 344072 | tf_op jit(solution)/shard_map/ppermute | solution.py:484
  10.8 1.1 %collective-permute-done.above = f32[4,56,128]{2,1,0:T(8,128)S(1)} collective-permute-done((f32[4,56,128]{2,1,0:T(8,128)S(1)}, f32[4,56,128]{2,1,0:T(8,128)S(1)}, u32[]{:S(2)}, u32[]{:S(2)}) %collective-permute-start) | collective-permute-done | bytes 114720 | tf_op jit(solution)/shard_map/ppermute | solution.py:483
  11.9 4.3 %collective-permute-done.1.below = f32[4,56,128]{2,1,0:T(8,128)S(1)} collective-permute-done((f32[4,56,128]{2,1,0:T(8,128)S(1)}, f32[4,56,128]{2,1,0:T(8,128)S(1)}, u32[]{:S(2)}, u32[]{:S(2)}) %collective-permute-start.1) | collective-permute-done | bytes 114720 | tf_op jit(solution)/shard_map/ppermute | solution.py:484
  16.2 0.1 pack.1.refs_0_
  16.2 1.6 %collective-permute-start.3 = (f32[4,200,128]{2,1,0:T(8,128)S(1)}, f32[4,200,128]{2,1,0:T(8,128)S(1)}, u32[]{:S(2)}, u32[]{:S(2)}) collective-permute-start(f32[4,200,128]{2,1,0:T(8,128)S(1)} %pack.1.refs_0_), channel_id=1, source_target_pairs={{0,2},{1,3},{2,0},{3,1},{4,6},{5,7},{6,4},{7,5},{8,10},{9,11},{10,... | collective-permute-start | bytes 1228808 | tf_op jit(solution)/shard_map/ppermute | solution.py:491
  17.8 1.5 %collective-permute-start.2 = (f32[4,200,128]{2,1,0:T(8,128)S(1)}, f32[4,200,128]{2,1,0:T(8,128)S(1)}, u32[]{:S(2)}, u32[]{:S(2)}) collective-permute-start(f32[4,200,128]{2,1,0:T(8,128)S(1)} %pack.1.refs_0_), channel_id=1, source_target_pairs={{0,16},{16,0},{1,17},{17,1},{2,18},{18,2},{3,19},{19,3},{4,20},{20... | collective-permute-start | bytes 1228808 | tf_op jit(solution)/shard_map/ppermute | solution.py:494
  19.3 0.0 collective-permute-start.6
  19.3 6.8 %collective-permute-done.3.refs_2_ = f32[4,200,128]{2,1,0:T(8,128)S(1)} collective-permute-done((f32[4,200,128]{2,1,0:T(8,128)S(1)}, f32[4,200,128]{2,1,0:T(8,128)S(1)}, u32[]{:S(2)}, u32[]{:S(2)}) %collective-permute-start.3) | collective-permute-done | bytes 409632 | tf_op jit(solution)/shard_map/ppermute | solution.py:491
  26.1 1.6 %collective-permute-start.5 = (f32[2,200,128]{2,1,0:T(8,128)S(1)}, f32[2,200,128]{2,1,0:T(8,128)S(1)}, u32[]{:S(2)}, u32[]{:S(2)}) collective-permute-start(f32[2,200,128]{2,1,0:T(8,128)S(1)} %slice.9), channel_id=1, source_target_pairs={{0,16},{16,0},{1,17},{17,1},{2,18},{18,2},{3,19},{19,3},{4,20},{20... | collective-permute-start | bytes 614408 | tf_op jit(solution)/shard_map/ppermute | solution.py:494
  27.6 0.7 collective-permute-done.2.refs_1_
  28.3 0.9 collective-permute-start.4
  29.2 0.0 collective-permute-start.8
  29.2 0.5 collective-permute-start.7
  29.7 2.1 %collective-permute-done.5.refs_4_ = f32[2,200,128]{2,1,0:T(8,128)S(1)} collective-permute-done((f32[2,200,128]{2,1,0:T(8,128)S(1)}, f32[2,200,128]{2,1,0:T(8,128)S(1)}, u32[]{:S(2)}, u32[]{:S(2)}) %collective-permute-start.5) | collective-permute-done | bytes 204832 | tf_op jit(solution)/shard_map/ppermute | solution.py:494
  31.9 0.0 collective-permute-start.10
  31.9 2.3 %collective-permute-done.4.refs_3_ = f32[2,200,128]{2,1,0:T(8,128)S(1)} collective-permute-done((f32[2,200,128]{2,1,0:T(8,128)S(1)}, f32[2,200,128]{2,1,0:T(8,128)S(1)}, u32[]{:S(2)}, u32[]{:S(2)}) %collective-permute-start.4) | collective-permute-done | bytes 204832 | tf_op jit(solution)/shard_map/ppermute | solution.py:491
  34.1 0.0 collective-permute-start.9
  34.2 1.2 %copy.8 = f32[1,8,128,128]{2,3,1,0:T(8,128)S(1)} copy(f32[1,8,128,128]{3,2,1,0:T(8,128)} %param.11) | data formatting | bytes 1048576 | tf_op args[5]
  35.4 0.0 collective-permute-done.6.refs_5_
  35.4 0.0 collective-permute-done.10.refs_9_
  35.4 0.0 collective-permute-done.8.refs_7_
  35.4 0.3 collective-permute-done.9.refs_8_
  35.7 0.0 collective-permute-done.7.refs_6_
  35.7 3.3 %begin.1 = (f32[8,4,64,128]{3,2,1,0:T(8,128)S(1)}, f32[8,4,64,128]{3,2,1,0:T(8,128)S(1)}, s32[8,4,64,128]{3,2,1,0:T(8,128)S(1)}, f32[10,4,80,128]{3,2,1,0:T(8,12...) custom-call(f32[4,200,128]{2,1,0:T(8,128)S(1)} %pack.1.refs_0_, ...), custom_call_target="tpu_custom_call" | custom-call | tf_op jit(solution)/shard_map/begin/pallas_call | solution.py:468
  39.0 11.9 %all_to_all.25.refs_0_ = f32[32,8,128]{2,1,0:T(8,128)S(1)} all-to-all(f32[32,8,128]{2,1,0:T(8,128)S(1)} %get-tuple-element.32), channel_id=1, replica_groups=mesh['gx'=2,'gy'=4,'col'=4] {'gx','gy','col'}, dimensions={0} | all-to-all | bytes 262144 | tf_op jit(solution)/shard_map/all_to_all | solution.py:533
  51.0 4.2 %step0.1 = (f32[6,4,32,128]{3,2,1,0:T(8,128)S(1)}, f32[32,1,1152]{2,1,0:T(1,128)S(1)}, f32[10,4,80,128]{3,2,1,0:T(8,128)S(1)}, f32[10,4,80,128]{3,2,1,0:T(8,128)S(1)}) custom-call(f32[32,8,128]{2,1,0:T(8,128)S(1)} %all_to_all.25.refs_0_, f32[8,4,64,128]{3,2,1,0:T(8,128)S(1)} %get-tuple-element.33.refs_1_.g, ...), custom_call_target="tpu_custom_call" | custom-call | tf_op jit(solution)/shard_map/step0/pallas_call | solution.py:468
  55.2 10.1 %all_to_all.26.refs_0_ = f32[32,1,1152]{2,1,0:T(1,128)S(1)} all-to-all(f32[32,1,1152]{2,1,0:T(1,128)S(1)} %get-tuple-element.39), channel_id=1, replica_groups=mesh['gx'=2,'gy'=4,'col'=4] {'gx','gy','col'}, dimensions={0} | all-to-all | bytes 294912 | tf_op jit(solution)/shard_map/all_to_all | solution.py:533
  65.3 4.2 %step1.1 = (f32[6,4,32,128]{3,2,1,0:T(8,128)S(1)}, f32[32,1,1152]{2,1,0:T(1,128)S(1)}, f32[10,4,80,128]{3,2,1,0:T(8,128)S(1)}, f32[10,4,80,128]{3,2,1,0:T(8,128)...) custom-call(f32[32,1,1152]{2,1,0:T(1,128)S(1)} %all_to_all.26.refs_0_, ...), custom_call_target="tpu_custom_call" | custom-call | tf_op jit(solution)/shard_map/step1/pallas_call | solution.py:468
  69.5 10.2 %all_to_all.27.refs_0_ = f32[32,1,1152]{2,1,0:T(1,128)S(1)} all-to-all(f32[32,1,1152]{2,1,0:T(1,128)S(1)} %get-tuple-element.43), channel_id=1, replica_groups=mesh['gx'=2,'gy'=4,'col'=4] {'gx','gy','col'}, dimensions={0} | all-to-all | bytes 294912 | tf_op jit(solution)/shard_map/all_to_all | solution.py:533
  79.8 3.6 %step2.1 = (f32[6,4,32,128]{3,2,1,0:T(8,128)S(1)}, f32[32,1,1152]{2,1,0:T(1,128)S(1)}, f32[10,4,80,128]{3,2,1,0:T(8,128)S(1)}, f32[10,4,80,128]{3,2,1,0:T(8,128)...) custom-call(f32[32,1,1152]{2,1,0:T(1,128)S(1)} %all_to_all.27.refs_0_, ...), custom_call_target="tpu_custom_call" | custom-call | tf_op jit(solution)/shard_map/step2/pallas_call | solution.py:468
  83.4 10.3 %all_to_all.28.refs_0_ = f32[32,1,1152]{2,1,0:T(1,128)S(1)} all-to-all(f32[32,1,1152]{2,1,0:T(1,128)S(1)} %get-tuple-element.49), channel_id=1, replica_groups=mesh['gx'=2,'gy'=4,'col'=4] {'gx','gy','col'}, dimensions={0} | all-to-all | bytes 294912 | tf_op jit(solution)/shard_map/all_to_all | solution.py:533
  93.6 2.4 %step3.1 = (f32[7,4,32,128]{3,2,1,0:T(8,128)S(1)}, f32[32,1,128]{2,1,0:T(1,128)S(1)}, f32[1,128]{1,0:T(1,128)S(1)}) custom-call(f32[32,1,1152]{2,1,0:T(1,128)S(1)} %all_to_all.28.refs_0_, f32[8,4,64,128]{3,2,1,0:T(8,128)S(1)} %get-tuple-element.33.refs_1_.g, f32[8,4,64,128]{3,2,1,0:T(8,128)S(1)} %get-tuple-element.34.refs_2_.s, ...), custom_call_target="tpu_custom_call" | custom-call | tf_op jit(solution)/shard_map/step3/pallas_call | solution.py:468
  96.0 9.0 %all_to_all.29.recv = f32[32,1,128]{2,1,0:T(1,128)S(1)} all-to-all(f32[32,1,128]{2,1,0:T(1,128)S(1)} %get-tuple-element.55), channel_id=1, replica_groups=mesh['gx'=2,'gy'=4,'col'=4] {'gx','gy','col'}, dimensions={0} | all-to-all | bytes 32768 | tf_op jit(solution)/shard_map/all_to_all | solution.py:533
  105.0 0.9 end.1
  (2 shorter events, 0.0 us)
Async XLA Ops:
  0.6 0.8 copy-start
  1.5 0.8 copy-start.1
  2.3 0.8 copy-start.2
  3.2 0.7 copy-start.3
  3.8 0.7 copy-start.4
  4.5 7.3 %collective-permute-start = (f32[4,56,128]{2,1,0:T(8,128)S(1)}, f32[4,56,128]{2,1,0:T(8,128)S(1)}, u32[]{:S(2)}, u32[]{:S(2)}) collective-permute-start(f32[4,56,128]{2,1,0:T(8,128)S(1)} %get-tuple-element.30), channel_id=1, source_target_pairs={{0,4},{4,8},{8,12},{1,5},{5,9},{9,13},{2,6},{6,10},{10,14},{3,7},{... | collective-permute-start | bytes 344072 | tf_op jit(solution)/shard_map/ppermute | solution.py:483
  9.5 6.7 %collective-permute-start.1 = (f32[4,56,128]{2,1,0:T(8,128)S(1)}, f32[4,56,128]{2,1,0:T(8,128)S(1)}, u32[]{:S(2)}, u32[]{:S(2)}) collective-permute-start(f32[4,56,128]{2,1,0:T(8,128)S(1)} %get-tuple-element.31), channel_id=1, source_target_pairs={{4,0},{8,4},{12,8},{5,1},{9,5},{13,9},{6,2},{10,6},{14,10},{7,3},{... | collective-permute-start | bytes 344072 | tf_op jit(solution)/shard_map/ppermute | solution.py:484
  16.2 9.8 %collective-permute-start.3 = (f32[4,200,128]{2,1,0:T(8,128)S(1)}, f32[4,200,128]{2,1,0:T(8,128)S(1)}, u32[]{:S(2)}, u32[]{:S(2)}) collective-permute-start(f32[4,200,128]{2,1,0:T(8,128)S(1)} %pack.1.refs_0_), channel_id=1, source_target_pairs={{0,2},{1,3},{2,0},{3,1},{4,6},{5,7},{6,4},{7,5},{8,10},{9,11},{10,... | collective-permute-start | bytes 1228808 | tf_op jit(solution)/shard_map/ppermute | solution.py:491
  17.8 10.5 %collective-permute-start.2 = (f32[4,200,128]{2,1,0:T(8,128)S(1)}, f32[4,200,128]{2,1,0:T(8,128)S(1)}, u32[]{:S(2)}, u32[]{:S(2)}) collective-permute-start(f32[4,200,128]{2,1,0:T(8,128)S(1)} %pack.1.refs_0_), channel_id=1, source_target_pairs={{0,16},{16,0},{1,17},{17,1},{2,18},{18,2},{3,19},{19,3},{4,20},{20... | collective-permute-start | bytes 1228808 | tf_op jit(solution)/shard_map/ppermute | solution.py:494
  19.3 16.1 %collective-permute-start.6 = (f32[4,200,128]{2,1,0:T(8,128)S(1)}, f32[4,200,128]{2,1,0:T(8,128)S(1)}, u32[]{:S(2)}, u32[]{:S(2)}) collective-permute-start(f32[4,200,128]{2,1,0:T(8,128)S(1)} %pack.1.refs_0_), channel_id=1, source_target_pairs={{0,1},{1,0},{2,3},{3,2},{4,5},{5,4},{6,7},{7,6},{8,9},{9,8},{10,11... | collective-permute-start | bytes 1228808 | tf_op jit(solution)/shard_map/ppermute | solution.py:491
  26.1 5.8 %collective-permute-start.5 = (f32[2,200,128]{2,1,0:T(8,128)S(1)}, f32[2,200,128]{2,1,0:T(8,128)S(1)}, u32[]{:S(2)}, u32[]{:S(2)}) collective-permute-start(f32[2,200,128]{2,1,0:T(8,128)S(1)} %slice.9), channel_id=1, source_target_pairs={{0,16},{16,0},{1,17},{17,1},{2,18},{18,2},{3,19},{19,3},{4,20},{20... | collective-permute-start | bytes 614408 | tf_op jit(solution)/shard_map/ppermute | solution.py:494
  28.3 5.8 %collective-permute-start.4 = (f32[2,200,128]{2,1,0:T(8,128)S(1)}, f32[2,200,128]{2,1,0:T(8,128)S(1)}, u32[]{:S(2)}, u32[]{:S(2)}) collective-permute-start(f32[2,200,128]{2,1,0:T(8,128)S(1)} %slice.8), channel_id=1, source_target_pairs={{0,2},{1,3},{2,0},{3,1},{4,6},{5,7},{6,4},{7,5},{8,10},{9,11},{10,... | collective-permute-start | bytes 614408 | tf_op jit(solution)/shard_map/ppermute | solution.py:491
  29.2 6.2 %collective-permute-start.8 = (f32[4,200,128]{2,1,0:T(8,128)S(1)}, f32[4,200,128]{2,1,0:T(8,128)S(1)}, u32[]{:S(2)}, u32[]{:S(2)}) collective-permute-start(f32[4,200,128]{2,1,0:T(8,128)S(1)} %collective-permute-done.3.refs_2_), channel_id=1, source_target_pairs={{0,1},{1,0},{2,3},{3,2},{4,5},{5,4},{6,7},{7,6},{8,9},{9,8},{10,11... | collective-permute-start | bytes 1228808 | tf_op jit(solution)/shard_map/ppermute | solution.py:491
  29.2 6.5 %collective-permute-start.7 = (f32[4,200,128]{2,1,0:T(8,128)S(1)}, f32[4,200,128]{2,1,0:T(8,128)S(1)}, u32[]{:S(2)}, u32[]{:S(2)}) collective-permute-start(f32[4,200,128]{2,1,0:T(8,128)S(1)} %collective-permute-done.2.refs_1_), channel_id=1, source_target_pairs={{0,1},{1,0},{2,3},{3,2},{4,5},{5,4},{6,7},{7,6},{8,9},{9,8},{10,11... | collective-permute-start | bytes 1228808 | tf_op jit(solution)/shard_map/ppermute | solution.py:491
  31.9 3.5 %collective-permute-start.10 = (f32[2,200,128]{2,1,0:T(8,128)S(1)}, f32[2,200,128]{2,1,0:T(8,128)}, u32[]{:S(2)}, u32[]{:S(2)}) collective-permute-start(f32[2,200,128]{2,1,0:T(8,128)S(1)} %collective-permute-done.5.refs_4_), channel_id=1, source_target_pairs={{0,1},{1,0},{2,3},{3,2},{4,5},{5,4},{6,7},{7,6},{8,9},{9,8},{10,11... | collective-permute-start | bytes 614408 | tf_op jit(solution)/shard_map/ppermute | solution.py:491
  34.1 1.6 %collective-permute-start.9 = (f32[2,200,128]{2,1,0:T(8,128)S(1)}, f32[2,200,128]{2,1,0:T(8,128)}, u32[]{:S(2)}, u32[]{:S(2)}) collective-permute-start(f32[2,200,128]{2,1,0:T(8,128)S(1)} %collective-permute-done.4.refs_3_), channel_id=1, source_target_pairs={{0,1},{1,0},{2,3},{3,2},{4,5},{5,4},{6,7},{7,6},{8,9},{9,8},{10,11... | collective-permute-start | bytes 614408 | tf_op jit(solution)/shard_map/ppermute | solution.py:491

commit v4 on v3

--- a/solution.py
+++ b/solution.py
@@ -184,46 +184,33 @@
     loop(z.ngroup, solve, z.small)
 
 
-def list_row(owner, group, z):
-    return (owner[...] * z.nblock + group[...]).astype(f32)
-
-
-def kernel_edges(z, r, d, s, owner, group, head, tail):
+def kernel_edges(z, block, head, tail, same):
     h, n = HALO, z.cy
-    names = list_row(owner, group, z)
-    for out, rows, extra, first in ((head, slice(0, h), h, 0), (tail, slice(n - h, n), n - h - 1, n - h)):
-        for k, field in enumerate((r, d, s)):
-            out[:, k * h : (k + 1) * h] = field[:, rows]
-        out[:, 3 * h : 3 * h + 8] = jnp.zeros((z.cx, 8, LANES), f32)
-        out[:, 3 * h : 3 * h + 1] = s[:, extra : extra + 1]
+    same[...] = block[...]
+    for out, first, extra in ((head, 0, h), (tail, n - h, n - h - 1)):
+        for k in range(3):
+            out[:, k * h : (k + 1) * h] = block[:, k * n + first : k * n + first + h]
+        out[:, 3 * h : 3 * h + 8] = block[:, 3 * n : 3 * n + 8]
+        out[:, 3 * h : 3 * h + 1] = block[:, 2 * n + extra : 2 * n + extra + 1]
+
+
+def kernel_halo(z, above, below, *refs):
+    m = above.shape[1]
+    outs = refs[len(refs) // 2 :] if len(refs) > 1 else refs
+    blocks = refs[: len(refs) // 2] if len(refs) > 1 else ()
+    for out in outs:
         for i in range(z.cx):
-            turn = (i * n + first) % LANES
-            out[i, 3 * h + 1 : 3 * h + 2] = pltpu.roll(names, (LANES - turn) % LANES, 1) if turn else names
-
-
-def kernel_pack(z, r, d, s, owner, group, above, below, out):
-    h, n, m = HALO, z.cy, z.rows
-    names = list_row(owner, group, z)
-    lane = iota((1, LANES), 1)
-    for k, field in enumerate((r, d, s)):
-        out[:, k * m : k * m + h] = above[:, k * h : (k + 1) * h]
-        out[:, k * m + h : k * m + h + n] = field[...]
-        out[:, k * m + h + n : (k + 1) * m] = below[:, k * h : (k + 1) * h]
-    out[:, 3 * m : 3 * m + 8] = jnp.zeros((z.cx, 8, LANES), f32)
-    out[:, 3 * m : 3 * m + 1] = above[:, 3 * h : 3 * h + 1]
-    out[:, 3 * m + 1 : 3 * m + 2] = below[:, 3 * h : 3 * h + 1]
-    for i in range(z.cx):
-        turn = (LANES + h - i * n) % LANES
-        mine = pltpu.roll(names, turn, 1) if turn else names
-        left = above[i, 3 * h + 1 : 3 * h + 2]
-        right = pltpu.roll(below[i, 3 * h + 1 : 3 * h + 2], h + n, 1)
-        out[i, 3 * m + 2 : 3 * m + 3] = jnp.where(lane < h, left, jnp.where(lane < h + n, mine, right))
-        out[i, 3 * m + 3 : 3 * m + 4] = names
-
-
-def kernel_first(z, layout, *refs):
-    pieces = refs[: len(layout)]
-    refs = refs[len(layout) :]
+            out[2 * m * i : 2 * m * i + m] = above[i]
+            out[2 * m * i + m : 2 * m * (i + 1)] = below[i]
+    for out, block, first in zip(outs, blocks, (z.cx // 2, 0)):
+        base, n = 2 * m * z.cx, block.shape[1]
+        for k in range(z.cx // 2):
+            out[base + k * n : base + (k + 1) * n] = block[first + k]
+
+
+def kernel_first(z, blocks, halos, count, rotated, *refs):
+    pieces = refs[:count]
+    refs = refs[count:]
     inv_t, g, s, targets, rho, y2, hot, out = refs[:8]
     parts, grouped, msg = refs[8:]
     wide = y2
@@ -233,30 +220,52 @@
     r = z.rows
     tiles = (0, r // 8)
 
-    lane = iota((r, LANES), 1)
-    row = iota((r, LANES), 0)
-
-    def unpack(piece, c, i, p):
-        rho[i + 1, c, PAD : PAD + r] = piece[p, 0:r]
-        g[i, c] = piece[p, r : 2 * r]
-        wide[i + 1, c, PAD : PAD + r] = piece[p, 2 * r : 3 * r]
-        wide[i + 1, c, PAD - 1 : PAD] = piece[p, 3 * r : 3 * r + 1]
-        wide[i + 1, c, PAD + r : PAD + r + 1] = piece[p, 3 * r + 1 : 3 * r + 2]
-        names = jnp.broadcast_to(piece[p, 3 * r + 2 : 3 * r + 3], (r, LANES))
-        names = jnp.sum(jnp.where(lane == row, names, 0.0), axis=1, keepdims=True)
-        targets[i, c] = jnp.broadcast_to(names, (r, LANES)).astype(jnp.int32)
-
-    for piece, (m, start, rotated) in zip(pieces, layout):
-
-        def each(p, carry, piece=piece, m=m, start=start, rotated=rotated):
-            i = p + start
-            if rotated:
-                i = i + gx * z.cx
-                i = jnp.where(i >= z.planes, i - z.planes, i)
-            unpack(piece, col ^ m, i, p)
+    n, h = z.cy, HALO
+    group = iota((z.nblock, LANES), 0).astype(f32) + (col * z.nblock).astype(f32)
+
+    def place(p):
+        if not rotated:
+            return p
+        i = p + gx * z.cx
+        return jnp.where(i >= z.planes, i - z.planes, i)
+
+    def spread(names, i, c, p, first, rows, at):
+        shape = (rows, LANES)
+        wanted = iota(shape, 1) == iota(shape, 0) + ((p % z.cx) * n + first)
+        value = jnp.sum(jnp.where(wanted, jnp.broadcast_to(names, shape), 0.0), axis=1, keepdims=True)
+        targets[i, c, at : at + rows] = jnp.broadcast_to(value, shape).astype(jnp.int32)
+
+    for which, base, m, start, planes in blocks:
+
+        def each(q, carry, piece=pieces[which], base=base, m=m, start=start):
+            p = q + start
+            i, c, row = place(p), col ^ m, base + q * (3 * n + 8)
+            rho[i + 1, c, PAD + h : PAD + h + n] = piece[pl.ds(row, n)]
+            g[i, c, h : h + n] = piece[pl.ds(row + n, n)]
+            wide[i + 1, c, PAD + h : PAD + h + n] = piece[pl.ds(row + 2 * n, n)]
+            spread(piece[pl.ds(row + 3 * n, 1)], i, c, p, 0, n, h)
             return carry
 
-        loop(piece.shape[0], each, z.small)
+        loop(planes, each, z.small)
+        if start == 0:
+            shift = 0 if rotated else gx * (z.cx * (3 * n + 8))
+            names = jnp.broadcast_to(pieces[which][pl.ds(base + shift + 3 * n, 1)], (z.nblock, LANES))
+            hot[:, m * LANES : (m + 1) * LANES] = (names == group).astype(jnp.bfloat16)
+
+    for which, base, m, start, planes in halos:
+
+        def each(q, carry, piece=pieces[which], base=base, m=m, start=start):
+            p = q + start
+            i, c, row = place(p), col ^ m, base + q * (6 * h + 16)
+            for top, first, edge, turn in ((row, 0, PAD - 1, n - h), (row + 3 * h + 8, h + n, PAD + r, 0)):
+                rho[i + 1, c, PAD + first : PAD + first + h] = piece[pl.ds(top, h)]
+                g[i, c, first : first + h] = piece[pl.ds(top + h, h)]
+                wide[i + 1, c, PAD + first : PAD + first + h] = piece[pl.ds(top + 2 * h, h)]
+                wide[i + 1, c, edge : edge + 1] = piece[pl.ds(top + 3 * h, 1)]
+                spread(piece[pl.ds(top + 3 * h + 1, 1)], i, c, p, turn, h, first)
+            return carry
+
+        loop(planes, each, z.small)
 
     def coefficients(i, t, c, x, total):
         diagonal = g[i, c, plain(t)] + x * total
@@ -269,13 +278,6 @@
         ]
 
     sweep(wide, tiles, z, coefficients)
-    group = iota((z.nblock, LANES), 0).astype(f32) + (col * z.nblock).astype(f32)
-    for piece, (m, start, _) in zip(pieces, layout):
-        if start:
-            continue
-        names = piece[0 if _ else gx * z.cx, 3 * r + 3 : 3 * r + 4, :].reshape(1, LANES)
-        match = jnp.broadcast_to(names, (z.nblock, LANES)) == group
-        hot[:, m * LANES : (m + 1) * LANES] = match.astype(jnp.bfloat16)
     presmooth(rho, g, y2, tiles, z)
     restrict_solve(rho, y2, g, s, hot, inv_t, parts, grouped, msg, z)
     for c in range(z.ngroup):
@@ -476,41 +478,59 @@
     )(*args)
 
 
-def gather_fields(z, right_side, diag_shift, stiffness, owner, group):
-    fields = (right_side, diag_shift, stiffness, owner, group)
-    edge = jax.ShapeDtypeStruct((z.cx, 3 * HALO + 8, LANES), f32)
-    head, tail = call(z, functools.partial(kernel_edges, z), [edge, edge], [], *fields, name="edges")
-    above = lax.ppermute(tail, "gy", [(i, i + 1) for i in range(z.gy - 1)])
-    below = lax.ppermute(head, "gy", [(i + 1, i) for i in range(z.gy - 1)])
-    (packed,) = call(
-        z, functools.partial(kernel_pack, z), [jax.ShapeDtypeStruct((z.cx, 3 * z.rows + 8, LANES), f32)],
-        [], *fields, above, below, name="pack",
+def gather_fields(z, fields, inverse):
+    cx, n, h = z.cx, 3 * z.cy + 8, 3 * HALO + 8
+    shape = lambda *dims: jax.ShapeDtypeStruct(dims, f32)
+    names = (fields[3] * z.nblock + fields[4]).astype(f32)
+    block = jnp.concatenate(fields[:3] + (jnp.broadcast_to(names, (cx, 8, LANES)),), axis=1)
+    edge = shape(cx, h, LANES)
+    head, tail, block = call(
+        z, functools.partial(kernel_edges, z), [edge, edge, shape(cx, n, LANES)], [], block, name="edges"
     )
+    def neighbours():
+        above = lax.ppermute(tail, "gy", [(i, i + 1) for i in range(z.gy - 1)])
+        return above, lax.ppermute(head, "gy", [(i + 1, i) for i in range(z.gy - 1)])
+
+    flat = lambda value: value.reshape(-1, LANES)
 
     def turn(value, bit):
         return lax.ppermute(value, "col", [(i, i ^ bit) for i in range(z.col)])
 
+    halo = functools.partial(kernel_halo, z)
     if z.gx == 2:
         swap = lambda value: lax.ppermute(value, "gx", [(0, 1), (1, 0)])
-        cut = z.cx // 2
-        across, beside = swap(packed), turn(packed, 2)
-        corner_low, corner_high = turn(across[:cut], 2), swap(beside[cut:])
-        pieces = [(packed, 0, 0), (across, 0, z.cx), (beside, 2, 0)]
-        pieces += [(corner_low, 2, z.cx), (corner_high, 2, z.cx + cut)]
-        rotated = True
+        across, beside = swap(block), turn(block, 2)
+        above, below = neighbours()
+        above, inverse = lax.optimization_barrier((above, inverse))
+        whole = shape(2 * cx * h + cx // 2 * n, LANES)
+        to_x, to_y = call(z, halo, [whole, whole], [], above, below, beside, across, name="halo")
+        from_x, from_y = swap(to_x), turn(to_y, 2)
+        half = cx * h
+        corner_low, corner_high = turn(from_x[:half], 2), swap(from_y[half : 2 * half])
+        pieces = [flat(block), flat(across), flat(beside), to_x, from_x, from_y, corner_low, corner_high]
+        end, cut = 2 * half, cx // 2
+        blocks = [(0, 0, 0, 0, cx), (1, 0, 0, cx, cx), (2, 0, 2, 0, cx)]
+        blocks += [(5, end, 2, cx, cut), (4, end, 2, cx + cut, cut)]
+        halos = [(3, 0, 0, 0, cx), (4, 0, 0, cx, cx), (5, 0, 2, 0, cx)]
+        halos += [(6, 0, 2, cx, cut), (7, 0, 2, cx + cut, cut)]
     else:
-        packed = lax.all_gather(packed, "gx", axis=0, tiled=True)
-        pieces = [(packed, 0, 0), (turn(packed, 2), 2, 0)]
-        rotated = False
-    pieces = pieces + [(turn(value, 1), m ^ 1, start) for value, m, start in pieces]
-    return [value for value, _, _ in pieces], [(m, start, rotated) for _, m, start in pieces]
+        above, below = neighbours()
+        (edges,) = call(z, halo, [shape(2 * cx * h, LANES)], [], above, below, name="halo")
+        pieces = [lax.all_gather(value, "gx", axis=0, tiled=True) for value in (flat(block), edges)]
+        pieces += [turn(value, 2) for value in pieces]
+        blocks = [(0, 0, 0, 0, z.planes), (2, 0, 2, 0, z.planes)]
+        halos = [(1, 0, 0, 0, z.planes), (3, 0, 2, 0, z.planes)]
+    count = len(pieces)
+    pieces = pieces + [turn(value, 1) for value in pieces]
+    mirror = lambda table: table + [(w + count, base, m ^ 1, a, b) for w, base, m, a, b in table]
+    return pieces, (mirror(blocks), mirror(halos), 2 * count, z.gx == 2), inverse
 
 
 def on_device(right_side, diag_shift, stiffness, block_owner, block_group, coarse_inverse):
     cx, cy, depth = right_side.shape
     z = Sizes([lax.axis_size(a) for a in ALL], cx, cy)
-    pieces, layout = gather_fields(z, right_side, diag_shift, stiffness, block_owner, block_group)
-    inv_t = jnp.swapaxes(coarse_inverse[0], 1, 2)
+    fields = (right_side, diag_shift, stiffness, block_owner, block_group)
+    pieces, layout, inv_t = gather_fields(z, fields, jnp.swapaxes(coarse_inverse[0], 1, 2))
 
     shape = lambda *dims, dtype=f32: jax.ShapeDtypeStruct(dims, dtype)
     field = (z.planes, z.col, z.rows, LANES)
@@ -522,7 +542,7 @@
     ]
     g, s, targets, rho, y2, hot, msg = call(
         z,
-        functools.partial(kernel_first, z, layout),
+        functools.partial(kernel_first, z, *layout),
         [
             shape(*field), shape(*field), shape(*field, dtype=jnp.int32), shape(*padded), shape(*padded),
             shape(z.nblock, z.col * LANES, dtype=jnp.bfloat16), shape(z.devices, z.ngroup, LANES),

time: 106 us -> 103 us (0.972)
  local copies, waits for them, and re-layouts: 5.09 us -> 1.26 us
  waiting for transfers between devices: 17.5 us -> 15.1 us
  other arithmetic: 0 us -> 1.59 us
  starting transfers between devices: 12.2 us -> 13.4 us
    unnamed x11 -> x1, local copies, waits for them, and re-layouts: 5.06 us -> 1.24 us
    ppermute x7 -> x11, starting transfers between devices: 2.99 us -> 6.04 us  [turn(): return lax.ppermute(value, 'col', [(i, i ^ bit) for i in range(z.col)])]
    ppermute x7 -> x11, waiting for transfers between devices: 9.33 us -> 7.28 us  [turn(): return lax.ppermute(value, 'col', [(i, i ^ bit) for i in range(z.col)])]
    ppermute x2, starting transfers between devices: 6.21 us -> 4.77 us  [the longest x1 3.47 us: neighbours(): above = lax.ppermute(tail, 'gy', [(i, i + 1) for i in range(z.gy - 1)])]
    ppermute x2, waiting for transfers between devices: 5.39 us -> 4.13 us  [the longest x1 4.13 us: neighbours(): lax.ppermute(head, 'gy', [(i + 1, i) for i in range(z.gy - 1)])]
    ppermute x2 -> x3, waiting for transfers between devices: 2.83 us -> 3.72 us  [gather_fields(): swap = lambda value: lax.ppermute(value, 'gx', [(0, 1), (1, 0)])]
    ppermute x2 -> x3, starting transfers between devices: 3.05 us -> 2.63 us  [gather_fields(): swap = lambda value: lax.ppermute(value, 'gx', [(0, 1), (1, 0)])]
  transfers between devices with their start and end apart: 11 -> 16, of which waited for: 7 -> 8; matrix products, arithmetic and copies ran while one was open for 1% -> 1% of each run, Pallas kernels for 0% -> 0%
where the time goes in v4:
time: 103 us
  blocking collectives  52.5 us (51%)
  Pallas kernels  18.5 us (18%)
  waiting for transfers between devices  15.1 us (15%)
  starting transfers between devices  13.4 us (13%)
  other arithmetic  1.59 us (2%)
  local copies, waits for them, and re-layouts  1.26 us (1%)
    all_to_all x5, blocking collectives, on_device(): lax.all_to_all(m, ALL, split_axis=0, concat_axis=0, tiled=True)  52.5 us
    pallas_call x8, Pallas kernels, call(): pl.pallas_call(body, out_shape=outs, in_specs=[vmem] * len(args), out_spe...  18.5 us
    ppermute x11, waiting for transfers between devices, turn(): return lax.ppermute(value, 'col', [(i, i ^ bit) for i in range(z.col)])  7.28 us
    ppermute x11, starting transfers between devices, turn(): return lax.ppermute(value, 'col', [(i, i ^ bit) for i in range(z.col)])  6.04 us
    ppermute x1, waiting for transfers between devices, neighbours(): lax.ppermute(head, 'gy', [(i + 1, i) for i in range(z.gy - 1)])  4.13 us
    ppermute x3, waiting for transfers between devices, gather_fields(): swap = lambda value: lax.ppermute(value, 'gx', [(0, 1), (1, 0)])  3.72 us
    ppermute x1, starting transfers between devices, neighbours(): above = lax.ppermute(tail, 'gy', [(i, i + 1) for i in range(z.gy - 1)])  3.47 us
    ppermute x3, starting transfers between devices, gather_fields(): swap = lambda value: lax.ppermute(value, 'gx', [(0, 1), (1, 0)])  2.63 us
  transfers between devices with their start and end apart: 16, of which 8 were waited for; matrix products, arithmetic and copies ran while one was open for 1% of the time, Pallas kernels for 0%

profile of v4, /device:TPU:0, one launch (start us, length us, event | category | flops | bytes accessed | tf_op | source)
XLA Modules:
  0.0 103.1 jit_solution(9654583760271278039)
XLA Ops:
  0.6 0.7 convert_bitcast_fusion
  1.3 0.9 pad_maximum_fusion.block
  2.3 3.0 %collective-permute-start.1 = (f32[4,104,128]{2,1,0:T(8,128)S(1)}, f32[4,104,128]{2,1,0:T(8,128)S(1)}, u32[]{:S(2)}, u32[]{:S(2)}) collective-permute-start(f32[4,104,128]{2,1,0:T(8,128)S(1)} %get-tuple-element.35), channel_id=1, source_target_pairs={{0,2},{1,3},{2,0},{3,1},{4,6},{5,7},{6,4},{7,5},{8,10},{9,11},{10,... | collective-permute-start | bytes 638984 | tf_op jit(solution)/shard_map/ppermute | solution.py:497
  5.3 1.5 %collective-permute-start = (f32[4,104,128]{2,1,0:T(8,128)S(1)}, f32[4,104,128]{2,1,0:T(8,128)S(1)}, u32[]{:S(2)}, u32[]{:S(2)}) collective-permute-start(f32[4,104,128]{2,1,0:T(8,128)S(1)} %get-tuple-element.35), channel_id=1, source_target_pairs={{0,16},{16,0},{1,17},{17,1},{2,18},{18,2},{3,19},{19,3},{4,20},{20... | collective-permute-start | bytes 638984 | tf_op jit(solution)/shard_map/ppermute | solution.py:501
  6.8 3.5 %collective-permute-start.2 = (f32[4,56,128]{2,1,0:T(8,128)S(1)}, f32[4,56,128]{2,1,0:T(8,128)S(1)}, u32[]{:S(2)}, u32[]{:S(2)}) collective-permute-start(f32[4,56,128]{2,1,0:T(8,128)S(1)} %get-tuple-element.36), channel_id=1, source_target_pairs={{0,4},{4,8},{8,12},{1,5},{5,9},{9,13},{2,6},{6,10},{10,14},{3,7},{... | collective-permute-start | bytes 344072 | tf_op jit(solution)/shard_map/ppermute | solution.py:491
  10.3 1.3 %collective-permute-start.3 = (f32[4,56,128]{2,1,0:T(8,128)S(1)}, f32[4,56,128]{2,1,0:T(8,128)S(1)}, u32[]{:S(2)}, u32[]{:S(2)}) collective-permute-start(f32[4,56,128]{2,1,0:T(8,128)S(1)} %get-tuple-element.38), channel_id=1, source_target_pairs={{4,0},{8,4},{12,8},{5,1},{9,5},{13,9},{6,2},{10,6},{14,10},{7,3},{... | collective-permute-start | bytes 344072 | tf_op jit(solution)/shard_map/ppermute | solution.py:492
  11.6 1.2 %copy.8 = f32[1,8,128,128]{2,3,1,0:T(8,128)S(1)} copy(f32[1,8,128,128]{3,2,1,0:T(8,128)} %param.11) | data formatting | bytes 1048576 | tf_op args[5]
  12.8 0.0 collective-permute-done.2.above
  12.8 4.1 %collective-permute-done.3.below = f32[4,56,128]{2,1,0:T(8,128)S(1)} collective-permute-done((f32[4,56,128]{2,1,0:T(8,128)S(1)}, f32[4,56,128]{2,1,0:T(8,128)S(1)}, u32[]{:S(2)}, u32[]{:S(2)}) %collective-permute-start.3) | collective-permute-done | bytes 114720 | tf_op jit(solution)/shard_map/ppermute | solution.py:492
  17.0 0.0 collective-permute-done.1.refs_0_
  17.0 0.0 collective-permute-done.refs_1_
  17.0 0.6 collective-permute-start.5
  17.6 0.5 collective-permute-start.4
  18.1 0.0 collective-permute-start.8
  18.1 0.5 collective-permute-start.10
  18.6 0.0 collective-permute-start.9
  18.6 1.0 collective-permute-done.8.refs_8_
  19.6 0.1 collective-permute-start.11
  19.7 5.0 %collective-permute-done.5.refs_5_ = f32[656,128]{1,0:T(8,128)S(1)} collective-permute-done((f32[656,128]{1,0:T(8,128)S(1)}, f32[656,128]{1,0:T(8,128)S(1)}, u32[]{:S(2)}, u32[]{:S(2)}) %collective-permute-start.5) | collective-permute-done | bytes 335904 | tf_op jit(solution)/shard_map/ppermute | solution.py:497
  24.7 0.0 collective-permute-start.13
  24.7 0.2 collective-permute-done.4.refs_4_
  25.0 0.3 collective-permute-start.12
  25.3 0.0 collective-permute-done.10.refs_10_
  25.3 0.6 collective-permute-start.7
  25.9 0.0 collective-permute-done.9.refs_9_
  25.9 1.2 %collective-permute-start.6 = (f32[224,128]{1,0:T(8,128)S(1)}, f32[224,128]{1,0:T(8,128)S(1)}, u32[]{:S(2)}, u32[]{:S(2)}) collective-permute-start(f32[224,128]{1,0:T(8,128)S(1)} %slice.8), channel_id=1, source_target_pairs={{0,2},{1,3},{2,0},{3,1},{4,6},{5,7},{6,4},{7,5},{8,10},{9,11},{10,... | collective-permute-start | bytes 344072 | tf_op jit(solution)/shard_map/ppermute | solution.py:497
  27.1 3.5 %collective-permute-done.7.refs_7_ = f32[224,128]{1,0:T(8,128)S(1)} collective-permute-done((f32[224,128]{1,0:T(8,128)S(1)}, f32[224,128]{1,0:T(8,128)S(1)}, u32[]{:S(2)}, u32[]{:S(2)}) %collective-permute-start.7) | collective-permute-done | bytes 114720 | tf_op jit(solution)/shard_map/ppermute | solution.py:501
  30.6 0.0 collective-permute-start.15
  30.6 0.3 collective-permute-done.6.refs_6_
  30.9 0.3 collective-permute-start.14
  31.1 0.0 collective-permute-done.11.refs_11_
  31.1 0.8 collective-permute-done.15.refs_15_
  31.9 0.3 collective-permute-done.14.refs_14_
  32.2 0.0 collective-permute-done.13.refs_13_
  32.2 0.0 collective-permute-done.12.refs_12_
  32.2 2.5 %begin.1 = (f32[8,4,64,128]{3,2,1,0:T(8,128)S(1)}, f32[8,4,64,128]{3,2,1,0:T(8,128)S(1)}, s32[8,4,64,128]{3,2,1,0:T(8,128)S(1)}, f32[10,4,80,128]{3,2,1,0:T(8,12...) custom-call(f32[416,128]{1,0:T(8,128)S(1)} %bitcast.18, ...), custom_call_target="tpu_custom_call" | custom-call | tf_op jit(solution)/shard_map/begin/pallas_call | solution.py:470
  34.7 12.9 %all_to_all.25.refs_0_ = f32[32,8,128]{2,1,0:T(8,128)S(1)} all-to-all(f32[32,8,128]{2,1,0:T(8,128)S(1)} %get-tuple-element.42), channel_id=1, replica_groups=mesh['gx'=2,'gy'=4,'col'=4] {'gx','gy','col'}, dimensions={0} | all-to-all | bytes 262144 | tf_op jit(solution)/shard_map/all_to_all | solution.py:553
  47.5 4.2 %step0.1 = (f32[6,4,32,128]{3,2,1,0:T(8,128)S(1)}, f32[32,1,1152]{2,1,0:T(1,128)S(1)}, f32[10,4,80,128]{3,2,1,0:T(8,128)S(1)}, f32[10,4,80,128]{3,2,1,0:T(8,128)S(1)}) custom-call(f32[32,8,128]{2,1,0:T(8,128)S(1)} %all_to_all.25.refs_0_, f32[8,4,64,128]{3,2,1,0:T(8,128)S(1)} %get-tuple-element.43.refs_1_.g, ...), custom_call_target="tpu_custom_call" | custom-call | tf_op jit(solution)/shard_map/step0/pallas_call | solution.py:470
  51.7 10.1 %all_to_all.26.refs_0_ = f32[32,1,1152]{2,1,0:T(1,128)S(1)} all-to-all(f32[32,1,1152]{2,1,0:T(1,128)S(1)} %get-tuple-element.49), channel_id=1, replica_groups=mesh['gx'=2,'gy'=4,'col'=4] {'gx','gy','col'}, dimensions={0} | all-to-all | bytes 294912 | tf_op jit(solution)/shard_map/all_to_all | solution.py:553
  61.8 4.3 %step1.1 = (f32[6,4,32,128]{3,2,1,0:T(8,128)S(1)}, f32[32,1,1152]{2,1,0:T(1,128)S(1)}, f32[10,4,80,128]{3,2,1,0:T(8,128)S(1)}, f32[10,4,80,128]{3,2,1,0:T(8,128)...) custom-call(f32[32,1,1152]{2,1,0:T(1,128)S(1)} %all_to_all.26.refs_0_, ...), custom_call_target="tpu_custom_call" | custom-call | tf_op jit(solution)/shard_map/step1/pallas_call | solution.py:470
  66.2 10.2 %all_to_all.27.refs_0_ = f32[32,1,1152]{2,1,0:T(1,128)S(1)} all-to-all(f32[32,1,1152]{2,1,0:T(1,128)S(1)} %get-tuple-element.53), channel_id=1, replica_groups=mesh['gx'=2,'gy'=4,'col'=4] {'gx','gy','col'}, dimensions={0} | all-to-all | bytes 294912 | tf_op jit(solution)/shard_map/all_to_all | solution.py:553
  76.4 3.8 %step2.1 = (f32[6,4,32,128]{3,2,1,0:T(8,128)S(1)}, f32[32,1,1152]{2,1,0:T(1,128)S(1)}, f32[10,4,80,128]{3,2,1,0:T(8,128)S(1)}, f32[10,4,80,128]{3,2,1,0:T(8,128)...) custom-call(f32[32,1,1152]{2,1,0:T(1,128)S(1)} %all_to_all.27.refs_0_, ...), custom_call_target="tpu_custom_call" | custom-call | tf_op jit(solution)/shard_map/step2/pallas_call | solution.py:470
  80.3 10.3 %all_to_all.28.refs_0_ = f32[32,1,1152]{2,1,0:T(1,128)S(1)} all-to-all(f32[32,1,1152]{2,1,0:T(1,128)S(1)} %get-tuple-element.59), channel_id=1, replica_groups=mesh['gx'=2,'gy'=4,'col'=4] {'gx','gy','col'}, dimensions={0} | all-to-all | bytes 294912 | tf_op jit(solution)/shard_map/all_to_all | solution.py:553
  90.6 2.7 %step3.1 = (f32[7,4,32,128]{3,2,1,0:T(8,128)S(1)}, f32[32,1,128]{2,1,0:T(1,128)S(1)}, f32[1,128]{1,0:T(1,128)S(1)}) custom-call(f32[32,1,1152]{2,1,0:T(1,128)S(1)} %all_to_all.28.refs_0_, f32[8,4,64,128]{3,2,1,0:T(8,128)S(1)} %get-tuple-element.43.refs_1_.g, f32[8,4,64,128]{3,2,1,0:T(8,128)S(1)} %get-tuple-element.44.refs_2_.s, ...), custom_call_target="tpu_custom_call" | custom-call | tf_op jit(solution)/shard_map/step3/pallas_call | solution.py:470
  93.2 9.0 %all_to_all.29.recv = f32[32,1,128]{2,1,0:T(1,128)S(1)} all-to-all(f32[32,1,128]{2,1,0:T(1,128)S(1)} %get-tuple-element.65), channel_id=1, replica_groups=mesh['gx'=2,'gy'=4,'col'=4] {'gx','gy','col'}, dimensions={0} | all-to-all | bytes 32768 | tf_op jit(solution)/shard_map/all_to_all | solution.py:553
  102.2 0.9 end.1
  (5 shorter events, 0.1 us)
Async XLA Ops:
  2.3 14.7 %collective-permute-start.1 = (f32[4,104,128]{2,1,0:T(8,128)S(1)}, f32[4,104,128]{2,1,0:T(8,128)S(1)}, u32[]{:S(2)}, u32[]{:S(2)}) collective-permute-start(f32[4,104,128]{2,1,0:T(8,128)S(1)} %get-tuple-element.35), channel_id=1, source_target_pairs={{0,2},{1,3},{2,0},{3,1},{4,6},{5,7},{6,4},{7,5},{8,10},{9,11},{10,... | collective-permute-start | bytes 638984 | tf_op jit(solution)/shard_map/ppermute | solution.py:497
  5.3 11.7 %collective-permute-start = (f32[4,104,128]{2,1,0:T(8,128)S(1)}, f32[4,104,128]{2,1,0:T(8,128)S(1)}, u32[]{:S(2)}, u32[]{:S(2)}) collective-permute-start(f32[4,104,128]{2,1,0:T(8,128)S(1)} %get-tuple-element.35), channel_id=1, source_target_pairs={{0,16},{16,0},{1,17},{17,1},{2,18},{18,2},{3,19},{19,3},{4,20},{20... | collective-permute-start | bytes 638984 | tf_op jit(solution)/shard_map/ppermute | solution.py:501
  6.8 6.0 %collective-permute-start.2 = (f32[4,56,128]{2,1,0:T(8,128)S(1)}, f32[4,56,128]{2,1,0:T(8,128)S(1)}, u32[]{:S(2)}, u32[]{:S(2)}) collective-permute-start(f32[4,56,128]{2,1,0:T(8,128)S(1)} %get-tuple-element.36), channel_id=1, source_target_pairs={{0,4},{4,8},{8,12},{1,5},{5,9},{9,13},{2,6},{6,10},{10,14},{3,7},{... | collective-permute-start | bytes 344072 | tf_op jit(solution)/shard_map/ppermute | solution.py:491
  10.3 6.7 %collective-permute-start.3 = (f32[4,56,128]{2,1,0:T(8,128)S(1)}, f32[4,56,128]{2,1,0:T(8,128)S(1)}, u32[]{:S(2)}, u32[]{:S(2)}) collective-permute-start(f32[4,56,128]{2,1,0:T(8,128)S(1)} %get-tuple-element.38), channel_id=1, source_target_pairs={{4,0},{8,4},{12,8},{5,1},{9,5},{13,9},{6,2},{10,6},{14,10},{7,3},{... | collective-permute-start | bytes 344072 | tf_op jit(solution)/shard_map/ppermute | solution.py:492
  17.0 7.7 %collective-permute-start.5 = (f32[656,128]{1,0:T(8,128)S(1)}, f32[656,128]{1,0:T(8,128)S(1)}, u32[]{:S(2)}, u32[]{:S(2)}) collective-permute-start(f32[656,128]{1,0:T(8,128)S(1)} %get-tuple-element.40), channel_id=1, source_target_pairs={{0,2},{1,3},{2,0},{3,1},{4,6},{5,7},{6,4},{7,5},{8,10},{9,11},{10,... | collective-permute-start | bytes 1007624 | tf_op jit(solution)/shard_map/ppermute | solution.py:497
  17.6 7.4 %collective-permute-start.4 = (f32[656,128]{1,0:T(8,128)S(1)}, f32[656,128]{1,0:T(8,128)S(1)}, u32[]{:S(2)}, u32[]{:S(2)}) collective-permute-start(f32[656,128]{1,0:T(8,128)S(1)} %get-tuple-element.39.refs_3_), channel_id=1, source_target_pairs={{0,16},{16,0},{1,17},{17,1},{2,18},{18,2},{3,19},{19,3},{4,20},{20... | collective-permute-start | bytes 1007624 | tf_op jit(solution)/shard_map/ppermute | solution.py:501
  18.1 1.5 %collective-permute-start.8 = (f32[416,128]{1,0:T(8,128)S(1)}, f32[416,128]{1,0:T(8,128)S(1)}, u32[]{:S(2)}, u32[]{:S(2)}) collective-permute-start(f32[416,128]{1,0:T(8,128)S(1)} %bitcast.17), channel_id=1, source_target_pairs={{0,1},{1,0},{2,3},{3,2},{4,5},{5,4},{6,7},{7,6},{8,9},{9,8},{10,11... | collective-permute-start | bytes 638984 | tf_op jit(solution)/shard_map/ppermute | solution.py:497
  18.1 7.1 %collective-permute-start.10 = (f32[416,128]{1,0:T(8,128)S(1)}, f32[416,128]{1,0:T(8,128)S(1)}, u32[]{:S(2)}, u32[]{:S(2)}) collective-permute-start(f32[416,128]{1,0:T(8,128)S(1)} %bitcast.13), channel_id=1, source_target_pairs={{0,1},{1,0},{2,3},{3,2},{4,5},{5,4},{6,7},{7,6},{8,9},{9,8},{10,11... | collective-permute-start | bytes 638984 | tf_op jit(solution)/shard_map/ppermute | solution.py:497
  18.6 7.2 %collective-permute-start.9 = (f32[416,128]{1,0:T(8,128)S(1)}, f32[416,128]{1,0:T(8,128)S(1)}, u32[]{:S(2)}, u32[]{:S(2)}) collective-permute-start(f32[416,128]{1,0:T(8,128)S(1)} %bitcast.15), channel_id=1, source_target_pairs={{0,1},{1,0},{2,3},{3,2},{4,5},{5,4},{6,7},{7,6},{8,9},{9,8},{10,11... | collective-permute-start | bytes 638984 | tf_op jit(solution)/shard_map/ppermute | solution.py:497
  19.6 11.5 %collective-permute-start.11 = (f32[656,128]{1,0:T(8,128)S(1)}, f32[656,128]{1,0:T(8,128)S(1)}, u32[]{:S(2)}, u32[]{:S(2)}) collective-permute-start(f32[656,128]{1,0:T(8,128)S(1)} %get-tuple-element.39.refs_3_), channel_id=1, source_target_pairs={{0,1},{1,0},{2,3},{3,2},{4,5},{5,4},{6,7},{7,6},{8,9},{9,8},{10,11... | collective-permute-start | bytes 1007624 | tf_op jit(solution)/shard_map/ppermute | solution.py:497
  24.7 7.5 %collective-permute-start.13 = (f32[656,128]{1,0:T(8,128)S(1)}, f32[656,128]{1,0:T(8,128)S(1)}, u32[]{:S(2)}, u32[]{:S(2)}) collective-permute-start(f32[656,128]{1,0:T(8,128)S(1)} %collective-permute-done.5.refs_5_), channel_id=1, source_target_pairs={{0,1},{1,0},{2,3},{3,2},{4,5},{5,4},{6,7},{7,6},{8,9},{9,8},{10,11... | collective-permute-start | bytes 1007624 | tf_op jit(solution)/shard_map/ppermute | solution.py:497
  25.0 7.3 %collective-permute-start.12 = (f32[656,128]{1,0:T(8,128)S(1)}, f32[656,128]{1,0:T(8,128)S(1)}, u32[]{:S(2)}, u32[]{:S(2)}) collective-permute-start(f32[656,128]{1,0:T(8,128)S(1)} %collective-permute-done.4.refs_4_), channel_id=1, source_target_pairs={{0,1},{1,0},{2,3},{3,2},{4,5},{5,4},{6,7},{7,6},{8,9},{9,8},{10,11... | collective-permute-start | bytes 1007624 | tf_op jit(solution)/shard_map/ppermute | solution.py:497
  25.3 5.3 %collective-permute-start.7 = (f32[224,128]{1,0:T(8,128)S(1)}, f32[224,128]{1,0:T(8,128)S(1)}, u32[]{:S(2)}, u32[]{:S(2)}) collective-permute-start(f32[224,128]{1,0:T(8,128)S(1)} %slice.9), channel_id=1, source_target_pairs={{0,16},{16,0},{1,17},{17,1},{2,18},{18,2},{3,19},{19,3},{4,20},{20... | collective-permute-start | bytes 344072 | tf_op jit(solution)/shard_map/ppermute | solution.py:501
  25.9 5.0 %collective-permute-start.6 = (f32[224,128]{1,0:T(8,128)S(1)}, f32[224,128]{1,0:T(8,128)S(1)}, u32[]{:S(2)}, u32[]{:S(2)}) collective-permute-start(f32[224,128]{1,0:T(8,128)S(1)} %slice.8), channel_id=1, source_target_pairs={{0,2},{1,3},{2,0},{3,1},{4,6},{5,7},{6,4},{7,5},{8,10},{9,11},{10,... | collective-permute-start | bytes 344072 | tf_op jit(solution)/shard_map/ppermute | solution.py:497
  30.6 1.3 %collective-permute-start.15 = (f32[224,128]{1,0:T(8,128)S(1)}, f32[224,128]{1,0:T(8,128)S(1)}, u32[]{:S(2)}, u32[]{:S(2)}) collective-permute-start(f32[224,128]{1,0:T(8,128)S(1)} %collective-permute-done.7.refs_7_), channel_id=1, source_target_pairs={{0,1},{1,0},{2,3},{3,2},{4,5},{5,4},{6,7},{7,6},{8,9},{9,8},{10,11... | collective-permute-start | bytes 344072 | tf_op jit(solution)/shard_map/ppermute | solution.py:497
  30.9 1.3 %collective-permute-start.14 = (f32[224,128]{1,0:T(8,128)S(1)}, f32[224,128]{1,0:T(8,128)S(1)}, u32[]{:S(2)}, u32[]{:S(2)}) collective-permute-start(f32[224,128]{1,0:T(8,128)S(1)} %collective-permute-done.6.refs_6_), channel_id=1, source_target_pairs={{0,1},{1,0},{2,3},{3,2},{4,5},{5,4},{6,7},{7,6},{8,9},{9,8},{10,11... | collective-permute-start | bytes 344072 | tf_op jit(solution)/shard_map/ppermute | solution.py:497

commit v5 on v4

--- a/solution.py
+++ b/solution.py
@@ -89,8 +89,13 @@
             self.release()
 
 
-def sweep(src, tiles, z, visit):
+def first_plane(z, span):
+    return lax.axis_index("gx") * (z.planes - span) if span else 0
+
+
+def sweep(src, tiles, z, visit, span=None):
     lo, hi = tiles
+    start = first_plane(z, span)
     each = hi - lo if z.small else 1
 
     def body(turn, carry):
@@ -98,8 +103,9 @@
         for part in range(each):
             t = lo + turn * each + part
             load = lambda i: [src[i, c, inner(t)] for c in range(z.col)]
-            below, mid = load(0), load(1)
-            for i in range(z.planes):
+            below, mid = load(start), load(start + 1)
+            for k in range(span or z.planes):
+                i = start + k
                 above = load(i + 2)
                 across = row_sums(src, i + 1, t, mid, z)
                 made = []
@@ -128,12 +134,12 @@
     sweep(rho, tiles, z, visit)
 
 
-def smooth(src, rho, g, out, w, tiles, z):
+def smooth(src, rho, g, out, w, tiles, z, span=None):
     def visit(i, t, c, value, total):
         moved = rho[i + 1, c, inner(t)] + g[i, c, plain(t)] * total
         return [(out, (i + 1, c, inner(t)), (1.0 - w) * value + w * moved)]
 
-    sweep(src, tiles, z, visit)
+    sweep(src, tiles, z, visit, span)
 
 
 def restrict_solve(rho, y2, g, s, hot, inv_t, parts, grouped, msg, z):
@@ -284,7 +290,7 @@
         out[:, c : c + 1, :] = jnp.broadcast_to(msg[c][None], (z.devices, 1, LANES))
 
 
-def prolong(recv, table, y2, s, targets, out, tiles, z, packed):
+def prolong(recv, table, y2, s, targets, out, tiles, z, packed, span=None):
     n = z.ngroup
     if packed:
 
@@ -301,7 +307,10 @@
 
     tiles = tuple(range(tiles[0], tiles[1]))
 
-    def body(i, carry):
+    start = first_plane(z, span)
+
+    def body(k, carry):
+        i = start + k
         gx = i // z.cx
         stores = Stores()
         for tile in tiles:
@@ -326,7 +335,7 @@
         stores.close()
         return carry
 
-    loop(z.planes, body, z.small)
+    loop(span or z.planes, body, z.small)
 
 
 def weighted(a, b, h):
@@ -356,9 +365,14 @@
     trim = 1 if step >= 1 else 0
     rows = (trim, z.rows // 8 - trim)
     early = (0, z.rows // 8) if step <= 1 else rows
-    prolong(k["recv"], table, k["y2"], s, k["targets"], ya, early, z, packed=not first)
-    smooth(ya, rho, g, yb, w2, early, z)
-    smooth(yb, rho, g, ya, w1, early, z)
+    spans = [None] * 4
+    if last:
+        rows = (HALO // 8, (HALO + z.cy) // 8)
+        if z.gx == 2 and z.cx > 3:
+            spans = [z.cx + n for n in (3, 2, 1, 0)]
+    prolong(k["recv"], table, k["y2"], s, k["targets"], ya, early, z, not first, spans[0])
+    smooth(ya, rho, g, yb, w2, early, z, spans[1])
+    smooth(yb, rho, g, ya, w1, early, z, spans[2])
 
     gx, col = lax.axis_index("gx"), lax.axis_index("col")
     own_rows = slice(HALO, HALO + z.cy)
@@ -407,7 +421,7 @@
 
         w_now = rho[planes1, col, own_inner]
         m_now = ya[planes1, col, own_inner]
-        sweep(ya, rows, z, image)
+        sweep(ya, rows, z, image, spans[3])
         state, state_out = k["state"], k["state_out"]
         r, u = state[0], state[1]
         p, q, sv = u, m_now, w_now

time: 103 us -> 103 us (level)
  no operation moved by 1% of the time
where the time goes in v5:
time: 103 us; the launch traced here: 102 us
  blocking collectives  52.5 us (51%)
  Pallas kernels  17.8 us (17%)
  waiting for transfers between devices  15.1 us (15%)
  starting transfers between devices  13.4 us (13%)
  other arithmetic  1.59 us (2%)
  local copies, waits for them, and re-layouts  1.26 us (1%)
    all_to_all x5, blocking collectives, on_device(): lax.all_to_all(m, ALL, split_axis=0, concat_axis=0, tiled=True)  52.5 us
    pallas_call x8, Pallas kernels, call(): pl.pallas_call(body, out_shape=outs, in_specs=[vmem] * len(args), out_spe...  17.8 us
    ppermute x11, waiting for transfers between devices, turn(): return lax.ppermute(value, 'col', [(i, i ^ bit) for i in range(z.col)])  7.28 us
    ppermute x11, starting transfers between devices, turn(): return lax.ppermute(value, 'col', [(i, i ^ bit) for i in range(z.col)])  6.04 us
    ppermute x1, waiting for transfers between devices, neighbours(): lax.ppermute(head, 'gy', [(i + 1, i) for i in range(z.gy - 1)])  4.13 us
    ppermute x3, waiting for transfers between devices, gather_fields(): swap = lambda value: lax.ppermute(value, 'gx', [(0, 1), (1, 0)])  3.72 us
    ppermute x1, starting transfers between devices, neighbours(): above = lax.ppermute(tail, 'gy', [(i, i + 1) for i in range(z.gy - 1)])  3.47 us
    ppermute x3, starting transfers between devices, gather_fields(): swap = lambda value: lax.ppermute(value, 'gx', [(0, 1), (1, 0)])  2.63 us
  transfers between devices with their start and end apart: 16, of which 8 were waited for; matrix products, arithmetic and copies ran while one was open for 1% of the time, Pallas kernels for 0%

profile of v5, /device:TPU:0, one launch (start us, length us, event | category | flops | bytes accessed | tf_op | source)
XLA Modules:
  0.0 102.5 jit_solution(5421830703270053568)
XLA Ops:
  0.6 0.7 convert_bitcast_fusion
  1.3 0.9 pad_maximum_fusion.block
  2.3 3.0 %collective-permute-start.1 = (f32[4,104,128]{2,1,0:T(8,128)S(1)}, f32[4,104,128]{2,1,0:T(8,128)S(1)}, u32[]{:S(2)}, u32[]{:S(2)}) collective-permute-start(f32[4,104,128]{2,1,0:T(8,128)S(1)} %get-tuple-element.35), channel_id=1, source_target_pairs={{0,2},{1,3},{2,0},{3,1},{4,6},{5,7},{6,4},{7,5},{8,10},{9,11},{10,... | collective-permute-start | bytes 638984 | tf_op jit(solution)/shard_map/ppermute | solution.py:511
  5.3 1.5 %collective-permute-start = (f32[4,104,128]{2,1,0:T(8,128)S(1)}, f32[4,104,128]{2,1,0:T(8,128)S(1)}, u32[]{:S(2)}, u32[]{:S(2)}) collective-permute-start(f32[4,104,128]{2,1,0:T(8,128)S(1)} %get-tuple-element.35), channel_id=1, source_target_pairs={{0,16},{16,0},{1,17},{17,1},{2,18},{18,2},{3,19},{19,3},{4,20},{20... | collective-permute-start | bytes 638984 | tf_op jit(solution)/shard_map/ppermute | solution.py:515
  6.8 3.5 %collective-permute-start.2 = (f32[4,56,128]{2,1,0:T(8,128)S(1)}, f32[4,56,128]{2,1,0:T(8,128)S(1)}, u32[]{:S(2)}, u32[]{:S(2)}) collective-permute-start(f32[4,56,128]{2,1,0:T(8,128)S(1)} %get-tuple-element.36), channel_id=1, source_target_pairs={{0,4},{4,8},{8,12},{1,5},{5,9},{9,13},{2,6},{6,10},{10,14},{3,7},{... | collective-permute-start | bytes 344072 | tf_op jit(solution)/shard_map/ppermute | solution.py:505
  10.3 1.3 %collective-permute-start.3 = (f32[4,56,128]{2,1,0:T(8,128)S(1)}, f32[4,56,128]{2,1,0:T(8,128)S(1)}, u32[]{:S(2)}, u32[]{:S(2)}) collective-permute-start(f32[4,56,128]{2,1,0:T(8,128)S(1)} %get-tuple-element.38), channel_id=1, source_target_pairs={{4,0},{8,4},{12,8},{5,1},{9,5},{13,9},{6,2},{10,6},{14,10},{7,3},{... | collective-permute-start | bytes 344072 | tf_op jit(solution)/shard_map/ppermute | solution.py:506
  11.6 1.2 %copy.8 = f32[1,8,128,128]{2,3,1,0:T(8,128)S(1)} copy(f32[1,8,128,128]{3,2,1,0:T(8,128)} %param.11) | data formatting | bytes 1048576 | tf_op args[5]
  12.8 0.0 collective-permute-done.2.above
  12.8 4.1 %collective-permute-done.3.below = f32[4,56,128]{2,1,0:T(8,128)S(1)} collective-permute-done((f32[4,56,128]{2,1,0:T(8,128)S(1)}, f32[4,56,128]{2,1,0:T(8,128)S(1)}, u32[]{:S(2)}, u32[]{:S(2)}) %collective-permute-start.3) | collective-permute-done | bytes 114720 | tf_op jit(solution)/shard_map/ppermute | solution.py:506
  17.0 0.0 collective-permute-done.1.refs_0_
  17.0 0.0 collective-permute-done.refs_1_
  17.0 0.6 collective-permute-start.5
  17.6 0.5 collective-permute-start.4
  18.1 0.0 collective-permute-start.8
  18.1 0.5 collective-permute-start.10
  18.6 0.0 collective-permute-start.9
  18.6 1.0 collective-permute-done.8.refs_8_
  19.6 0.1 collective-permute-start.11
  19.7 5.0 %collective-permute-done.5.refs_5_ = f32[656,128]{1,0:T(8,128)S(1)} collective-permute-done((f32[656,128]{1,0:T(8,128)S(1)}, f32[656,128]{1,0:T(8,128)S(1)}, u32[]{:S(2)}, u32[]{:S(2)}) %collective-permute-start.5) | collective-permute-done | bytes 335904 | tf_op jit(solution)/shard_map/ppermute | solution.py:511
  24.7 0.0 collective-permute-start.13
  24.7 0.2 collective-permute-done.4.refs_4_
  25.0 0.3 collective-permute-start.12
  25.3 0.0 collective-permute-done.10.refs_10_
  25.3 0.6 collective-permute-start.7
  25.9 0.0 collective-permute-done.9.refs_9_
  25.9 1.2 %collective-permute-start.6 = (f32[224,128]{1,0:T(8,128)S(1)}, f32[224,128]{1,0:T(8,128)S(1)}, u32[]{:S(2)}, u32[]{:S(2)}) collective-permute-start(f32[224,128]{1,0:T(8,128)S(1)} %slice.8), channel_id=1, source_target_pairs={{0,2},{1,3},{2,0},{3,1},{4,6},{5,7},{6,4},{7,5},{8,10},{9,11},{10,... | collective-permute-start | bytes 344072 | tf_op jit(solution)/shard_map/ppermute | solution.py:511
  27.1 3.5 %collective-permute-done.7.refs_7_ = f32[224,128]{1,0:T(8,128)S(1)} collective-permute-done((f32[224,128]{1,0:T(8,128)S(1)}, f32[224,128]{1,0:T(8,128)S(1)}, u32[]{:S(2)}, u32[]{:S(2)}) %collective-permute-start.7) | collective-permute-done | bytes 114720 | tf_op jit(solution)/shard_map/ppermute | solution.py:515
  30.6 0.0 collective-permute-start.15
  30.6 0.3 collective-permute-done.6.refs_6_
  30.9 0.3 collective-permute-start.14
  31.1 0.0 collective-permute-done.11.refs_11_
  31.1 0.8 collective-permute-done.15.refs_15_
  31.9 0.3 collective-permute-done.14.refs_14_
  32.2 0.0 collective-permute-done.13.refs_13_
  32.2 0.0 collective-permute-done.12.refs_12_
  32.2 2.5 %begin.1 = (f32[8,4,64,128]{3,2,1,0:T(8,128)S(1)}, f32[8,4,64,128]{3,2,1,0:T(8,128)S(1)}, s32[8,4,64,128]{3,2,1,0:T(8,128)S(1)}, f32[10,4,80,128]{3,2,1,0:T(8,12...) custom-call(f32[416,128]{1,0:T(8,128)S(1)} %bitcast.18, ...), custom_call_target="tpu_custom_call" | custom-call | tf_op jit(solution)/shard_map/begin/pallas_call | solution.py:484
  34.7 12.9 %all_to_all.25.refs_0_ = f32[32,8,128]{2,1,0:T(8,128)S(1)} all-to-all(f32[32,8,128]{2,1,0:T(8,128)S(1)} %get-tuple-element.42), channel_id=1, replica_groups=mesh['gx'=2,'gy'=4,'col'=4] {'gx','gy','col'}, dimensions={0} | all-to-all | bytes 262144 | tf_op jit(solution)/shard_map/all_to_all | solution.py:567
  47.5 4.2 %step0.1 = (f32[6,4,32,128]{3,2,1,0:T(8,128)S(1)}, f32[32,1,1152]{2,1,0:T(1,128)S(1)}, f32[10,4,80,128]{3,2,1,0:T(8,128)S(1)}, f32[10,4,80,128]{3,2,1,0:T(8,128)S(1)}) custom-call(f32[32,8,128]{2,1,0:T(8,128)S(1)} %all_to_all.25.refs_0_, f32[8,4,64,128]{3,2,1,0:T(8,128)S(1)} %get-tuple-element.43.refs_1_.g, ...), custom_call_target="tpu_custom_call" | custom-call | tf_op jit(solution)/shard_map/step0/pallas_call | solution.py:484
  51.7 10.1 %all_to_all.26.refs_0_ = f32[32,1,1152]{2,1,0:T(1,128)S(1)} all-to-all(f32[32,1,1152]{2,1,0:T(1,128)S(1)} %get-tuple-element.49), channel_id=1, replica_groups=mesh['gx'=2,'gy'=4,'col'=4] {'gx','gy','col'}, dimensions={0} | all-to-all | bytes 294912 | tf_op jit(solution)/shard_map/all_to_all | solution.py:567
  61.8 4.3 %step1.1 = (f32[6,4,32,128]{3,2,1,0:T(8,128)S(1)}, f32[32,1,1152]{2,1,0:T(1,128)S(1)}, f32[10,4,80,128]{3,2,1,0:T(8,128)S(1)}, f32[10,4,80,128]{3,2,1,0:T(8,128)...) custom-call(f32[32,1,1152]{2,1,0:T(1,128)S(1)} %all_to_all.26.refs_0_, ...), custom_call_target="tpu_custom_call" | custom-call | tf_op jit(solution)/shard_map/step1/pallas_call | solution.py:484
  66.2 10.2 %all_to_all.27.refs_0_ = f32[32,1,1152]{2,1,0:T(1,128)S(1)} all-to-all(f32[32,1,1152]{2,1,0:T(1,128)S(1)} %get-tuple-element.53), channel_id=1, replica_groups=mesh['gx'=2,'gy'=4,'col'=4] {'gx','gy','col'}, dimensions={0} | all-to-all | bytes 294912 | tf_op jit(solution)/shard_map/all_to_all | solution.py:567
  76.4 3.8 %step2.1 = (f32[6,4,32,128]{3,2,1,0:T(8,128)S(1)}, f32[32,1,1152]{2,1,0:T(1,128)S(1)}, f32[10,4,80,128]{3,2,1,0:T(8,128)S(1)}, f32[10,4,80,128]{3,2,1,0:T(8,128)...) custom-call(f32[32,1,1152]{2,1,0:T(1,128)S(1)} %all_to_all.27.refs_0_, ...), custom_call_target="tpu_custom_call" | custom-call | tf_op jit(solution)/shard_map/step2/pallas_call | solution.py:484
  80.3 10.3 %all_to_all.28.refs_0_ = f32[32,1,1152]{2,1,0:T(1,128)S(1)} all-to-all(f32[32,1,1152]{2,1,0:T(1,128)S(1)} %get-tuple-element.59), channel_id=1, replica_groups=mesh['gx'=2,'gy'=4,'col'=4] {'gx','gy','col'}, dimensions={0} | all-to-all | bytes 294912 | tf_op jit(solution)/shard_map/all_to_all | solution.py:567
  90.6 2.0 %step3.1 = (f32[7,4,32,128]{3,2,1,0:T(8,128)S(1)}, f32[32,1,128]{2,1,0:T(1,128)S(1)}, f32[1,128]{1,0:T(1,128)S(1)}) custom-call(f32[32,1,1152]{2,1,0:T(1,128)S(1)} %all_to_all.28.refs_0_, f32[8,4,64,128]{3,2,1,0:T(8,128)S(1)} %get-tuple-element.43.refs_1_.g, f32[8,4,64,128]{3,2,1,0:T(8,128)S(1)} %get-tuple-element.44.refs_2_.s, ...), custom_call_target="tpu_custom_call" | custom-call | tf_op jit(solution)/shard_map/step3/pallas_call | solution.py:484
  92.5 9.0 %all_to_all.29.recv = f32[32,1,128]{2,1,0:T(1,128)S(1)} all-to-all(f32[32,1,128]{2,1,0:T(1,128)S(1)} %get-tuple-element.65), channel_id=1, replica_groups=mesh['gx'=2,'gy'=4,'col'=4] {'gx','gy','col'}, dimensions={0} | all-to-all | bytes 32768 | tf_op jit(solution)/shard_map/all_to_all | solution.py:567
  101.5 0.9 end.1
  (5 shorter events, 0.1 us)
Async XLA Ops:
  2.3 14.7 %collective-permute-start.1 = (f32[4,104,128]{2,1,0:T(8,128)S(1)}, f32[4,104,128]{2,1,0:T(8,128)S(1)}, u32[]{:S(2)}, u32[]{:S(2)}) collective-permute-start(f32[4,104,128]{2,1,0:T(8,128)S(1)} %get-tuple-element.35), channel_id=1, source_target_pairs={{0,2},{1,3},{2,0},{3,1},{4,6},{5,7},{6,4},{7,5},{8,10},{9,11},{10,... | collective-permute-start | bytes 638984 | tf_op jit(solution)/shard_map/ppermute | solution.py:511
  5.3 11.7 %collective-permute-start = (f32[4,104,128]{2,1,0:T(8,128)S(1)}, f32[4,104,128]{2,1,0:T(8,128)S(1)}, u32[]{:S(2)}, u32[]{:S(2)}) collective-permute-start(f32[4,104,128]{2,1,0:T(8,128)S(1)} %get-tuple-element.35), channel_id=1, source_target_pairs={{0,16},{16,0},{1,17},{17,1},{2,18},{18,2},{3,19},{19,3},{4,20},{20... | collective-permute-start | bytes 638984 | tf_op jit(solution)/shard_map/ppermute | solution.py:515
  6.8 6.0 %collective-permute-start.2 = (f32[4,56,128]{2,1,0:T(8,128)S(1)}, f32[4,56,128]{2,1,0:T(8,128)S(1)}, u32[]{:S(2)}, u32[]{:S(2)}) collective-permute-start(f32[4,56,128]{2,1,0:T(8,128)S(1)} %get-tuple-element.36), channel_id=1, source_target_pairs={{0,4},{4,8},{8,12},{1,5},{5,9},{9,13},{2,6},{6,10},{10,14},{3,7},{... | collective-permute-start | bytes 344072 | tf_op jit(solution)/shard_map/ppermute | solution.py:505
  10.3 6.7 %collective-permute-start.3 = (f32[4,56,128]{2,1,0:T(8,128)S(1)}, f32[4,56,128]{2,1,0:T(8,128)S(1)}, u32[]{:S(2)}, u32[]{:S(2)}) collective-permute-start(f32[4,56,128]{2,1,0:T(8,128)S(1)} %get-tuple-element.38), channel_id=1, source_target_pairs={{4,0},{8,4},{12,8},{5,1},{9,5},{13,9},{6,2},{10,6},{14,10},{7,3},{... | collective-permute-start | bytes 344072 | tf_op jit(solution)/shard_map/ppermute | solution.py:506
  17.0 7.7 %collective-permute-start.5 = (f32[656,128]{1,0:T(8,128)S(1)}, f32[656,128]{1,0:T(8,128)S(1)}, u32[]{:S(2)}, u32[]{:S(2)}) collective-permute-start(f32[656,128]{1,0:T(8,128)S(1)} %get-tuple-element.40), channel_id=1, source_target_pairs={{0,2},{1,3},{2,0},{3,1},{4,6},{5,7},{6,4},{7,5},{8,10},{9,11},{10,... | collective-permute-start | bytes 1007624 | tf_op jit(solution)/shard_map/ppermute | solution.py:511
  17.6 7.4 %collective-permute-start.4 = (f32[656,128]{1,0:T(8,128)S(1)}, f32[656,128]{1,0:T(8,128)S(1)}, u32[]{:S(2)}, u32[]{:S(2)}) collective-permute-start(f32[656,128]{1,0:T(8,128)S(1)} %get-tuple-element.39.refs_3_), channel_id=1, source_target_pairs={{0,16},{16,0},{1,17},{17,1},{2,18},{18,2},{3,19},{19,3},{4,20},{20... | collective-permute-start | bytes 1007624 | tf_op jit(solution)/shard_map/ppermute | solution.py:515
  18.1 1.5 %collective-permute-start.8 = (f32[416,128]{1,0:T(8,128)S(1)}, f32[416,128]{1,0:T(8,128)S(1)}, u32[]{:S(2)}, u32[]{:S(2)}) collective-permute-start(f32[416,128]{1,0:T(8,128)S(1)} %bitcast.17), channel_id=1, source_target_pairs={{0,1},{1,0},{2,3},{3,2},{4,5},{5,4},{6,7},{7,6},{8,9},{9,8},{10,11... | collective-permute-start | bytes 638984 | tf_op jit(solution)/shard_map/ppermute | solution.py:511
  18.1 7.1 %collective-permute-start.10 = (f32[416,128]{1,0:T(8,128)S(1)}, f32[416,128]{1,0:T(8,128)S(1)}, u32[]{:S(2)}, u32[]{:S(2)}) collective-permute-start(f32[416,128]{1,0:T(8,128)S(1)} %bitcast.13), channel_id=1, source_target_pairs={{0,1},{1,0},{2,3},{3,2},{4,5},{5,4},{6,7},{7,6},{8,9},{9,8},{10,11... | collective-permute-start | bytes 638984 | tf_op jit(solution)/shard_map/ppermute | solution.py:511
  18.6 7.2 %collective-permute-start.9 = (f32[416,128]{1,0:T(8,128)S(1)}, f32[416,128]{1,0:T(8,128)S(1)}, u32[]{:S(2)}, u32[]{:S(2)}) collective-permute-start(f32[416,128]{1,0:T(8,128)S(1)} %bitcast.15), channel_id=1, source_target_pairs={{0,1},{1,0},{2,3},{3,2},{4,5},{5,4},{6,7},{7,6},{8,9},{9,8},{10,11... | collective-permute-start | bytes 638984 | tf_op jit(solution)/shard_map/ppermute | solution.py:511
  19.6 11.5 %collective-permute-start.11 = (f32[656,128]{1,0:T(8,128)S(1)}, f32[656,128]{1,0:T(8,128)S(1)}, u32[]{:S(2)}, u32[]{:S(2)}) collective-permute-start(f32[656,128]{1,0:T(8,128)S(1)} %get-tuple-element.39.refs_3_), channel_id=1, source_target_pairs={{0,1},{1,0},{2,3},{3,2},{4,5},{5,4},{6,7},{7,6},{8,9},{9,8},{10,11... | collective-permute-start | bytes 1007624 | tf_op jit(solution)/shard_map/ppermute | solution.py:511
  24.7 7.5 %collective-permute-start.13 = (f32[656,128]{1,0:T(8,128)S(1)}, f32[656,128]{1,0:T(8,128)S(1)}, u32[]{:S(2)}, u32[]{:S(2)}) collective-permute-start(f32[656,128]{1,0:T(8,128)S(1)} %collective-permute-done.5.refs_5_), channel_id=1, source_target_pairs={{0,1},{1,0},{2,3},{3,2},{4,5},{5,4},{6,7},{7,6},{8,9},{9,8},{10,11... | collective-permute-start | bytes 1007624 | tf_op jit(solution)/shard_map/ppermute | solution.py:511
  25.0 7.3 %collective-permute-start.12 = (f32[656,128]{1,0:T(8,128)S(1)}, f32[656,128]{1,0:T(8,128)S(1)}, u32[]{:S(2)}, u32[]{:S(2)}) collective-permute-start(f32[656,128]{1,0:T(8,128)S(1)} %collective-permute-done.4.refs_4_), channel_id=1, source_target_pairs={{0,1},{1,0},{2,3},{3,2},{4,5},{5,4},{6,7},{7,6},{8,9},{9,8},{10,11... | collective-permute-start | bytes 1007624 | tf_op jit(solution)/shard_map/ppermute | solution.py:511
  25.3 5.3 %collective-permute-start.7 = (f32[224,128]{1,0:T(8,128)S(1)}, f32[224,128]{1,0:T(8,128)S(1)}, u32[]{:S(2)}, u32[]{:S(2)}) collective-permute-start(f32[224,128]{1,0:T(8,128)S(1)} %slice.9), channel_id=1, source_target_pairs={{0,16},{16,0},{1,17},{17,1},{2,18},{18,2},{3,19},{19,3},{4,20},{20... | collective-permute-start | bytes 344072 | tf_op jit(solution)/shard_map/ppermute | solution.py:515
  25.9 5.0 %collective-permute-start.6 = (f32[224,128]{1,0:T(8,128)S(1)}, f32[224,128]{1,0:T(8,128)S(1)}, u32[]{:S(2)}, u32[]{:S(2)}) collective-permute-start(f32[224,128]{1,0:T(8,128)S(1)} %slice.8), channel_id=1, source_target_pairs={{0,2},{1,3},{2,0},{3,1},{4,6},{5,7},{6,4},{7,5},{8,10},{9,11},{10,... | collective-permute-start | bytes 344072 | tf_op jit(solution)/shard_map/ppermute | solution.py:511
  30.6 1.3 %collective-permute-start.15 = (f32[224,128]{1,0:T(8,128)S(1)}, f32[224,128]{1,0:T(8,128)S(1)}, u32[]{:S(2)}, u32[]{:S(2)}) collective-permute-start(f32[224,128]{1,0:T(8,128)S(1)} %collective-permute-done.7.refs_7_), channel_id=1, source_target_pairs={{0,1},{1,0},{2,3},{3,2},{4,5},{5,4},{6,7},{7,6},{8,9},{9,8},{10,11... | collective-permute-start | bytes 344072 | tf_op jit(solution)/shard_map/ppermute | solution.py:511
  30.9 1.3 %collective-permute-start.14 = (f32[224,128]{1,0:T(8,128)S(1)}, f32[224,128]{1,0:T(8,128)S(1)}, u32[]{:S(2)}, u32[]{:S(2)}) collective-permute-start(f32[224,128]{1,0:T(8,128)S(1)} %collective-permute-done.6.refs_6_), channel_id=1, source_target_pairs={{0,1},{1,0},{2,3},{3,2},{4,5},{5,4},{6,7},{7,6},{8,9},{9,8},{10,11... | collective-permute-start | bytes 344072 | tf_op jit(solution)/shard_map/ppermute | solution.py:511

commit v6 on v5

--- a/solution.py
+++ b/solution.py
@@ -125,13 +125,13 @@
     ref[z.planes + 1] = zero
 
 
-def presmooth(rho, g, out, tiles, z):
+def presmooth(rho, g, out, tiles, z, span=None):
     c0, c1 = w1 * (1.0 - w2) + w2, w1 * w2
 
     def visit(i, t, c, value, total):
         return [(out, (i + 1, c, inner(t)), c0 * value + (c1 * g[i, c, plain(t)]) * total)]
 
-    sweep(rho, tiles, z, visit)
+    sweep(rho, tiles, z, visit, span)
 
 
 def smooth(src, rho, g, out, w, tiles, z, span=None):
@@ -447,7 +447,8 @@
     if last:
         out[...] = jnp.broadcast_to(line[None], (z.devices, 1, LANES))
         return
-    presmooth(w_new, g, k["y2_out"], rows, z)
+    ends = step == ITERS - 2 and z.gx == 2 and z.cx > 3
+    presmooth(w_new, g, k["y2_out"], rows, z, z.cx + 3 if ends else None)
     restrict_solve(
         w_new, k["y2_out"], g, s, k["hot"], k["inv_t"], k["parts"], k["grouped"], k["msg"], z
     )

time: 103 us -> 103 us (level)
  no operation moved by 1% of the time
where the time goes in v6:
time: 103 us; the launch traced here: 102 us
  blocking collectives  52.5 us (51%)
  Pallas kernels  17.8 us (17%)
  waiting for transfers between devices  15.1 us (15%)
  starting transfers between devices  13.4 us (13%)
  other arithmetic  1.59 us (2%)
  local copies, waits for them, and re-layouts  1.26 us (1%)
    all_to_all x5, blocking collectives, on_device(): lax.all_to_all(m, ALL, split_axis=0, concat_axis=0, tiled=True)  52.5 us
    pallas_call x8, Pallas kernels, call(): pl.pallas_call(body, out_shape=outs, in_specs=[vmem] * len(args), out_spe...  17.8 us
    ppermute x11, waiting for transfers between devices, turn(): return lax.ppermute(value, 'col', [(i, i ^ bit) for i in range(z.col)])  7.28 us
    ppermute x11, starting transfers between devices, turn(): return lax.ppermute(value, 'col', [(i, i ^ bit) for i in range(z.col)])  6.04 us
    ppermute x1, waiting for transfers between devices, neighbours(): lax.ppermute(head, 'gy', [(i + 1, i) for i in range(z.gy - 1)])  4.13 us
    ppermute x3, waiting for transfers between devices, gather_fields(): swap = lambda value: lax.ppermute(value, 'gx', [(0, 1), (1, 0)])  3.72 us
    ppermute x1, starting transfers between devices, neighbours(): above = lax.ppermute(tail, 'gy', [(i, i + 1) for i in range(z.gy - 1)])  3.47 us
    ppermute x3, starting transfers between devices, gather_fields(): swap = lambda value: lax.ppermute(value, 'gx', [(0, 1), (1, 0)])  2.63 us
  transfers between devices with their start and end apart: 16, of which 8 were waited for; matrix products, arithmetic and copies ran while one was open for 1% of the time, Pallas kernels for 0%

profile of v6, /device:TPU:0, one launch (start us, length us, event | category | flops | bytes accessed | tf_op | source)
XLA Modules:
  0.0 102.4 jit_solution(11898648369996910280)
XLA Ops:
  0.6 0.7 convert_bitcast_fusion
  1.3 0.9 pad_maximum_fusion.block
  2.3 3.0 %collective-permute-start.1 = (f32[4,104,128]{2,1,0:T(8,128)S(1)}, f32[4,104,128]{2,1,0:T(8,128)S(1)}, u32[]{:S(2)}, u32[]{:S(2)}) collective-permute-start(f32[4,104,128]{2,1,0:T(8,128)S(1)} %get-tuple-element.35), channel_id=1, source_target_pairs={{0,2},{1,3},{2,0},{3,1},{4,6},{5,7},{6,4},{7,5},{8,10},{9,11},{10,... | collective-permute-start | bytes 638984 | tf_op jit(solution)/shard_map/ppermute | solution.py:512
  5.3 1.5 %collective-permute-start = (f32[4,104,128]{2,1,0:T(8,128)S(1)}, f32[4,104,128]{2,1,0:T(8,128)S(1)}, u32[]{:S(2)}, u32[]{:S(2)}) collective-permute-start(f32[4,104,128]{2,1,0:T(8,128)S(1)} %get-tuple-element.35), channel_id=1, source_target_pairs={{0,16},{16,0},{1,17},{17,1},{2,18},{18,2},{3,19},{19,3},{4,20},{20... | collective-permute-start | bytes 638984 | tf_op jit(solution)/shard_map/ppermute | solution.py:516
  6.8 3.5 %collective-permute-start.2 = (f32[4,56,128]{2,1,0:T(8,128)S(1)}, f32[4,56,128]{2,1,0:T(8,128)S(1)}, u32[]{:S(2)}, u32[]{:S(2)}) collective-permute-start(f32[4,56,128]{2,1,0:T(8,128)S(1)} %get-tuple-element.36), channel_id=1, source_target_pairs={{0,4},{4,8},{8,12},{1,5},{5,9},{9,13},{2,6},{6,10},{10,14},{3,7},{... | collective-permute-start | bytes 344072 | tf_op jit(solution)/shard_map/ppermute | solution.py:506
  10.3 1.3 %collective-permute-start.3 = (f32[4,56,128]{2,1,0:T(8,128)S(1)}, f32[4,56,128]{2,1,0:T(8,128)S(1)}, u32[]{:S(2)}, u32[]{:S(2)}) collective-permute-start(f32[4,56,128]{2,1,0:T(8,128)S(1)} %get-tuple-element.38), channel_id=1, source_target_pairs={{4,0},{8,4},{12,8},{5,1},{9,5},{13,9},{6,2},{10,6},{14,10},{7,3},{... | collective-permute-start | bytes 344072 | tf_op jit(solution)/shard_map/ppermute | solution.py:507
  11.6 1.2 %copy.8 = f32[1,8,128,128]{2,3,1,0:T(8,128)S(1)} copy(f32[1,8,128,128]{3,2,1,0:T(8,128)} %param.11) | data formatting | bytes 1048576 | tf_op args[5]
  12.8 0.0 collective-permute-done.2.above
  12.8 4.1 %collective-permute-done.3.below = f32[4,56,128]{2,1,0:T(8,128)S(1)} collective-permute-done((f32[4,56,128]{2,1,0:T(8,128)S(1)}, f32[4,56,128]{2,1,0:T(8,128)S(1)}, u32[]{:S(2)}, u32[]{:S(2)}) %collective-permute-start.3) | collective-permute-done | bytes 114720 | tf_op jit(solution)/shard_map/ppermute | solution.py:507
  17.0 0.0 collective-permute-done.1.refs_0_
  17.0 0.0 collective-permute-done.refs_1_
  17.0 0.6 collective-permute-start.5
  17.6 0.5 collective-permute-start.4
  18.1 0.0 collective-permute-start.8
  18.1 0.5 collective-permute-start.10
  18.6 0.0 collective-permute-start.9
  18.6 1.0 collective-permute-done.8.refs_8_
  19.6 0.1 collective-permute-start.11
  19.7 5.0 %collective-permute-done.5.refs_5_ = f32[656,128]{1,0:T(8,128)S(1)} collective-permute-done((f32[656,128]{1,0:T(8,128)S(1)}, f32[656,128]{1,0:T(8,128)S(1)}, u32[]{:S(2)}, u32[]{:S(2)}) %collective-permute-start.5) | collective-permute-done | bytes 335904 | tf_op jit(solution)/shard_map/ppermute | solution.py:512
  24.7 0.0 collective-permute-start.13
  24.7 0.2 collective-permute-done.4.refs_4_
  25.0 0.3 collective-permute-start.12
  25.3 0.0 collective-permute-done.10.refs_10_
  25.3 0.6 collective-permute-start.7
  25.9 0.0 collective-permute-done.9.refs_9_
  25.9 1.2 %collective-permute-start.6 = (f32[224,128]{1,0:T(8,128)S(1)}, f32[224,128]{1,0:T(8,128)S(1)}, u32[]{:S(2)}, u32[]{:S(2)}) collective-permute-start(f32[224,128]{1,0:T(8,128)S(1)} %slice.8), channel_id=1, source_target_pairs={{0,2},{1,3},{2,0},{3,1},{4,6},{5,7},{6,4},{7,5},{8,10},{9,11},{10,... | collective-permute-start | bytes 344072 | tf_op jit(solution)/shard_map/ppermute | solution.py:512
  27.1 3.5 %collective-permute-done.7.refs_7_ = f32[224,128]{1,0:T(8,128)S(1)} collective-permute-done((f32[224,128]{1,0:T(8,128)S(1)}, f32[224,128]{1,0:T(8,128)S(1)}, u32[]{:S(2)}, u32[]{:S(2)}) %collective-permute-start.7) | collective-permute-done | bytes 114720 | tf_op jit(solution)/shard_map/ppermute | solution.py:516
  30.6 0.0 collective-permute-start.15
  30.6 0.3 collective-permute-done.6.refs_6_
  30.9 0.3 collective-permute-start.14
  31.1 0.0 collective-permute-done.11.refs_11_
  31.1 0.8 collective-permute-done.15.refs_15_
  31.9 0.3 collective-permute-done.14.refs_14_
  32.2 0.0 collective-permute-done.13.refs_13_
  32.2 0.0 collective-permute-done.12.refs_12_
  32.2 2.5 %begin.1 = (f32[8,4,64,128]{3,2,1,0:T(8,128)S(1)}, f32[8,4,64,128]{3,2,1,0:T(8,128)S(1)}, s32[8,4,64,128]{3,2,1,0:T(8,128)S(1)}, f32[10,4,80,128]{3,2,1,0:T(8,12...) custom-call(f32[416,128]{1,0:T(8,128)S(1)} %bitcast.18, ...), custom_call_target="tpu_custom_call" | custom-call | tf_op jit(solution)/shard_map/begin/pallas_call | solution.py:485
  34.7 12.9 %all_to_all.25.refs_0_ = f32[32,8,128]{2,1,0:T(8,128)S(1)} all-to-all(f32[32,8,128]{2,1,0:T(8,128)S(1)} %get-tuple-element.42), channel_id=1, replica_groups=mesh['gx'=2,'gy'=4,'col'=4] {'gx','gy','col'}, dimensions={0} | all-to-all | bytes 262144 | tf_op jit(solution)/shard_map/all_to_all | solution.py:568
  47.5 4.2 %step0.1 = (f32[6,4,32,128]{3,2,1,0:T(8,128)S(1)}, f32[32,1,1152]{2,1,0:T(1,128)S(1)}, f32[10,4,80,128]{3,2,1,0:T(8,128)S(1)}, f32[10,4,80,128]{3,2,1,0:T(8,128)S(1)}) custom-call(f32[32,8,128]{2,1,0:T(8,128)S(1)} %all_to_all.25.refs_0_, f32[8,4,64,128]{3,2,1,0:T(8,128)S(1)} %get-tuple-element.43.refs_1_.g, ...), custom_call_target="tpu_custom_call" | custom-call | tf_op jit(solution)/shard_map/step0/pallas_call | solution.py:485
  51.7 10.1 %all_to_all.26.refs_0_ = f32[32,1,1152]{2,1,0:T(1,128)S(1)} all-to-all(f32[32,1,1152]{2,1,0:T(1,128)S(1)} %get-tuple-element.49), channel_id=1, replica_groups=mesh['gx'=2,'gy'=4,'col'=4] {'gx','gy','col'}, dimensions={0} | all-to-all | bytes 294912 | tf_op jit(solution)/shard_map/all_to_all | solution.py:568
  61.8 4.3 %step1.1 = (f32[6,4,32,128]{3,2,1,0:T(8,128)S(1)}, f32[32,1,1152]{2,1,0:T(1,128)S(1)}, f32[10,4,80,128]{3,2,1,0:T(8,128)S(1)}, f32[10,4,80,128]{3,2,1,0:T(8,128)...) custom-call(f32[32,1,1152]{2,1,0:T(1,128)S(1)} %all_to_all.26.refs_0_, ...), custom_call_target="tpu_custom_call" | custom-call | tf_op jit(solution)/shard_map/step1/pallas_call | solution.py:485
  66.2 10.2 %all_to_all.27.refs_0_ = f32[32,1,1152]{2,1,0:T(1,128)S(1)} all-to-all(f32[32,1,1152]{2,1,0:T(1,128)S(1)} %get-tuple-element.53), channel_id=1, replica_groups=mesh['gx'=2,'gy'=4,'col'=4] {'gx','gy','col'}, dimensions={0} | all-to-all | bytes 294912 | tf_op jit(solution)/shard_map/all_to_all | solution.py:568
  76.4 3.8 %step2.1 = (f32[6,4,32,128]{3,2,1,0:T(8,128)S(1)}, f32[32,1,1152]{2,1,0:T(1,128)S(1)}, f32[10,4,80,128]{3,2,1,0:T(8,128)S(1)}, f32[10,4,80,128]{3,2,1,0:T(8,128)...) custom-call(f32[32,1,1152]{2,1,0:T(1,128)S(1)} %all_to_all.27.refs_0_, ...), custom_call_target="tpu_custom_call" | custom-call | tf_op jit(solution)/shard_map/step2/pallas_call | solution.py:485
  80.3 10.3 %all_to_all.28.refs_0_ = f32[32,1,1152]{2,1,0:T(1,128)S(1)} all-to-all(f32[32,1,1152]{2,1,0:T(1,128)S(1)} %get-tuple-element.59), channel_id=1, replica_groups=mesh['gx'=2,'gy'=4,'col'=4] {'gx','gy','col'}, dimensions={0} | all-to-all | bytes 294912 | tf_op jit(solution)/shard_map/all_to_all | solution.py:568
  90.5 2.0 %step3.1 = (f32[7,4,32,128]{3,2,1,0:T(8,128)S(1)}, f32[32,1,128]{2,1,0:T(1,128)S(1)}, f32[1,128]{1,0:T(1,128)S(1)}) custom-call(f32[32,1,1152]{2,1,0:T(1,128)S(1)} %all_to_all.28.refs_0_, f32[8,4,64,128]{3,2,1,0:T(8,128)S(1)} %get-tuple-element.43.refs_1_.g, f32[8,4,64,128]{3,2,1,0:T(8,128)S(1)} %get-tuple-element.44.refs_2_.s, ...), custom_call_target="tpu_custom_call" | custom-call | tf_op jit(solution)/shard_map/step3/pallas_call | solution.py:485
  92.5 9.0 %all_to_all.29.recv = f32[32,1,128]{2,1,0:T(1,128)S(1)} all-to-all(f32[32,1,128]{2,1,0:T(1,128)S(1)} %get-tuple-element.65), channel_id=1, replica_groups=mesh['gx'=2,'gy'=4,'col'=4] {'gx','gy','col'}, dimensions={0} | all-to-all | bytes 32768 | tf_op jit(solution)/shard_map/all_to_all | solution.py:568
  101.5 0.9 end.1
  (5 shorter events, 0.1 us)
Async XLA Ops:
  2.3 14.7 %collective-permute-start.1 = (f32[4,104,128]{2,1,0:T(8,128)S(1)}, f32[4,104,128]{2,1,0:T(8,128)S(1)}, u32[]{:S(2)}, u32[]{:S(2)}) collective-permute-start(f32[4,104,128]{2,1,0:T(8,128)S(1)} %get-tuple-element.35), channel_id=1, source_target_pairs={{0,2},{1,3},{2,0},{3,1},{4,6},{5,7},{6,4},{7,5},{8,10},{9,11},{10,... | collective-permute-start | bytes 638984 | tf_op jit(solution)/shard_map/ppermute | solution.py:512
  5.3 11.7 %collective-permute-start = (f32[4,104,128]{2,1,0:T(8,128)S(1)}, f32[4,104,128]{2,1,0:T(8,128)S(1)}, u32[]{:S(2)}, u32[]{:S(2)}) collective-permute-start(f32[4,104,128]{2,1,0:T(8,128)S(1)} %get-tuple-element.35), channel_id=1, source_target_pairs={{0,16},{16,0},{1,17},{17,1},{2,18},{18,2},{3,19},{19,3},{4,20},{20... | collective-permute-start | bytes 638984 | tf_op jit(solution)/shard_map/ppermute | solution.py:516
  6.8 6.0 %collective-permute-start.2 = (f32[4,56,128]{2,1,0:T(8,128)S(1)}, f32[4,56,128]{2,1,0:T(8,128)S(1)}, u32[]{:S(2)}, u32[]{:S(2)}) collective-permute-start(f32[4,56,128]{2,1,0:T(8,128)S(1)} %get-tuple-element.36), channel_id=1, source_target_pairs={{0,4},{4,8},{8,12},{1,5},{5,9},{9,13},{2,6},{6,10},{10,14},{3,7},{... | collective-permute-start | bytes 344072 | tf_op jit(solution)/shard_map/ppermute | solution.py:506
  10.3 6.7 %collective-permute-start.3 = (f32[4,56,128]{2,1,0:T(8,128)S(1)}, f32[4,56,128]{2,1,0:T(8,128)S(1)}, u32[]{:S(2)}, u32[]{:S(2)}) collective-permute-start(f32[4,56,128]{2,1,0:T(8,128)S(1)} %get-tuple-element.38), channel_id=1, source_target_pairs={{4,0},{8,4},{12,8},{5,1},{9,5},{13,9},{6,2},{10,6},{14,10},{7,3},{... | collective-permute-start | bytes 344072 | tf_op jit(solution)/shard_map/ppermute | solution.py:507
  17.0 7.7 %collective-permute-start.5 = (f32[656,128]{1,0:T(8,128)S(1)}, f32[656,128]{1,0:T(8,128)S(1)}, u32[]{:S(2)}, u32[]{:S(2)}) collective-permute-start(f32[656,128]{1,0:T(8,128)S(1)} %get-tuple-element.40), channel_id=1, source_target_pairs={{0,2},{1,3},{2,0},{3,1},{4,6},{5,7},{6,4},{7,5},{8,10},{9,11},{10,... | collective-permute-start | bytes 1007624 | tf_op jit(solution)/shard_map/ppermute | solution.py:512
  17.6 7.4 %collective-permute-start.4 = (f32[656,128]{1,0:T(8,128)S(1)}, f32[656,128]{1,0:T(8,128)S(1)}, u32[]{:S(2)}, u32[]{:S(2)}) collective-permute-start(f32[656,128]{1,0:T(8,128)S(1)} %get-tuple-element.39.refs_3_), channel_id=1, source_target_pairs={{0,16},{16,0},{1,17},{17,1},{2,18},{18,2},{3,19},{19,3},{4,20},{20... | collective-permute-start | bytes 1007624 | tf_op jit(solution)/shard_map/ppermute | solution.py:516
  18.1 1.5 %collective-permute-start.8 = (f32[416,128]{1,0:T(8,128)S(1)}, f32[416,128]{1,0:T(8,128)S(1)}, u32[]{:S(2)}, u32[]{:S(2)}) collective-permute-start(f32[416,128]{1,0:T(8,128)S(1)} %bitcast.17), channel_id=1, source_target_pairs={{0,1},{1,0},{2,3},{3,2},{4,5},{5,4},{6,7},{7,6},{8,9},{9,8},{10,11... | collective-permute-start | bytes 638984 | tf_op jit(solution)/shard_map/ppermute | solution.py:512
  18.1 7.1 %collective-permute-start.10 = (f32[416,128]{1,0:T(8,128)S(1)}, f32[416,128]{1,0:T(8,128)S(1)}, u32[]{:S(2)}, u32[]{:S(2)}) collective-permute-start(f32[416,128]{1,0:T(8,128)S(1)} %bitcast.13), channel_id=1, source_target_pairs={{0,1},{1,0},{2,3},{3,2},{4,5},{5,4},{6,7},{7,6},{8,9},{9,8},{10,11... | collective-permute-start | bytes 638984 | tf_op jit(solution)/shard_map/ppermute | solution.py:512
  18.6 7.2 %collective-permute-start.9 = (f32[416,128]{1,0:T(8,128)S(1)}, f32[416,128]{1,0:T(8,128)S(1)}, u32[]{:S(2)}, u32[]{:S(2)}) collective-permute-start(f32[416,128]{1,0:T(8,128)S(1)} %bitcast.15), channel_id=1, source_target_pairs={{0,1},{1,0},{2,3},{3,2},{4,5},{5,4},{6,7},{7,6},{8,9},{9,8},{10,11... | collective-permute-start | bytes 638984 | tf_op jit(solution)/shard_map/ppermute | solution.py:512
  19.6 11.5 %collective-permute-start.11 = (f32[656,128]{1,0:T(8,128)S(1)}, f32[656,128]{1,0:T(8,128)S(1)}, u32[]{:S(2)}, u32[]{:S(2)}) collective-permute-start(f32[656,128]{1,0:T(8,128)S(1)} %get-tuple-element.39.refs_3_), channel_id=1, source_target_pairs={{0,1},{1,0},{2,3},{3,2},{4,5},{5,4},{6,7},{7,6},{8,9},{9,8},{10,11... | collective-permute-start | bytes 1007624 | tf_op jit(solution)/shard_map/ppermute | solution.py:512
  24.7 7.5 %collective-permute-start.13 = (f32[656,128]{1,0:T(8,128)S(1)}, f32[656,128]{1,0:T(8,128)S(1)}, u32[]{:S(2)}, u32[]{:S(2)}) collective-permute-start(f32[656,128]{1,0:T(8,128)S(1)} %collective-permute-done.5.refs_5_), channel_id=1, source_target_pairs={{0,1},{1,0},{2,3},{3,2},{4,5},{5,4},{6,7},{7,6},{8,9},{9,8},{10,11... | collective-permute-start | bytes 1007624 | tf_op jit(solution)/shard_map/ppermute | solution.py:512
  25.0 7.3 %collective-permute-start.12 = (f32[656,128]{1,0:T(8,128)S(1)}, f32[656,128]{1,0:T(8,128)S(1)}, u32[]{:S(2)}, u32[]{:S(2)}) collective-permute-start(f32[656,128]{1,0:T(8,128)S(1)} %collective-permute-done.4.refs_4_), channel_id=1, source_target_pairs={{0,1},{1,0},{2,3},{3,2},{4,5},{5,4},{6,7},{7,6},{8,9},{9,8},{10,11... | collective-permute-start | bytes 1007624 | tf_op jit(solution)/shard_map/ppermute | solution.py:512
  25.3 5.3 %collective-permute-start.7 = (f32[224,128]{1,0:T(8,128)S(1)}, f32[224,128]{1,0:T(8,128)S(1)}, u32[]{:S(2)}, u32[]{:S(2)}) collective-permute-start(f32[224,128]{1,0:T(8,128)S(1)} %slice.9), channel_id=1, source_target_pairs={{0,16},{16,0},{1,17},{17,1},{2,18},{18,2},{3,19},{19,3},{4,20},{20... | collective-permute-start | bytes 344072 | tf_op jit(solution)/shard_map/ppermute | solution.py:516
  25.9 5.0 %collective-permute-start.6 = (f32[224,128]{1,0:T(8,128)S(1)}, f32[224,128]{1,0:T(8,128)S(1)}, u32[]{:S(2)}, u32[]{:S(2)}) collective-permute-start(f32[224,128]{1,0:T(8,128)S(1)} %slice.8), channel_id=1, source_target_pairs={{0,2},{1,3},{2,0},{3,1},{4,6},{5,7},{6,4},{7,5},{8,10},{9,11},{10,... | collective-permute-start | bytes 344072 | tf_op jit(solution)/shard_map/ppermute | solution.py:512
  30.6 1.3 %collective-permute-start.15 = (f32[224,128]{1,0:T(8,128)S(1)}, f32[224,128]{1,0:T(8,128)S(1)}, u32[]{:S(2)}, u32[]{:S(2)}) collective-permute-start(f32[224,128]{1,0:T(8,128)S(1)} %collective-permute-done.7.refs_7_), channel_id=1, source_target_pairs={{0,1},{1,0},{2,3},{3,2},{4,5},{5,4},{6,7},{7,6},{8,9},{9,8},{10,11... | collective-permute-start | bytes 344072 | tf_op jit(solution)/shard_map/ppermute | solution.py:512
  30.9 1.3 %collective-permute-start.14 = (f32[224,128]{1,0:T(8,128)S(1)}, f32[224,128]{1,0:T(8,128)S(1)}, u32[]{:S(2)}, u32[]{:S(2)}) collective-permute-start(f32[224,128]{1,0:T(8,128)S(1)} %collective-permute-done.6.refs_6_), channel_id=1, source_target_pairs={{0,1},{1,0},{2,3},{3,2},{4,5},{5,4},{6,7},{7,6},{8,9},{9,8},{10,11... | collective-permute-start | bytes 344072 | tf_op jit(solution)/shard_map/ppermute | solution.py:512
